TPU v7x, 128 devices: a whole 4x4x4 slice. The times are simulated.
128 devices in a mesh: dp: 4 (over z), cell: 32 (over x, y, core).
Axes of the slice: x: 4, y: 4, z: 4, core: 2. Of those that a mesh axis runs over, the one named last changes fastest.
Arguments:
- vectors: bfloat16 [4, 12288, 64, 128], P('dp', 'cell'), may hold values from -120 to 120
- block_cells: int32 [4, 12288], P('dp', 'cell'), may hold values from 0 to 30
- dest_counts: int32 [4, 32, 32], P('dp', 'cell'), may hold values from 0 to 24, as said below
Outputs:
- cell_mean: float32 [1024, 128], P('cell')
- cell_cov: float32 [1024, 128, 128], P('cell')
Inputs may be any that keep to these rules, and one draw needn't show every extreme that they name: Each device's dest_counts sum to 384; in each group one owner receives exactly 24 blocks from every device of the group, and every device sends no block to one other owner.
All inputs are finite; a program needn't handle non-finite values.
Results may differ from a plain program's by a relative error of at most 0.0003.
Values may be sent and summed in bfloat16 or wider, within the bound.
No kernel may reach another device: no remote copies, remote signals or barrier semaphores. Data moves between devices by JAX's collectives and lax.ppermute only.
A program may use at most 128 MiB of HBM per device.

v0:
```python
import math

import jax
import jax.numpy as jnp
from jax import lax
from jax.sharding import PartitionSpec as P

CELLS = 1024


def joined(part, axis, combine):
    gathered = jax.tree.map(lambda a: lax.all_gather(a, axis), part)

    def take(source):
        return jax.tree.map(lambda a: lax.dynamic_index_in_dim(a, source, 0, False), gathered)

    return lax.fori_loop(
        1, lax.axis_size(axis), lambda source, state: combine(state, take(source)), take(0)
    )


def chan_update(left, right):
    left_count, left_mean, left_scatter = left
    right_count, right_mean, right_scatter = right
    total_count = left_count + right_count
    safe_count = jnp.maximum(total_count, 1.0)
    difference = right_mean - left_mean
    average = left_mean + difference * (right_count / safe_count)[:, None]
    weight = left_count * right_count / safe_count
    scatter = (
        left_scatter
        + right_scatter
        + weight[:, None, None] * difference[:, :, None] * difference[:, None, :]
    )
    return (total_count, average, scatter)


def add_moments(running, arrived, arrived_codes, cell_dev):
    block_rows = arrived.shape[2]
    width = arrived.shape[3]
    slot_total = arrived.shape[0] * arrived.shape[1]
    batch_size = math.gcd(slot_total, 256)
    batch_count = slot_total // batch_size
    local_cells = jnp.arange(cell_dev, dtype=jnp.int32).astype(jnp.float32)

    def accumulate(carried, batch_item):
        rows_in, codes_in = batch_item
        gram_blocks = jnp.einsum(
            "brd,bre->bde", rows_in, rows_in, preferred_element_type=jnp.float32
        ).reshape(batch_size, width * width)
        row_sums = jnp.sum(rows_in.astype(jnp.float32), axis=1)
        onehot = (local_cells[:, None] == codes_in.astype(jnp.float32)[None, :]).astype(jnp.float32)
        new_counts = carried[0] + jnp.sum(onehot, axis=1) * float(block_rows)
        new_sums = carried[1] + jnp.dot(onehot, row_sums, precision=lax.Precision.HIGHEST)
        new_grams = carried[2] + jnp.dot(onehot, gram_blocks, precision=lax.Precision.HIGHEST)
        return ((new_counts, new_sums, new_grams), None)

    items = (
        arrived.reshape(batch_count, batch_size, block_rows, width),
        arrived_codes.reshape(batch_count, batch_size),
    )
    moments, _ = lax.scan(accumulate, running, items)
    return moments


def local(vectors, block_cells, dest_counts):
    owner_count = lax.axis_size("cell")
    own_blocks = vectors.shape[1]
    block_rows = vectors.shape[2]
    width = vectors.shape[3]
    capacity = 2 * own_blocks // owner_count
    cell_dev = CELLS // owner_count
    counts = dest_counts[0, 0]
    offsets = jnp.cumsum(counts) - counts
    slot_index = jnp.arange(capacity, dtype=jnp.int32)
    is_live = slot_index[None, :] < counts[:, None]
    block_index = jnp.where(is_live, offsets[:, None] + slot_index[None, :], 0).reshape(-1)
    outgoing = jnp.take(vectors[0], block_index, axis=0).reshape(
        owner_count, capacity, block_rows, width
    )
    outgoing = jnp.where(is_live[:, :, None, None], outgoing, jnp.zeros_like(outgoing))
    taken_cells = (
        jnp.take(block_cells[0], block_index).reshape(owner_count, capacity).astype(jnp.float32)
    )
    cell_codes = jnp.where(is_live, taken_cells, -1.0).astype(jnp.bfloat16)
    initial = (
        jnp.zeros((cell_dev,), jnp.float32),
        jnp.zeros((cell_dev, width), jnp.float32),
        jnp.zeros((cell_dev, width * width), jnp.float32),
    )
    arrived, arrived_codes = (
        lax.all_to_all(outgoing, "cell", split_axis=0, concat_axis=0, tiled=True),
        lax.all_to_all(cell_codes, "cell", split_axis=0, concat_axis=0, tiled=True),
    )
    moments = add_moments(initial, arrived, arrived_codes, cell_dev)
    counts_here, sums_here, grams_here = moments
    average = sums_here / jnp.maximum(counts_here, 1.0)[:, None]
    scatter = (
        grams_here.reshape(cell_dev, width, width)
        - counts_here[:, None, None] * average[:, :, None] * average[:, None, :]
    )
    total_count, cell_mean, scatter_all = joined((counts_here, average, scatter), "dp", chan_update)
    cell_cov = scatter_all / jnp.maximum(total_count, 1.0)[:, None, None]
    return (cell_mean, cell_cov)


def solution(mesh):
    in_specs = (P("dp", "cell", None, None), P("dp", "cell"), P("dp", "cell", None))
    out_specs = (P("cell", None), P("cell", None, None))
    return jax.shard_map(local, mesh=mesh, in_specs=in_specs, out_specs=out_specs, check_vma=False)
```

profile of v0, /device:TPU:1, one launch (start us, length us, event | category | flops | bytes accessed | tf_op | source)
XLA Modules:
  0.0 475.1 jit_solution(9608617637986715844)
XLA Ops:
  9.7 5.0 %gather_fusion = s32[768]{0:T(1024)S(1)} fusion(s32[384]{0:T(512)S(1)} %reduce.1, s32[1024]{0:T(1024)S(1)} %pad_clamp_fusion), kind=kCustom, calls=%fused_computation | custom fusion | bytes 9216 | tf_op jit(solution)/shard_map/jit(_take)/gather | solution.py:83
  15.5 8.6 %all-to-all-start = ((bf16[32,1,24]{2,1,0:T(2,128)(2,1)}), bf16[32,1,24]{2,1,0:T(2,128)(2,1)S(1)}, u32[]{:S(2)}, u32[]{:S(2)}) async-start(bf16[32,1,24]{2,1,0:T(2,128)(2,1)} %copy.13), calls=%async_computation | async-start | bytes 32768 | tf_op jit(solution)/shard_map/all_to_all | solution.py:93
  24.2 22.3 %gather_fusion.1 = bf16[768,64,128]{2,1,0:T(8,128)(2,1)} fusion(bf16[384,64,128]{2,1,0:T(8,128)(2,1)} %bitcast.63, s32[1024]{0:T(1024)S(1)} %pad_clamp_fusion), kind=kCustom, calls=%fused_computation.1 | custom fusion | bytes 25168896 | tf_op jit(solution)/shard_map/jit(_take)/gather | solution.py:78
  46.5 11.1 %select_select_fusion = bf16[32,24,64,128]{3,2,1,0:T(8,128)(2,1)} fusion(bf16[32,24,64,128]{3,2,1,0:T(8,128)(2,1)} %bitcast.62, pred[32,24]{1,0:T(8,128)(4,1)S(1)} %get-tuple-element.281, pred[32,24]{1,0:T(8,128)(4,1)S(1)} %get-tuple-element.280), kind=kLoop, calls=%fused_computation.34 | loop fusion | flops 12582912 | bytes 25167360 | tf_op jit(solution)/shard_map/jit(_where)/select_n | solution.py:81
  57.6 7.3 %all-to-all-start.1 = ((bf16[32,24,64,128]{3,2,1,0:T(8,128)(2,1)}), bf16[32,24,64,128]{3,2,1,0:T(8,128)(2,1)}, u32[]{:S(2)}, u32[]{:S(2)}) async-start(bf16[32,24,64,128]{3,2,1,0:T(8,128)(2,1)} %select_select_fusion), calls=%async_computation.1 | async-start | bytes 25165824 | tf_op jit(solution)/shard_map/all_to_all | solution.py:92
  65.2 174.4 %all-to-all-done.1 = bf16[32,24,64,128]{3,2,1,0:T(8,128)(2,1)} async-done(((bf16[32,24,64,128]{3,2,1,0:T(8,128)(2,1)}), bf16[32,24,64,128]{3,2,1,0:T(8,128)(2,1)}, u32[]{:S(2)}, u32[]{:S(2)}) %all-to-all-start.1) | async-done | bytes 12582944 | tf_op jit(solution)/shard_map/all_to_all | solution.py:92
  239.6 108.7 %while.35 = (s32[]{:T(128)}, f32[32]{0:T(128)S(1)}, f32[32,128]{1,0:T(8,128)S(1)}, f32[32,16384]{1,0:T(8,128)S(1)}, bf16[3,256]{1,0:T(4,128)(2,1)S(1)}, /*index=...) while((s32[]{:T(128)}, f32[32]{0:T(128)S(1)}, f32[32,128]{1,0:T(8,128)S(1)}, ...), condition=%wide.region_4.5_spmd.clone, body=%wide.region_1.4_spmd.clone.sunk | while | flops 2165326336 | bytes 46438504 | solution.py:62
  239.6 11.6 %fusion.42 = f32[256,128,128]{2,1,0:T(8,128)} fusion(bf16[3,256,64,128]{3,2,1,0:T(8,128)(2,1)} %get-tuple-element.391, s32[]{:T(128)} %get-tuple-element.378), kind=kOutput, calls=%fused_computation.17.clone.1 | convolution fusion | flops 536870912 | bytes 20972032 | tf_op jit(solution)/shard_map/while/body/eval_jaxpr/brd,bre->bde/dot_general | solution.py:48
  251.2 20.4 %convolution_add_fusion.5 = f32[32,16384]{1,0:T(8,128)S(1)} fusion(f32[32,8,128,128]{3,2,1,0:T(8,128)} %bitcast.60, f32[32,16384]{1,0:T(8,128)S(1)} %get-tuple-element.381, pred[]{:T(512)S(6)} %compare.3, f32[256]{0:T(256)S(1)} %bitcast.66, f32[32]{0:T(128)S(1)} %iota_convert_fusion.2), kind=kOutput, calls=%fused_computation.13.clone.1 | convolution fusion | flops 1611669504 | bytes 20972672 | tf_op jit(solution)/shard_map/while/body/eval_jaxpr/dot_general | solution.py:55
  271.7 3.7 convert_reduce_fusion.2
  275.8 11.6 %fusion.42 = f32[256,128,128]{2,1,0:T(8,128)} fusion(bf16[3,256,64,128]{3,2,1,0:T(8,128)(2,1)} %get-tuple-element.391, s32[]{:T(128)} %get-tuple-element.378), kind=kOutput, calls=%fused_computation.17.clone.1 | convolution fusion | flops 536870912 | bytes 20972032 | tf_op jit(solution)/shard_map/while/body/eval_jaxpr/brd,bre->bde/dot_general | solution.py:48
  287.5 20.4 %convolution_add_fusion.5 = f32[32,16384]{1,0:T(8,128)S(1)} fusion(f32[32,8,128,128]{3,2,1,0:T(8,128)} %bitcast.60, f32[32,16384]{1,0:T(8,128)S(1)} %get-tuple-element.381, pred[]{:T(512)S(6)} %compare.3, f32[256]{0:T(256)S(1)} %bitcast.66, f32[32]{0:T(128)S(1)} %iota_convert_fusion.2), kind=kOutput, calls=%fused_computation.13.clone.1 | convolution fusion | flops 1611669504 | bytes 20972672 | tf_op jit(solution)/shard_map/while/body/eval_jaxpr/dot_general | solution.py:55
  307.9 3.7 convert_reduce_fusion.2
  312.1 11.6 %fusion.42 = f32[256,128,128]{2,1,0:T(8,128)} fusion(bf16[3,256,64,128]{3,2,1,0:T(8,128)(2,1)} %get-tuple-element.391, s32[]{:T(128)} %get-tuple-element.378), kind=kOutput, calls=%fused_computation.17.clone.1 | convolution fusion | flops 536870912 | bytes 20972032 | tf_op jit(solution)/shard_map/while/body/eval_jaxpr/brd,bre->bde/dot_general | solution.py:48
  323.7 20.4 %convolution_add_fusion.5 = f32[32,16384]{1,0:T(8,128)S(1)} fusion(f32[32,8,128,128]{3,2,1,0:T(8,128)} %bitcast.60, f32[32,16384]{1,0:T(8,128)S(1)} %get-tuple-element.381, pred[]{:T(512)S(6)} %compare.3, f32[256]{0:T(256)S(1)} %bitcast.66, f32[32]{0:T(128)S(1)} %iota_convert_fusion.2), kind=kOutput, calls=%fused_computation.13.clone.1 | convolution fusion | flops 1611669504 | bytes 20972672 | tf_op jit(solution)/shard_map/while/body/eval_jaxpr/dot_general | solution.py:55
  344.1 3.7 convert_reduce_fusion.2
  352.2 10.2 %all-gather.1 = f32[128,128]{1,0:T(8,128)S(1)} all-gather(f32[32,128]{1,0:T(8,128)S(1)} %get-tuple-element.279), channel_id=3, replica_groups=mesh['dp'=4,'cell'=32] {'dp'}, dimensions={0}, use_global_device_ids=true | all-gather | bytes 81920 | tf_op jit(solution)/shard_map/all_gather | solution.py:12
  362.6 8.5 %all-reduce = f32[128]{0:T(128)S(1)} all-reduce(f32[128]{0:T(128)S(1)} %dynamic-update-slice), channel_id=2, replica_groups=mesh['dp'=4,'cell'=32] {'dp'}, use_global_device_ids=true, to_apply=%add | all-reduce | flops 128 | bytes 1024
  371.2 86.9 %all-gather.4.cloned.1.call-done = f32[4,32,128,128]{3,2,1,0:T(8,128)} async-done(((f32[1,32,128,128]{3,2,1,0:T(8,128)}), f32[4,32,128,128]{3,2,1,0:T(8,128)}) %all-gather.4.cloned.1.call-update) | async-done | bytes 8388624 | tf_op jit(solution)/shard_map/all_gather | solution.py:12
  458.2 1.7 slice_bitcast_fusion
  459.9 6.7 %while.34 = (s32[]{:T(128)}, f32[32]{0:T(128)S(1)}, f32[32,128]{1,0:T(8,128)S(1)}, f32[32,128,128]{2,1,0:T(8,128)S(1)}, f32[4,32]{1,0:T(4,128)S(1)}, /*index=5*/...) while((s32[]{:T(128)}, f32[32]{0:T(128)S(1)}, ...), condition=%wide.region_6.7_spmd, body=%wide.region_5.6_spmd.sunk | while | flops 1589445 | bytes 6440223 | solution.py:17
  460.0 2.0 fusion.34
  462.3 2.0 fusion.34
  464.5 2.0 fusion.34
  (70 shorter events, 10.6 us)
Async XLA Ops:
  7.2 2.5 copy-start
  9.6 5.2 %copy-start.3 = (s32[1,1,32]{2,1,0:T(1,128)S(1)}, s32[1,1,32]{2,1,0:T(1,128)}, u32[]{:S(2)}) copy-start(s32[1,1,32]{2,1,0:T(1,128)} %param.9) | copy-start | bytes 388
  15.5 42.1 %all-to-all-start = ((bf16[32,1,24]{2,1,0:T(2,128)(2,1)}), bf16[32,1,24]{2,1,0:T(2,128)(2,1)S(1)}, u32[]{:S(2)}, u32[]{:S(2)}) async-start(bf16[32,1,24]{2,1,0:T(2,128)(2,1)} %copy.13), calls=%async_computation | async-start | bytes 32768 | tf_op jit(solution)/shard_map/all_to_all | solution.py:93
  57.6 182.0 %all-to-all-start.1 = ((bf16[32,24,64,128]{3,2,1,0:T(8,128)(2,1)}), bf16[32,24,64,128]{3,2,1,0:T(8,128)(2,1)}, u32[]{:S(2)}, u32[]{:S(2)}) async-start(bf16[32,24,64,128]{3,2,1,0:T(8,128)(2,1)} %select_select_fusion), calls=%async_computation.1 | async-start | bytes 25165824 | tf_op jit(solution)/shard_map/all_to_all | solution.py:92
  64.9 393.2 %all-gather.4.cloned.1.call-start = ((), (), s32[]{:S(2)}) async-start(), calls=%async_computation.2 | async-start | bytes 10485760 | tf_op jit(solution)/shard_map/all_gather | solution.py:12
  350.4 0.7 copy-start.4
  466.7 1.6 copy-start.2
  466.7 1.6 copy-start.1
Sparse Core Ops, SparseCore 0:
  350.6 107.5 all-gather.3
where the time goes:
time: 476 us; the launch traced here: 475 us
  waiting for transfers between devices  261 us (55%)
  matrix products  96.8 us (20%)
  other arithmetic  34.6 us (7%)
  local copies, waits for them, and re-layouts  32.7 us (7%)
  blocking collectives  18.7 us (4%)
  starting transfers between devices  15.9 us (3%)
  between operations  14.8 us (3%)
    all_to_all x1, waiting for transfers between devices, local(): lax.all_to_all(outgoing, 'cell', split_axis=0, concat_axis=0, tiled=True)  174 us
    all_gather x1, waiting for transfers between devices, joined(): gathered = jax.tree.map(lambda a: lax.all_gather(a, axis), part)  86.9 us
    dot_general x3, matrix products, accumulate(): jnp.dot(onehot, gram_blocks, precision=lax.Precision.HIGHEST)  61.3 us
    dot_general x3, matrix products, accumulate(): jnp.einsum('brd,bre->bde', rows_in, rows_in, preferred_element_type=jnp.f...  34.9 us
    gather x1, local copies, waits for them, and re-layouts, local(): jnp.take(vectors[0], block_index, axis=0)  22.3 us
    reduce_sum x3, other arithmetic, accumulate(): row_sums = jnp.sum(rows_in.astype(jnp.float32), axis=1)  11.1 us
    select_n x1, other arithmetic, local(): jnp.where(is_live[:, :, None, None], outgoing, jnp.zeros_like(outgoing))  11.1 us
    all_gather x1, blocking collectives, joined(): gathered = jax.tree.map(lambda a: lax.all_gather(a, axis), part)  10.2 us
  transfers between devices with their start and end apart: 3, of which 2 were waited for; matrix products, arithmetic and copies ran while one was open for 7% of the time, Pallas kernels for 0%

commit v1 on v0

v1 whole, which is shorter than its diff:
```python
import jax
import jax.numpy as jnp
from jax import lax
from jax.experimental import pallas as pl
from jax.experimental.pallas import tpu as pltpu
from jax.sharding import PartitionSpec as P

CELLS = 1024
NX = NY = NZ = 4
NC = 2
OWNERS = NX * NY * NC
CELL_DEV = CELLS // OWNERS
BLK = 384
ROWS = 64
D = 128
RUN = 12
SLOTS = 4 * RUN
SHIFTS = [(d, dc) for d in (0, 1, 3, 2) for dc in (0, 1)]
GROUPS = len(SHIFTS)
TRASH = 4 * CELL_DEV
LIST = 400
PAIR = 8
F32 = jnp.float32
I32 = jnp.int32
PACKED = CELL_DEV * ROWS
PIECE = PACKED + 3 * CELL_DEV
QCELL = CELL_DEV // NZ
QPACKED = QCELL * ROWS
QPIECE = QPACKED + 3 * QCELL
VMEM_LIMIT = 48 * 1024 * 1024


def at(x, y, c):
    return (x * NY + y) * NC + c


def cell_perm(dx, dy, dc):
    return [
        (at(x, y, c), at((x + dx) % NX, (y + dy) % NY, c ^ dc))
        for x in range(NX)
        for y in range(NY)
        for c in range(NC)
    ]


def dp_perm(dz):
    return [(z, (z + dz) % NZ) for z in range(NZ)]


def place():
    me = lax.axis_index("cell")
    return me // (NY * NC), (me // NC) % NY, me % NC


def other_core(c, dc):
    return (c + dc) % NC


def run_bounds(count, offset, half):
    first = (count + 1) // 2
    n = first if half == 0 else count - first
    start = offset if half == 0 else offset + first
    return n, start, jnp.minimum(start, BLK - RUN)


def pack_body(pos, counts, vectors, *refs):
    outs = refs[: 2 * GROUPS]
    offsets, sems = refs[2 * GROUPS :]
    x, y, c = pos[0], pos[1], pos[2]
    total = jnp.int32(0)
    for o in range(OWNERS):
        offsets[o] = total
        total = total + counts[o]
    copies = []
    for half in (0, 1):
        for g, (d, dc) in enumerate(SHIFTS):
            oc = other_core(c, dc)
            for k in range(4):
                o = at((x + d) % NX, k, oc) if half == 0 else at(k, (y + d) % NY, oc)
                _, _, start = run_bounds(counts[o], offsets[o], half)
                copies.append(
                    pltpu.make_async_copy(
                        vectors.at[pl.ds(start, RUN)],
                        outs[half * GROUPS + g].at[pl.ds(k * RUN, RUN)],
                        sems.at[(half * GROUPS + g) * 4 + k],
                    )
                )
                copies[-1].start()
    for copy in copies:
        copy.wait()


def pack(pos, counts, vectors):
    shape = jax.ShapeDtypeStruct((SLOTS, ROWS, D), vectors.dtype)
    return pl.pallas_call(
        pack_body,
        out_shape=[shape] * (2 * GROUPS),
        in_specs=[
            pl.BlockSpec(memory_space=pltpu.SMEM),
            pl.BlockSpec(memory_space=pltpu.SMEM),
            pl.BlockSpec(memory_space=pl.ANY),
        ],
        out_specs=[pl.BlockSpec(memory_space=pl.ANY)] * (2 * GROUPS),
        scratch_shapes=[pltpu.SMEM((OWNERS,), I32), pltpu.SemaphoreType.DMA((2 * GROUPS * 4,))],
        name="pack",
    )(pos, counts, vectors)


def lists_body(pos, meta, lists, sizes, tallies):
    x, y, c = pos[0], pos[1], pos[2]

    def clear(i, _):
        tallies[i] = jnp.int32(0)
        return 0

    lax.fori_loop(0, 2 * TRASH, clear, 0)

    def prefix(s, _):
        def step(o, total):
            count = meta[s, BLK + o]
            meta_next = total + count
            lists[2 * LIST + s * OWNERS + o] = total
            return meta_next

        lax.fori_loop(0, OWNERS, step, jnp.int32(0))
        return 0

    lax.fori_loop(0, OWNERS, prefix, 0)
    for half in (0, 1):
        filled = jnp.int32(0)
        for g, (d, dc) in enumerate(SHIFTS):
            sc = other_core(c, dc)
            s = at((x + NX - d) % NX, y, sc) if half == 0 else at(x, (y + NY - d) % NY, sc)
            for k in range(4):
                o = at(x, k, c) if half == 0 else at(k, y, c)
                n, start, copied = run_bounds(meta[s, BLK + o], lists[2 * LIST + s * OWNERS + o], half)
                slot = (g * 4 + k) * RUN + start - copied
                piece = lax.rem(k + 4 - (y if half == 0 else x), 4)

                def add(j, f, s=s, start=start, slot=slot, piece=piece, half=half):
                    cell = piece * CELL_DEV + meta[s, start + j]
                    lists[half * LIST + f] = (slot + j) * 256 + cell
                    tallies[half * TRASH + cell] = tallies[half * TRASH + cell] + ROWS
                    return f + 1

                filled = lax.fori_loop(0, n, add, filled)
        for j in range(PAIR):
            lists[half * LIST + filled + j] = jnp.int32(TRASH)
        sizes[half] = (filled + PAIR - 1) // PAIR


def make_lists(pos, meta):
    smem = pl.BlockSpec(memory_space=pltpu.SMEM)
    return pl.pallas_call(
        lists_body,
        out_shape=[
            jax.ShapeDtypeStruct((2 * LIST + OWNERS * OWNERS,), I32),
            jax.ShapeDtypeStruct((2,), I32),
            jax.ShapeDtypeStruct((2 * TRASH,), I32),
        ],
        in_specs=[smem, smem],
        out_specs=[smem, smem, smem],
        name="lists",
    )(pos, meta)


def gram_body(half, lists, sizes, tallies, *refs):
    blocks = refs[:GROUPS]
    outs = refs[GROUPS : GROUPS + 4]
    buf, acc, acc_s, acc_q, stage, in_sems, out_sems = refs[GROUPS + 4 :]
    loads = [
        pltpu.make_async_copy(blocks[g], buf.at[pl.ds(g * SLOTS, SLOTS)], in_sems.at[g]) for g in range(GROUPS)
    ]
    for load in loads:
        load.start()

    def clear(i, _):
        acc[pl.ds(pl.multiple_of(i * ROWS, ROWS), ROWS), :] = jnp.zeros((ROWS, D), F32)
        acc_s[pl.ds(pl.multiple_of(i * 8, 8), 8), :] = jnp.zeros((8, D), F32)
        acc_q[pl.ds(pl.multiple_of(i * 8, 8), 8), :] = jnp.zeros((8, D), F32)
        return 0

    lax.fori_loop(0, TRASH + 1, clear, 0)
    for load in loads:
        load.wait()
    row = lax.broadcasted_iota(I32, (ROWS, D), 0)
    lane = lax.broadcasted_iota(I32, (ROWS, D), 1)
    upper = lane >= row

    def step(i, _):
        done = []
        for u in range(PAIR):
            entry = lists[half * LIST + i * PAIR + u]
            cell = entry & 255
            block = buf[entry >> 8]
            turned = jnp.concatenate([block[:, ROWS:], block[:, :ROWS]], axis=1)
            contract = (((0,), (0,)), ((), ()))
            top = lax.dot_general(block[:, :ROWS], block, contract, preferred_element_type=F32)
            low = lax.dot_general(block[:, ROWS:], turned, contract, preferred_element_type=F32)
            wide = block.astype(F32)
            done.append(
                (
                    cell,
                    jnp.where(upper, top, low),
                    jnp.sum(wide.reshape(8, 8, D), axis=0),
                    jnp.sum((wide * wide).reshape(8, 8, D), axis=0),
                )
            )
        for cell, gram, total, square in done:
            here = pl.ds(pl.multiple_of(cell * ROWS, ROWS), ROWS)
            acc[here, :] = acc[here, :] + gram
            near = pl.ds(pl.multiple_of(cell * 8, 8), 8)
            acc_s[near, :] = acc_s[near, :] + total
            acc_q[near, :] = acc_q[near, :] + square
        return 0

    lax.fori_loop(0, sizes[half], step, 0)
    stores = [
        pltpu.make_async_copy(acc.at[pl.ds(p * PACKED, PACKED)], outs[p].at[pl.ds(0, PACKED)], out_sems.at[p])
        for p in range(4)
    ]
    for store in stores:
        store.start()
    for p in range(4):
        base = p * 3 * CELL_DEV
        for k, source in enumerate((acc_s, acc_q)):
            total = source[pl.ds(p * CELL_DEV * 8, CELL_DEV, stride=8), :]
            for j in range(1, 8):
                total = total + source[pl.ds(p * CELL_DEV * 8 + j, CELL_DEV, stride=8), :]
            stage[pl.ds(base + k * CELL_DEV, CELL_DEV), :] = total
        for j in range(CELL_DEV):
            count = tallies[half * TRASH + p * CELL_DEV + j].astype(F32)
            stage[pl.ds(base + 2 * CELL_DEV + j, 1), :] = jnp.full((1, D), count, F32)
    tails = [
        pltpu.make_async_copy(
            stage.at[pl.ds(p * 3 * CELL_DEV, 3 * CELL_DEV)],
            outs[p].at[pl.ds(PACKED, 3 * CELL_DEV)],
            out_sems.at[4 + p],
        )
        for p in range(4)
    ]
    for tail in tails:
        tail.start()
    for copy in stores + tails:
        copy.wait()


def gram(half, lists, sizes, tallies, blocks):
    smem = pl.BlockSpec(memory_space=pltpu.SMEM)
    hbm = pl.BlockSpec(memory_space=pl.ANY)

    def body(*refs):
        gram_body(half, *refs)

    return pl.pallas_call(
        body,
        out_shape=[jax.ShapeDtypeStruct((PIECE, D), F32)] * 4,
        in_specs=[smem, smem, smem] + [hbm] * GROUPS,
        out_specs=[hbm] * 4,
        scratch_shapes=[
            pltpu.VMEM((GROUPS * SLOTS, ROWS, D), jnp.bfloat16),
            pltpu.VMEM(((TRASH + 1) * ROWS, D), F32),
            pltpu.VMEM(((TRASH + 1) * 8, D), F32),
            pltpu.VMEM(((TRASH + 1) * 8, D), F32),
            pltpu.VMEM((4 * 3 * CELL_DEV, D), F32),
            pltpu.SemaphoreType.DMA((GROUPS,)),
            pltpu.SemaphoreType.DMA((8,)),
        ],
        compiler_params=pltpu.CompilerParams(vmem_limit_bytes=VMEM_LIMIT),
        cost_estimate=pl.CostEstimate(flops=2 * 10**9, bytes_accessed=11 * 10**6, transcendentals=0),
        name=f"gram{half}",
    )(lists, sizes, tallies, *blocks)


def join_body(pos, *refs):
    parts = refs[:8]
    outs = refs[8:]
    z = pos[3]

    def total(rows):
        value = parts[0][rows, :]
        for part in parts[1:]:
            value = value + part[rows, :]
        return value

    for dz in range(NZ):
        q = lax.rem(z + dz, NZ)

        def step(i, _, dz=dz, q=q):
            outs[dz][pl.ds(pl.multiple_of(i * ROWS, ROWS), ROWS), :] = total(
                pl.ds(pl.multiple_of(q * QPACKED + i * ROWS, ROWS), ROWS)
            )
            return 0

        lax.fori_loop(0, QCELL, step, 0)
        for k in range(3):
            outs[dz][pl.ds(QPACKED + k * QCELL, QCELL), :] = total(
                pl.ds(pl.multiple_of(PACKED + k * CELL_DEV + q * QCELL, QCELL), QCELL)
            )


def join(pos, parts):
    vmem = pl.BlockSpec(memory_space=pltpu.VMEM)
    return pl.pallas_call(
        join_body,
        out_shape=[jax.ShapeDtypeStruct((QPIECE, D), F32)] * NZ,
        in_specs=[pl.BlockSpec(memory_space=pltpu.SMEM)] + [vmem] * 8,
        out_specs=[vmem] * NZ,
        compiler_params=pltpu.CompilerParams(vmem_limit_bytes=VMEM_LIMIT),
        name="join",
    )(pos, *parts)


def finish_body(pos, *refs):
    parts = refs[:NZ]
    mean_out, cov_out = refs[NZ:]
    z = pos[3]
    row = lax.broadcasted_iota(I32, (ROWS, D), 0)
    lane = lax.broadcasted_iota(I32, (ROWS, D), 1)
    for dz in range(NZ):
        q = lax.rem(z + NZ - dz, NZ)
        part = parts[dz]
        sums = part[pl.ds(QPACKED, QCELL), :]
        counts = part[pl.ds(QPACKED + 2 * QCELL, QCELL), :]
        safe = jnp.maximum(counts, 1.0)
        mean = sums / safe
        inverse = 1.0 / safe
        mean_out[pl.ds(pl.multiple_of(q * QCELL, QCELL), QCELL), :] = mean
        scaled = jnp.transpose(jnp.concatenate([mean * counts] * (D // QCELL), axis=0))
        for j in range(QCELL):
            packed = part[pl.ds(j * ROWS, ROWS), :]
            diagonal = part[pl.ds(QPACKED + QCELL + j, 1), :]
            flipped = jnp.transpose(jnp.concatenate([packed, packed], axis=0))
            rolled = pltpu.roll(packed, ROWS, 1)
            high, low = flipped[:ROWS], flipped[ROWS:]
            top = jnp.where(lane >= row, packed, high)
            corner = jnp.where(lane - ROWS < row, rolled, jnp.where(lane - ROWS == row, diagonal, high))
            bottom = jnp.where(lane < ROWS, low, corner)
            full = jnp.concatenate([top, bottom], axis=0)
            outer = scaled[:, j : j + 1] * mean[j : j + 1, :]
            cov_out[q * QCELL + j] = (full - outer) * inverse[j : j + 1, :]


def finish(pos, parts):
    vmem = pl.BlockSpec(memory_space=pltpu.VMEM)
    return pl.pallas_call(
        finish_body,
        out_shape=[
            jax.ShapeDtypeStruct((CELL_DEV, D), F32),
            jax.ShapeDtypeStruct((CELL_DEV, D, D), F32),
        ],
        in_specs=[pl.BlockSpec(memory_space=pltpu.SMEM)] + [vmem] * NZ,
        out_specs=[vmem, vmem],
        compiler_params=pltpu.CompilerParams(vmem_limit_bytes=VMEM_LIMIT),
        name="finish",
    )(pos, *parts)


def local(vectors, block_cells, dest_counts):
    x, y, c = place()
    pos = jnp.stack([x, y, c, lax.axis_index("dp")]).astype(I32)
    counts = dest_counts[0, 0]
    sent = pack(pos, counts, vectors[0])
    meta = lax.all_gather(jnp.concatenate([block_cells[0], counts]), "cell")
    halves = ([], [])
    for g, (d, dc) in enumerate(SHIFTS):
        for half in (0, 1):
            block = sent[half * GROUPS + g]
            if d or dc:
                block = lax.ppermute(block, "cell", cell_perm(d, 0, dc) if half == 0 else cell_perm(0, d, dc))
            halves[half].append(block)
    lists, sizes, tallies = make_lists(pos, meta)
    parts = []
    for half in (0, 1):
        pieces = gram(half, lists, sizes, tallies, halves[half])
        parts.append(pieces[0])
        for d in range(1, 4):
            parts.append(lax.ppermute(pieces[d], "cell", cell_perm(0, d, 0) if half == 0 else cell_perm(d, 0, 0)))
    quarters = join(pos, parts)
    mine = quarters[0]
    for dz in range(1, NZ):
        mine = mine + lax.ppermute(quarters[dz], "dp", dp_perm(dz))
    whole = [mine] + [lax.ppermute(mine, "dp", dp_perm(dz)) for dz in range(1, NZ)]
    return tuple(finish(pos, whole))


def solution(mesh):
    in_specs = (P("dp", "cell", None, None), P("dp", "cell"), P("dp", "cell", None))
    out_specs = (P("cell", None), P("cell", None, None))
    return jax.shard_map(local, mesh=mesh, in_specs=in_specs, out_specs=out_specs, check_vma=False)
```

time: 476 us -> 842 us (1.77)
  Pallas kernels: 0 us -> 439 us
  blocking collectives: 18.7 us -> 162 us
  waiting for transfers between devices: 261 us -> 127 us
  matrix products: 96.8 us -> 0 us
  starting transfers between devices: 15.9 us -> 97.3 us
  other arithmetic: 34.6 us -> 0.83 us
  local copies, waits for them, and re-layouts: 32.7 us -> 14.7 us
  between operations: 14.8 us -> 1.51 us
    pallas_call x0 -> x6, Pallas kernels: none -> 439 us  [the longest x1 384 us: pack(): pl.pallas_call(pack_body, out_shape=[shape] * (2 * GROUPS), in_specs=[pl....]
    all_to_all x2 -> x0, waiting for transfers between devices: 174 us -> none  [the longest x1 174 us: local(): lax.all_to_all(outgoing, 'cell', split_axis=0, concat_axis=0, tiled=True)]
    unnamed x1, blocking collectives: 8.5 us -> 162 us
    ppermute x0 -> x26, waiting for transfers between devices: none -> 127 us  [the longest x14 55.9 us: local(): lax.ppermute(block, 'cell', cell_perm(d, 0, dc) if half == 0 else cell_pe...]
    ppermute x0 -> x26, starting transfers between devices: none -> 97.3 us  [the longest x6 63.4 us: local(): lax.ppermute(pieces[d], 'cell', cell_perm(0, d, 0) if half == 0 else cell...]
    dot_general x9 -> x0, matrix products: 96.8 us -> none  [the longest x3 61.3 us: accumulate(): jnp.dot(onehot, gram_blocks, precision=lax.Precision.HIGHEST)]
    all_gather x1 -> x0, waiting for transfers between devices: 86.9 us -> none  [joined(): gathered = jax.tree.map(lambda a: lax.all_gather(a, axis), part)]
    gather x4 -> x0, local copies, waits for them, and re-layouts: 27.4 us -> none  [the longest x1 22.3 us: local(): jnp.take(vectors[0], block_index, axis=0)]
  transfers between devices with their start and end apart: 3 -> 26, of which waited for: 2 -> 13; matrix products, arithmetic and copies ran while one was open for 7% -> 0% of each run, Pallas kernels for 0% -> 6%
where the time goes in v1:
time: 842 us; the launch traced here: 843 us
  Pallas kernels  439 us (52%)
  blocking collectives  162 us (19%)
  waiting for transfers between devices  127 us (15%)
  starting transfers between devices  97.3 us (12%)
  local copies, waits for them, and re-layouts  14.7 us (2%)
    pallas_call x1, Pallas kernels, pack(): pl.pallas_call(pack_body, out_shape=[shape] * (2 * GROUPS), in_specs=[pl....  384 us
    unnamed x1, blocking collectives  162 us
    ppermute x6, starting transfers between devices, local(): lax.ppermute(pieces[d], 'cell', cell_perm(0, d, 0) if half == 0 else cell...  63.4 us
    ppermute x14, waiting for transfers between devices, local(): lax.ppermute(block, 'cell', cell_perm(d, 0, dc) if half == 0 else cell_pe...  55.9 us
    ppermute x6, waiting for transfers between devices, local(): lax.ppermute(pieces[d], 'cell', cell_perm(0, d, 0) if half == 0 else cell...  46.2 us
    pallas_call x2, Pallas kernels, gram(): pl.pallas_call(body, out_shape=[jax.ShapeDtypeStruct((PIECE, D), F32)] *...  28.4 us
    ppermute x14, starting transfers between devices, local(): lax.ppermute(block, 'cell', cell_perm(d, 0, dc) if half == 0 else cell_pe...  21.8 us
    pallas_call x1, Pallas kernels, make_lists(): pl.pallas_call(lists_body, out_shape=[jax.ShapeDtypeStruct((2 * LIST + OW...  20.6 us
  transfers between devices with their start and end apart: 26, of which 13 were waited for; matrix products, arithmetic and copies ran while one was open for 0% of the time, Pallas kernels for 6%

profile of v1, /device:TPU:1, one launch (start us, length us, event | category | flops | bytes accessed | tf_op | source)
XLA Modules:
  0.0 842.5 jit_solution(2856381889370151590)
XLA Ops:
  1.3 383.7 %pack.1 = (bf16[48,64,128]{2,1,0:T(8,128)(2,1)}, bf16[48,64,128]{2,1,0:T(8,128)(2,1)}, bf16[48,64,128]{2,1,0:T(8,128)(2,1)}, bf16[48,64,128]{2,1,0:T(8,128)(2,1)...) custom-call(s32[4]{0:T(128)} %pad_add_fusion.pos, ...), custom_call_target="tpu_custom_call" | custom-call | tf_op jit(solution)/shard_map/pack/pallas_call | solution.py:95
  393.0 14.3 %collective-permute-done.11.refs_5_ = bf16[48,64,128]{2,1,0:T(8,128)(2,1)S(1)} collective-permute-done((bf16[48,64,128]{2,1,0:T(8,128)(2,1)}, bf16[48,64,128]{2,1,0:T(8,128)(2,1)S(1)}, u32[]{:S(2)}, u32[]{:S(2)}) %collective-permute-start.11) | collective-permute-done | bytes 786464 | tf_op jit(solution)/shard_map/ppermute | solution.py:370
  408.2 2.7 collective-permute-start.16
  410.9 13.2 %collective-permute-done.12.refs_6_ = bf16[48,64,128]{2,1,0:T(8,128)(2,1)S(1)} collective-permute-done((bf16[48,64,128]{2,1,0:T(8,128)(2,1)}, bf16[48,64,128]{2,1,0:T(8,128)(2,1)S(1)}, u32[]{:S(2)}, u32[]{:S(2)}) %collective-permute-start.12) | collective-permute-done | bytes 786464 | tf_op jit(solution)/shard_map/ppermute | solution.py:370
  431.4 162.2 %all-reduce = s32[13312]{0:T(1024)S(1)} all-reduce(s32[13312]{0:T(1024)S(1)} %add_dynamic-update-slice_fusion), channel_id=2, replica_groups=mesh['dp'=4,'cell'=32] {'cell'}, use_global_device_ids=true, to_apply=%add | all-reduce | flops 13312 | bytes 106496
  594.3 20.6 %lists.1 = (s32[1824]{0:T(1024)}, s32[2]{0:T(128)}, s32[256]{0:T(256)}) custom-call(s32[4]{0:T(128)} %pad_add_fusion.pos, s32[32,416]{1,0:T(8,128)} %reshape.4.meta), custom_call_target="tpu_custom_call" | custom-call | tf_op jit(solution)/shard_map/lists/pallas_call | solution.py:154
  622.6 14.6 %gram1.1 = (f32[2144,128]{1,0:T(8,128)}, f32[2144,128]{1,0:T(8,128)}, f32[2144,128]{1,0:T(8,128)}, f32[2144,128]{1,0:T(8,128)}) custom-call(s32[1824]{0:T(1024)S(1)} %copy-done.12, s32[2]{0:T(128)S(1)} %copy-done.14, s32[256]{0:T(256)S(1)} %copy-done.13, bf16[48,64,128]{2,1,0:T(8,128)(2,1)S(1)} %copy-done.3, ...), custom_call_target="tpu_custom_call" | custom-call | flops 2000000000 | bytes 11000000 | tf_op jit(solution)/shard_map/gram1/pallas_call | solution.py:255
  637.3 2.7 collective-permute-start.3
  642.3 3.0 collective-permute-start.6
  645.2 9.7 %collective-permute-done.3.refs_7_ = bf16[48,64,128]{2,1,0:T(8,128)(2,1)S(1)} collective-permute-done((bf16[48,64,128]{2,1,0:T(8,128)(2,1)S(1)}, bf16[48,64,128]{2,1,0:T(8,128)(2,1)S(1)}, u32[]{:S(2)}, u32[]{:S(2)}) %collective-permute-start.3) | collective-permute-done | bytes 786464 | tf_op jit(solution)/shard_map/ppermute | solution.py:370
  657.2 18.6 %collective-permute-done.4.refs_8_ = bf16[48,64,128]{2,1,0:T(8,128)(2,1)S(1)} collective-permute-done((bf16[48,64,128]{2,1,0:T(8,128)(2,1)S(1)}, bf16[48,64,128]{2,1,0:T(8,128)(2,1)S(1)}, u32[]{:S(2)}, u32[]{:S(2)}) %collective-permute-start.4) | collective-permute-done | bytes 786464 | tf_op jit(solution)/shard_map/ppermute | solution.py:370
  675.8 58.3 %collective-permute-start.19 = (f32[2144,128]{1,0:T(8,128)}, f32[2144,128]{1,0:T(8,128)S(1)}, u32[]{:S(2)}, u32[]{:S(2)}) collective-permute-start(f32[2144,128]{1,0:T(8,128)} %get-tuple-element.59), channel_id=1, source_target_pairs={{0,24},{1,25},{2,26},{3,27},{4,28},{5,29},{6,30},{7,31},{8,0},{9,1... | collective-permute-start | bytes 3293192 | tf_op jit(solution)/shard_map/ppermute | solution.py:378
  735.0 13.8 %gram0.1 = (f32[2144,128]{1,0:T(8,128)}, f32[2144,128]{1,0:T(8,128)}, f32[2144,128]{1,0:T(8,128)}, f32[2144,128]{1,0:T(8,128)}) custom-call(s32[1824]{0:T(1024)S(1)} %copy-done.12, s32[2]{0:T(128)S(1)} %copy-done.14, s32[256]{0:T(256)S(1)} %copy-done.13, bf16[48,64,128]{2,1,0:T(8,128)(2,1)S(1)} %copy-done.2, ...), custom_call_target="tpu_custom_call" | custom-call | flops 2000000000 | bytes 11000000 | tf_op jit(solution)/shard_map/gram0/pallas_call | solution.py:255
  749.0 2.6 collective-permute-start.9
  751.6 3.9 collective-permute-done.19.refs_7_
  755.6 18.4 %collective-permute-done.7.refs_1_ = f32[2144,128]{1,0:T(8,128)S(1)} collective-permute-done((f32[2144,128]{1,0:T(8,128)}, f32[2144,128]{1,0:T(8,128)S(1)}, u32[]{:S(2)}, u32[]{:S(2)}) %collective-permute-start.7) | collective-permute-done | bytes 1097760 | tf_op jit(solution)/shard_map/ppermute | solution.py:378
  774.0 22.4 %collective-permute-done.8.refs_2_ = f32[2144,128]{1,0:T(8,128)S(1)} collective-permute-done((f32[2144,128]{1,0:T(8,128)}, f32[2144,128]{1,0:T(8,128)S(1)}, u32[]{:S(2)}, u32[]{:S(2)}) %collective-permute-start.8) | collective-permute-done | bytes 1097760 | tf_op jit(solution)/shard_map/ppermute | solution.py:378
  799.1 2.9 join.1
  802.0 4.9 collective-permute-start.20
  811.9 8.7 %collective-permute-done.21 = f32[536,128]{1,0:T(8,128)S(1)} collective-permute-done((f32[536,128]{1,0:T(8,128)S(1)}, f32[536,128]{1,0:T(8,128)S(1)}, u32[]{:S(2)}, u32[]{:S(2)}) %collective-permute-start.21) | collective-permute-done | bytes 274464 | tf_op jit(solution)/shard_map/ppermute | solution.py:382
  824.8 4.6 collective-permute-done.25.refs_3_
  829.4 2.7 collective-permute-done.24.refs_2_
  832.0 7.0 collective-permute-done.23.refs_1_
  839.0 3.5 finish.1
  (94 shorter events, 41.9 us)
Async XLA Ops:
  386.5 20.8 %collective-permute-start.11 = (bf16[48,64,128]{2,1,0:T(8,128)(2,1)}, bf16[48,64,128]{2,1,0:T(8,128)(2,1)S(1)}, u32[]{:S(2)}, u32[]{:S(2)}) collective-permute-start(bf16[48,64,128]{2,1,0:T(8,128)(2,1)} %get-tuple-element.50), channel_id=1, source_target_pairs={{0,2},{1,3},{2,4},{3,5},{4,6},{5,7},{6,0},{7,1},{8,10},{9,11},{10,... | collective-permute-start | bytes 2359304 | tf_op jit(solution)/shard_map/ppermute | solution.py:370
  387.9 36.3 %collective-permute-start.12 = (bf16[48,64,128]{2,1,0:T(8,128)(2,1)}, bf16[48,64,128]{2,1,0:T(8,128)(2,1)S(1)}, u32[]{:S(2)}, u32[]{:S(2)}) collective-permute-start(bf16[48,64,128]{2,1,0:T(8,128)(2,1)} %get-tuple-element.51), channel_id=1, source_target_pairs={{0,3},{1,2},{2,5},{3,4},{4,7},{5,6},{6,1},{7,0},{8,11},{9,10},{10,... | collective-permute-start | bytes 2359304 | tf_op jit(solution)/shard_map/ppermute | solution.py:370
  389.4 36.0 %collective-permute-start.13 = (bf16[48,64,128]{2,1,0:T(8,128)(2,1)}, bf16[48,64,128]{2,1,0:T(8,128)(2,1)S(1)}, u32[]{:S(2)}, u32[]{:S(2)}) collective-permute-start(bf16[48,64,128]{2,1,0:T(8,128)(2,1)} %get-tuple-element.52), channel_id=1, source_target_pairs={{0,6},{1,7},{2,0},{3,1},{4,2},{5,3},{6,4},{7,5},{8,14},{9,15},{10,... | collective-permute-start | bytes 2359304 | tf_op jit(solution)/shard_map/ppermute | solution.py:370
  390.8 36.7 %collective-permute-start.14 = (bf16[48,64,128]{2,1,0:T(8,128)(2,1)}, bf16[48,64,128]{2,1,0:T(8,128)(2,1)S(1)}, u32[]{:S(2)}, u32[]{:S(2)}) collective-permute-start(bf16[48,64,128]{2,1,0:T(8,128)(2,1)} %get-tuple-element.53), channel_id=1, source_target_pairs={{0,7},{1,6},{2,1},{3,0},{4,3},{5,2},{6,5},{7,4},{8,15},{9,14},{10,... | collective-permute-start | bytes 2359304 | tf_op jit(solution)/shard_map/ppermute | solution.py:370
  391.4 223.5 %collective-permute-start.15 = (bf16[48,64,128]{2,1,0:T(8,128)(2,1)}, bf16[48,64,128]{2,1,0:T(8,128)(2,1)}, u32[]{:S(2)}, u32[]{:S(2)}) collective-permute-start(bf16[48,64,128]{2,1,0:T(8,128)(2,1)} %get-tuple-element.54), channel_id=1, source_target_pairs={{0,4},{1,5},{2,6},{3,7},{4,0},{5,1},{6,2},{7,3},{8,12},{9,13},{10,... | collective-permute-start | bytes 2359304 | tf_op jit(solution)/shard_map/ppermute | solution.py:370
  408.2 206.7 %collective-permute-start.16 = (bf16[48,64,128]{2,1,0:T(8,128)(2,1)}, bf16[48,64,128]{2,1,0:T(8,128)(2,1)}, u32[]{:S(2)}, u32[]{:S(2)}) collective-permute-start(bf16[48,64,128]{2,1,0:T(8,128)(2,1)} %get-tuple-element.55), channel_id=1, source_target_pairs={{0,5},{1,4},{2,7},{3,6},{4,1},{5,0},{6,3},{7,2},{8,13},{9,12},{10,... | collective-permute-start | bytes 2359304 | tf_op jit(solution)/shard_map/ppermute | solution.py:370
  425.1 214.8 %collective-permute-start = (bf16[48,64,128]{2,1,0:T(8,128)(2,1)}, bf16[48,64,128]{2,1,0:T(8,128)(2,1)S(1)}, u32[]{:S(2)}, u32[]{:S(2)}) collective-permute-start(bf16[48,64,128]{2,1,0:T(8,128)(2,1)} %get-tuple-element.37), channel_id=1, source_target_pairs={{0,1},{1,0},{2,3},{3,2},{4,5},{5,4},{6,7},{7,6},{8,9},{9,8},{10,11... | collective-permute-start | bytes 2359304 | tf_op jit(solution)/shard_map/ppermute | solution.py:370
  426.3 215.3 %collective-permute-start.1 = (bf16[48,64,128]{2,1,0:T(8,128)(2,1)}, bf16[48,64,128]{2,1,0:T(8,128)(2,1)S(1)}, u32[]{:S(2)}, u32[]{:S(2)}) collective-permute-start(bf16[48,64,128]{2,1,0:T(8,128)(2,1)} %get-tuple-element.38), channel_id=1, source_target_pairs={{0,8},{1,9},{2,10},{3,11},{4,12},{5,13},{6,14},{7,15},{8,16},{9,17... | collective-permute-start | bytes 2359304 | tf_op jit(solution)/shard_map/ppermute | solution.py:370
  428.4 213.9 %collective-permute-start.2 = (bf16[48,64,128]{2,1,0:T(8,128)(2,1)}, bf16[48,64,128]{2,1,0:T(8,128)(2,1)S(1)}, u32[]{:S(2)}, u32[]{:S(2)}) collective-permute-start(bf16[48,64,128]{2,1,0:T(8,128)(2,1)} %get-tuple-element.39), channel_id=1, source_target_pairs={{0,9},{1,8},{2,11},{3,10},{4,13},{5,12},{6,15},{7,14},{8,17},{9,16... | collective-permute-start | bytes 2359304 | tf_op jit(solution)/shard_map/ppermute | solution.py:370
  637.2 111.9 %collective-permute-start.17 = (f32[2144,128]{1,0:T(8,128)}, f32[2144,128]{1,0:T(8,128)S(1)}, u32[]{:S(2)}, u32[]{:S(2)}) collective-permute-start(f32[2144,128]{1,0:T(8,128)} %get-tuple-element.57), channel_id=1, source_target_pairs={{0,8},{1,9},{2,10},{3,11},{4,12},{5,13},{6,14},{7,15},{8,16},{9,17... | collective-permute-start | bytes 3293192 | tf_op jit(solution)/shard_map/ppermute | solution.py:378
  637.3 17.7 %collective-permute-start.3 = (bf16[48,64,128]{2,1,0:T(8,128)(2,1)S(1)}, bf16[48,64,128]{2,1,0:T(8,128)(2,1)S(1)}, u32[]{:S(2)}, u32[]{:S(2)}) collective-permute-start(bf16[48,64,128]{2,1,0:T(8,128)(2,1)S(1)} %copy-done.23), channel_id=1, source_target_pairs={{0,24},{1,25},{2,26},{3,27},{4,28},{5,29},{6,30},{7,31},{8,0},{9,1... | collective-permute-start | bytes 2359304 | tf_op jit(solution)/shard_map/ppermute | solution.py:370
  639.9 35.8 %collective-permute-start.4 = (bf16[48,64,128]{2,1,0:T(8,128)(2,1)S(1)}, bf16[48,64,128]{2,1,0:T(8,128)(2,1)S(1)}, u32[]{:S(2)}, u32[]{:S(2)}) collective-permute-start(bf16[48,64,128]{2,1,0:T(8,128)(2,1)S(1)} %copy-done.22), channel_id=1, source_target_pairs={{0,25},{1,24},{2,27},{3,26},{4,29},{5,28},{6,31},{7,30},{8,1},{9,0... | collective-permute-start | bytes 2359304 | tf_op jit(solution)/shard_map/ppermute | solution.py:370
  641.7 92.4 %collective-permute-start.5 = (bf16[48,64,128]{2,1,0:T(8,128)(2,1)S(1)}, bf16[48,64,128]{2,1,0:T(8,128)(2,1)S(1)}, u32[]{:S(2)}, u32[]{:S(2)}) collective-permute-start(bf16[48,64,128]{2,1,0:T(8,128)(2,1)S(1)} %copy-done.21), channel_id=1, source_target_pairs={{0,16},{1,17},{2,18},{3,19},{4,20},{5,21},{6,22},{7,23},{8,24},{9,... | collective-permute-start | bytes 2359304 | tf_op jit(solution)/shard_map/ppermute | solution.py:370
  642.3 91.8 %collective-permute-start.6 = (bf16[48,64,128]{2,1,0:T(8,128)(2,1)S(1)}, bf16[48,64,128]{2,1,0:T(8,128)(2,1)S(1)}, u32[]{:S(2)}, u32[]{:S(2)}) collective-permute-start(bf16[48,64,128]{2,1,0:T(8,128)(2,1)S(1)} %copy-done.20), channel_id=1, source_target_pairs={{0,17},{1,16},{2,19},{3,18},{4,21},{5,20},{6,23},{7,22},{8,25},{9,... | collective-permute-start | bytes 2359304 | tf_op jit(solution)/shard_map/ppermute | solution.py:370
  655.0 96.7 %collective-permute-start.18 = (f32[2144,128]{1,0:T(8,128)}, f32[2144,128]{1,0:T(8,128)S(1)}, u32[]{:S(2)}, u32[]{:S(2)}) collective-permute-start(f32[2144,128]{1,0:T(8,128)} %get-tuple-element.58), channel_id=1, source_target_pairs={{0,16},{1,17},{2,18},{3,19},{4,20},{5,21},{6,22},{7,23},{8,24},{9,... | collective-permute-start | bytes 3293192 | tf_op jit(solution)/shard_map/ppermute | solution.py:378
  675.8 79.8 %collective-permute-start.19 = (f32[2144,128]{1,0:T(8,128)}, f32[2144,128]{1,0:T(8,128)S(1)}, u32[]{:S(2)}, u32[]{:S(2)}) collective-permute-start(f32[2144,128]{1,0:T(8,128)} %get-tuple-element.59), channel_id=1, source_target_pairs={{0,24},{1,25},{2,26},{3,27},{4,28},{5,29},{6,30},{7,31},{8,0},{9,1... | collective-permute-start | bytes 3293192 | tf_op jit(solution)/shard_map/ppermute | solution.py:378
  748.8 25.2 %collective-permute-start.7 = (f32[2144,128]{1,0:T(8,128)}, f32[2144,128]{1,0:T(8,128)S(1)}, u32[]{:S(2)}, u32[]{:S(2)}) collective-permute-start(f32[2144,128]{1,0:T(8,128)} %get-tuple-element.45), channel_id=1, source_target_pairs={{0,2},{1,3},{2,4},{3,5},{4,6},{5,7},{6,0},{7,1},{8,10},{9,11},{10,... | collective-permute-start | bytes 3293192 | tf_op jit(solution)/shard_map/ppermute | solution.py:378
  748.9 47.5 %collective-permute-start.8 = (f32[2144,128]{1,0:T(8,128)}, f32[2144,128]{1,0:T(8,128)S(1)}, u32[]{:S(2)}, u32[]{:S(2)}) collective-permute-start(f32[2144,128]{1,0:T(8,128)} %get-tuple-element.46), channel_id=1, source_target_pairs={{0,4},{1,5},{2,6},{3,7},{4,0},{5,1},{6,2},{7,3},{8,12},{9,13},{10,... | collective-permute-start | bytes 3293192 | tf_op jit(solution)/shard_map/ppermute | solution.py:378
  749.0 48.8 %collective-permute-start.9 = (f32[2144,128]{1,0:T(8,128)}, f32[2144,128]{1,0:T(8,128)S(1)}, u32[]{:S(2)}, u32[]{:S(2)}) collective-permute-start(f32[2144,128]{1,0:T(8,128)} %get-tuple-element.47), channel_id=1, source_target_pairs={{0,6},{1,7},{2,0},{3,1},{4,2},{5,3},{6,4},{7,5},{8,14},{9,15},{10,... | collective-permute-start | bytes 3293192 | tf_op jit(solution)/shard_map/ppermute | solution.py:378
  802.0 9.9 %collective-permute-start.20 = (f32[536,128]{1,0:T(8,128)S(1)}, f32[536,128]{1,0:T(8,128)S(1)}, u32[]{:S(2)}, u32[]{:S(2)}) collective-permute-start(f32[536,128]{1,0:T(8,128)S(1)} %get-tuple-element.61), channel_id=1, source_target_pairs={{0,32},{32,64},{64,96},{96,0},{1,33},{33,65},{65,97},{97,1},{2,34}... | collective-permute-start | bytes 823304 | tf_op jit(solution)/shard_map/ppermute | solution.py:382
  806.9 13.8 %collective-permute-start.21 = (f32[536,128]{1,0:T(8,128)S(1)}, f32[536,128]{1,0:T(8,128)S(1)}, u32[]{:S(2)}, u32[]{:S(2)}) collective-permute-start(f32[536,128]{1,0:T(8,128)S(1)} %get-tuple-element.62), channel_id=1, source_target_pairs={{0,64},{32,96},{64,0},{96,32},{1,65},{33,97},{65,1},{97,33},{2,66}... | collective-permute-start | bytes 823304 | tf_op jit(solution)/shard_map/ppermute | solution.py:382
  808.1 12.5 %collective-permute-start.22 = (f32[536,128]{1,0:T(8,128)S(1)}, f32[536,128]{1,0:T(8,128)S(1)}, u32[]{:S(2)}, u32[]{:S(2)}) collective-permute-start(f32[536,128]{1,0:T(8,128)S(1)} %get-tuple-element.63), channel_id=1, source_target_pairs={{0,96},{32,0},{64,32},{96,64},{1,97},{33,1},{65,33},{97,65},{2,98}... | collective-permute-start | bytes 823304 | tf_op jit(solution)/shard_map/ppermute | solution.py:382
  823.2 8.9 %collective-permute-start.24 = (f32[536,128]{1,0:T(8,128)S(1)}, f32[536,128]{1,0:T(8,128)S(1)}, u32[]{:S(2)}, u32[]{:S(2)}) collective-permute-start(f32[536,128]{1,0:T(8,128)S(1)} %add_add_fusion.refs_0_), channel_id=1, source_target_pairs={{0,64},{32,96},{64,0},{96,32},{1,65},{33,97},{65,1},{97,33},{2,66}... | collective-permute-start | bytes 823304 | tf_op jit(solution)/shard_map/ppermute | solution.py:383
  824.0 15.0 %collective-permute-start.23 = (f32[536,128]{1,0:T(8,128)S(1)}, f32[536,128]{1,0:T(8,128)S(1)}, u32[]{:S(2)}, u32[]{:S(2)}) collective-permute-start(f32[536,128]{1,0:T(8,128)S(1)} %add_add_fusion.refs_0_), channel_id=1, source_target_pairs={{0,32},{32,64},{64,96},{96,0},{1,33},{33,65},{65,97},{97,1},{2,34}... | collective-permute-start | bytes 823304 | tf_op jit(solution)/shard_map/ppermute | solution.py:383
  (28 other events, 1699.2 us)

commit v2 on v1

v2 whole, which is shorter than its diff:
```python
import jax
import jax.numpy as jnp
from jax import lax
from jax.experimental import pallas as pl
from jax.experimental.pallas import tpu as pltpu
from jax.sharding import PartitionSpec as P

CELLS = 1024
NX = NY = NZ = 4
NC = 2
OWNERS = NX * NY * NC
CELL_DEV = CELLS // OWNERS
BLK = 384
ROWS = 64
D = 128
RUN = 24
SLOTS = 4 * NC * RUN
SHIFTS = (0, 1, 3, 2)
GROUPS = len(SHIFTS)
CHIP_CELLS = NC * CELL_DEV
TRASH = 4 * CHIP_CELLS
SHIFT_BITS = 9
LIST = GROUPS * SLOTS + 128
PAIR = 8
F32 = jnp.float32
I32 = jnp.int32
META = 512
PACKED = CELL_DEV * ROWS
PIECE = PACKED + 3 * CELL_DEV
QCELL = CELL_DEV // NZ
QPACKED = QCELL * ROWS
QPIECE = QPACKED + 3 * QCELL
VMEM_LIMIT = 32 * 1024 * 1024

SMEM_SPEC = pl.BlockSpec(memory_space=pltpu.SMEM)
VMEM_SPEC = pl.BlockSpec(memory_space=pltpu.VMEM)
HBM_SPEC = pl.BlockSpec(memory_space=pltpu.HBM)


def at(x, y, c):
    return (x * NY + y) * NC + c


def cell_perm(even, odd, dc=0):
    steps = (even, odd)
    return [
        (at(x, y, c), at((x + steps[c][0]) % NX, (y + steps[c][1]) % NY, c ^ dc))
        for x in range(NX)
        for y in range(NY)
        for c in range(NC)
    ]


def along(d):
    return cell_perm((d, 0), (0, d))


def across(d):
    return cell_perm((0, d), (d, 0))


SWAP = cell_perm((0, 0), (0, 0), 1)


def dp_perm(dz):
    return [(z, (z + dz) % NZ) for z in range(NZ)]


def place():
    me = lax.axis_index("cell")
    x, y, c = me // (NY * NC), (me // NC) % NY, me % NC
    first, second = jnp.where(c == 0, x, y), jnp.where(c == 0, y, x)
    return jnp.stack([first, second, c, lax.axis_index("dp")]).astype(I32)


def owner(c, first, second, oc):
    return jnp.where(c == 0, at(first, second, oc), at(second, first, oc))


def pack_body(pos, counts, vectors, *refs):
    outs = refs[:GROUPS]
    offsets, sems = refs[GROUPS:]
    total = jnp.int32(0)
    for o in range(OWNERS):
        offsets[o] = total
        total = total + counts[o]
    copies = []
    for g, d in enumerate(SHIFTS):
        for k in range(4):
            for oc in range(NC):
                o = owner(pos[2], (pos[0] + d) % 4, k, oc)
                start = jnp.minimum(offsets[o], BLK - RUN)
                copies.append(
                    pltpu.make_async_copy(
                        vectors.at[pl.ds(start, RUN)],
                        outs[g].at[pl.ds((k * NC + oc) * RUN, RUN)],
                        sems.at[(g * 4 + k) * NC + oc],
                    )
                )
                copies[-1].start()
    for copy in copies:
        copy.wait()


def pack(pos, counts, vectors):
    shape = jax.ShapeDtypeStruct((SLOTS, ROWS, D), vectors.dtype)
    return pl.pallas_call(
        pack_body,
        out_shape=[shape] * GROUPS,
        in_specs=[SMEM_SPEC, SMEM_SPEC, VMEM_SPEC],
        out_specs=[HBM_SPEC] * GROUPS,
        scratch_shapes=[pltpu.SMEM((OWNERS,), I32), pltpu.SemaphoreType.DMA((OWNERS,))],
        compiler_params=pltpu.CompilerParams(vmem_limit_bytes=VMEM_LIMIT),
        name="pack",
    )(pos, counts, vectors)


def lists_body(pos, *refs):
    metas = refs[:GROUPS]
    lists, sizes, tallies, offsets = refs[GROUPS:]

    def clear(i, _):
        for u in range(8):
            tallies[i * 8 + u] = jnp.int32(0)
        return 0

    lax.fori_loop(0, TRASH // 8, clear, 0)
    for g in range(GROUPS):
        total = jnp.int32(0)
        for o in range(OWNERS):
            offsets[g * OWNERS + o] = total
            total = total + metas[g][BLK + o]
    filled = jnp.int32(0)
    begin = jnp.int32(0)
    for g in range(GROUPS):
        for k in range(4):
            for oc in range(NC):
                o = owner(pos[2], pos[0], k, oc)
                n = metas[g][BLK + o]
                start = offsets[g * OWNERS + o]
                slot = (k * NC + oc) * RUN + start - jnp.minimum(start, BLK - RUN)
                base = (lax.rem(k + 4 - pos[1], 4) * NC + lax.rem(oc + pos[2], 2)) * CELL_DEV

                def add(j, f, g=g, start=start, slot=slot, base=base):
                    cell = base + metas[g][start + j]
                    lists[f + j] = ((slot + j) << SHIFT_BITS) + cell
                    tallies[cell] = tallies[cell] + ROWS
                    return f

                lax.fori_loop(0, n, add, filled)
                filled = filled + n
        for j in range(PAIR):
            lists[filled + j] = jnp.int32(TRASH)
        sizes[2 * g] = begin
        sizes[2 * g + 1] = (filled - begin + PAIR - 1) // PAIR
        filled = begin + sizes[2 * g + 1] * PAIR
        begin = filled


def make_lists(pos, metas):
    return pl.pallas_call(
        lists_body,
        out_shape=[
            jax.ShapeDtypeStruct((LIST,), I32),
            jax.ShapeDtypeStruct((2 * GROUPS,), I32),
            jax.ShapeDtypeStruct((TRASH,), I32),
        ],
        in_specs=[SMEM_SPEC] * (1 + GROUPS),
        out_specs=[SMEM_SPEC] * 3,
        scratch_shapes=[pltpu.SMEM((GROUPS * OWNERS,), I32)],
        name="lists",
    )(pos, *metas)


def add_blocks(begin, steps, lists, buf, acc, acc_s, acc_q):
    row = lax.broadcasted_iota(I32, (ROWS, D), 0)
    lane = lax.broadcasted_iota(I32, (ROWS, D), 1)
    upper = lane >= row
    contract = (((0,), (0,)), ((), ()))

    def step(i, _):
        done = []
        for u in range(PAIR):
            entry = lists[begin + i * PAIR + u]
            cell = entry & (2**SHIFT_BITS - 1)
            block = buf[entry >> SHIFT_BITS]
            turned = jnp.concatenate([block[:, ROWS:], block[:, :ROWS]], axis=1)
            top = lax.dot_general(block[:, :ROWS], block, contract, preferred_element_type=F32)
            low = lax.dot_general(block[:, ROWS:], turned, contract, preferred_element_type=F32)
            wide = block.astype(F32)
            done.append(
                (
                    cell,
                    jnp.where(upper, top, low),
                    jnp.sum(wide.reshape(8, 8, D), axis=0),
                    jnp.sum((wide * wide).reshape(8, 8, D), axis=0),
                )
            )
        for cell, gram, total, square in done:
            here = pl.ds(pl.multiple_of(cell * ROWS, ROWS), ROWS)
            acc[here, :] = acc[here, :] + gram
            near = pl.ds(pl.multiple_of(cell * 8, 8), 8)
            acc_s[near, :] = acc_s[near, :] + total
            acc_q[near, :] = acc_q[near, :] + square
        return 0

    lax.fori_loop(0, steps, step, 0)


def early_body(lists, sizes, *refs):
    blocks = refs[: GROUPS - 1]
    acc_out, acc_s, acc_q, acc, out_sem = refs[GROUPS - 1 :]

    def clear(i, _):
        acc[pl.ds(pl.multiple_of(i * ROWS, ROWS), ROWS), :] = jnp.zeros((ROWS, D), F32)
        acc_s[pl.ds(pl.multiple_of(i * 8, 8), 8), :] = jnp.zeros((8, D), F32)
        acc_q[pl.ds(pl.multiple_of(i * 8, 8), 8), :] = jnp.zeros((8, D), F32)
        return 0

    lax.fori_loop(0, TRASH + 1, clear, 0)
    for g in range(GROUPS - 1):
        add_blocks(sizes[2 * g], sizes[2 * g + 1], lists, blocks[g], acc, acc_s, acc_q)
    store = pltpu.make_async_copy(acc, acc_out, out_sem.at[0])
    store.start()
    store.wait()


def early(lists, sizes, blocks):
    n = GROUPS - 1
    return pl.pallas_call(
        early_body,
        out_shape=[
            jax.ShapeDtypeStruct(((TRASH + 1) * ROWS, D), F32),
            jax.ShapeDtypeStruct(((TRASH + 1) * 8, D), F32),
            jax.ShapeDtypeStruct(((TRASH + 1) * 8, D), F32),
        ],
        in_specs=[SMEM_SPEC, SMEM_SPEC] + [VMEM_SPEC] * n,
        out_specs=[HBM_SPEC, VMEM_SPEC, VMEM_SPEC],
        scratch_shapes=[
            pltpu.VMEM(((TRASH + 1) * ROWS, D), F32),
            pltpu.SemaphoreType.DMA((1,)),
        ],
        compiler_params=pltpu.CompilerParams(vmem_limit_bytes=VMEM_LIMIT),
        cost_estimate=pl.CostEstimate(flops=2 * 10**9, bytes_accessed=20 * 10**6, transcendentals=0),
        name="early",
    )(lists, sizes, *blocks)


def late_body(lists, sizes, tallies, blocks, acc_in, in_s, in_q, *refs):
    outs = refs[:4]
    acc, acc_s, acc_q, stage, in_sems, out_sems = refs[4:]
    loads = [
        pltpu.make_async_copy(source, target, in_sems.at[i])
        for i, (source, target) in enumerate(((acc_in, acc), (in_s, acc_s), (in_q, acc_q)))
    ]
    for load in loads:
        load.start()
    for load in loads:
        load.wait()
    add_blocks(sizes[2 * GROUPS - 2], sizes[2 * GROUPS - 1], lists, blocks, acc, acc_s, acc_q)
    copies = []
    for part in range(4 * NC):
        copies.append(
            pltpu.make_async_copy(
                acc.at[pl.ds(part * PACKED, PACKED)],
                outs[part // NC].at[pl.ds((part % NC) * PIECE, PACKED)],
                out_sems.at[part],
            )
        )
        copies[-1].start()
    for part in range(4 * NC):
        base = part * 3 * CELL_DEV
        for k, source in enumerate((acc_s, acc_q)):
            total = source[pl.ds(part * CELL_DEV * 8, CELL_DEV, stride=8), :]
            for j in range(1, 8):
                total = total + source[pl.ds(part * CELL_DEV * 8 + j, CELL_DEV, stride=8), :]
            stage[pl.ds(base + k * CELL_DEV, CELL_DEV), :] = total
        for j in range(CELL_DEV):
            count = tallies[part * CELL_DEV + j].astype(F32)
            stage[pl.ds(base + 2 * CELL_DEV + j, 1), :] = jnp.full((1, D), count, F32)
        copies.append(
            pltpu.make_async_copy(
                stage.at[pl.ds(base, 3 * CELL_DEV)],
                outs[part // NC].at[pl.ds((part % NC) * PIECE + PACKED, 3 * CELL_DEV)],
                out_sems.at[4 * NC + part],
            )
        )
        copies[-1].start()
    for copy in copies:
        copy.wait()


def late(lists, sizes, tallies, blocks, acc, acc_s, acc_q):
    return pl.pallas_call(
        late_body,
        out_shape=[jax.ShapeDtypeStruct((NC * PIECE, D), F32)] * 4,
        in_specs=[SMEM_SPEC] * 3 + [VMEM_SPEC] + [HBM_SPEC] * 3,
        out_specs=[HBM_SPEC] * 4,
        scratch_shapes=[
            pltpu.VMEM(((TRASH + 1) * ROWS, D), F32),
            pltpu.VMEM(((TRASH + 1) * 8, D), F32),
            pltpu.VMEM(((TRASH + 1) * 8, D), F32),
            pltpu.VMEM((4 * NC * 3 * CELL_DEV, D), F32),
            pltpu.SemaphoreType.DMA((3,)),
            pltpu.SemaphoreType.DMA((8 * NC,)),
        ],
        compiler_params=pltpu.CompilerParams(vmem_limit_bytes=VMEM_LIMIT),
        cost_estimate=pl.CostEstimate(flops=10**9, bytes_accessed=20 * 10**6, transcendentals=0),
        name="late",
    )(lists, sizes, tallies, blocks, acc, acc_s, acc_q)


def total_body(*refs):
    value = refs[0][...]
    for part in refs[1:-1]:
        value = value + part[...]
    refs[-1][...] = value


def other_total(parts):
    steps = 2
    rows = PIECE // steps
    return pl.pallas_call(
        total_body,
        out_shape=jax.ShapeDtypeStruct((PIECE, D), F32),
        grid=(steps,),
        in_specs=[pl.BlockSpec((rows, D), lambda i: (steps + i, 0))] * len(parts),
        out_specs=pl.BlockSpec((rows, D), lambda i: (i, 0)),
        compiler_params=pltpu.CompilerParams(vmem_limit_bytes=VMEM_LIMIT),
        name="other_total",
    )(*parts)


def join_body(pos, *refs):
    parts = refs[:5]
    outs = refs[5:]
    z = pos[3]

    def total(rows):
        value = parts[0][rows, :]
        for part in parts[1:]:
            value = value + part[rows, :]
        return value

    for dz in range(NZ):
        q = lax.rem(z + dz, NZ)

        def step(i, _, dz=dz, q=q):
            outs[dz][pl.ds(pl.multiple_of(i * ROWS, ROWS), ROWS), :] = total(
                pl.ds(pl.multiple_of(q * QPACKED + i * ROWS, ROWS), ROWS)
            )
            return 0

        lax.fori_loop(0, QCELL, step, 0)
        for k in range(3):
            outs[dz][pl.ds(QPACKED + k * QCELL, QCELL), :] = total(
                pl.ds(pl.multiple_of(PACKED + k * CELL_DEV + q * QCELL, QCELL), QCELL)
            )


def join(pos, parts, swapped):
    own = pl.BlockSpec((PIECE, D), lambda i: (0, 0))
    quarter = pl.BlockSpec((QPIECE, D), lambda i: (0, 0))
    return pl.pallas_call(
        join_body,
        out_shape=[jax.ShapeDtypeStruct((QPIECE, D), F32)] * NZ,
        grid=(1,),
        in_specs=[SMEM_SPEC] + [own] * 5,
        out_specs=[quarter] * NZ,
        compiler_params=pltpu.CompilerParams(vmem_limit_bytes=VMEM_LIMIT),
        name="join",
    )(pos, *parts, swapped)


def finish_body(pos, *refs):
    parts = refs[:NZ]
    mean_out, cov_out = refs[NZ:]
    z = pos[3]
    row = lax.broadcasted_iota(I32, (ROWS, D), 0)
    lane = lax.broadcasted_iota(I32, (ROWS, D), 1)
    for dz in range(NZ):
        q = lax.rem(z + NZ - dz, NZ)
        part = parts[dz]
        sums = part[pl.ds(QPACKED, QCELL), :]
        counts = part[pl.ds(QPACKED + 2 * QCELL, QCELL), :]
        safe = jnp.maximum(counts, 1.0)
        mean = sums / safe
        inverse = 1.0 / safe
        mean_out[pl.ds(pl.multiple_of(q * QCELL, QCELL), QCELL), :] = mean
        scaled = jnp.transpose(jnp.concatenate([mean * counts] * (D // QCELL), axis=0))
        for j in range(QCELL):
            packed = part[pl.ds(j * ROWS, ROWS), :]
            diagonal = part[pl.ds(QPACKED + QCELL + j, 1), :]
            flipped = jnp.transpose(jnp.concatenate([packed, packed], axis=0))
            rolled = pltpu.roll(packed, ROWS, 1)
            high, low = flipped[:ROWS], flipped[ROWS:]
            top = jnp.where(lane >= row, packed, high)
            corner = jnp.where(lane - ROWS < row, rolled, jnp.where(lane - ROWS == row, diagonal, high))
            bottom = jnp.where(lane < ROWS, low, corner)
            full = jnp.concatenate([top, bottom], axis=0)
            outer = scaled[:, j : j + 1] * mean[j : j + 1, :]
            cov_out[q * QCELL + j] = (full - outer) * inverse[j : j + 1, :]


def finish(pos, parts):
    return pl.pallas_call(
        finish_body,
        out_shape=[
            jax.ShapeDtypeStruct((CELL_DEV, D), F32),
            jax.ShapeDtypeStruct((CELL_DEV, D, D), F32),
        ],
        in_specs=[SMEM_SPEC] + [VMEM_SPEC] * NZ,
        out_specs=[VMEM_SPEC, VMEM_SPEC],
        compiler_params=pltpu.CompilerParams(vmem_limit_bytes=VMEM_LIMIT),
        name="finish",
    )(pos, *parts)


def local(vectors, block_cells, dest_counts):
    pos = place()
    counts = dest_counts[0, 0]
    meta = jnp.concatenate([block_cells[0], counts, jnp.zeros((META - BLK - OWNERS,), I32)])
    metas = [meta] + [lax.ppermute(meta, "cell", along(d)) for d in SHIFTS[1:]]
    sent = pack(pos, counts, vectors[0])
    *metas, first, second = lax.optimization_barrier((*metas, sent[1], sent[2]))
    near = [sent[0], lax.ppermute(first, "cell", along(SHIFTS[1])), lax.ppermute(second, "cell", along(SHIFTS[2]))]
    held, *near = lax.optimization_barrier((sent[3], *near))
    far = lax.ppermute(held, "cell", along(SHIFTS[3]))
    lists, sizes, tallies = make_lists(pos, metas)
    pieces = late(lists, sizes, tallies, far, *early(lists, sizes, near))
    parts = [pieces[0]] + [lax.ppermute(pieces[d], "cell", across(d)) for d in range(1, 4)]
    swapped = lax.ppermute(other_total(parts), "cell", SWAP)
    quarters = join(pos, parts, swapped)
    mine = quarters[0]
    for dz in range(1, NZ):
        mine = mine + lax.ppermute(quarters[dz], "dp", dp_perm(dz))
    whole = [mine] + [lax.ppermute(mine, "dp", dp_perm(dz)) for dz in range(1, NZ)]
    return tuple(finish(pos, whole))


def solution(mesh):
    in_specs = (P("dp", "cell", None, None), P("dp", "cell"), P("dp", "cell", None))
    out_specs = (P("cell", None), P("cell", None, None))
    return jax.shard_map(local, mesh=mesh, in_specs=in_specs, out_specs=out_specs, check_vma=False)
```

time: 842 us -> 209 us (0.25)
  Pallas kernels: 439 us -> 43.7 us
  blocking collectives: 162 us -> 0 us
  starting transfers between devices: 97.3 us -> 26.1 us
    pallas_call x4 -> x5, Pallas kernels: 433 us -> 39.2 us  [the longest x1 16.7 us: early(): pl.pallas_call(early_body, out_shape=[jax.ShapeDtypeStruct(((TRASH + 1) *...]
    unnamed x1 -> x0, blocking collectives: 162 us -> none
    ppermute x20 -> x10, starting transfers between devices: 85.2 us -> 15.9 us  [the longest x3 5.22 us: local(): metas = [meta] + [lax.ppermute(meta, 'cell', along(d)) for d in SHIFTS[1:]]]
    ppermute x20 -> x10, waiting for transfers between devices: 102 us -> 94.1 us  [the longest x3 48.3 us: local(): lax.ppermute(pieces[d], 'cell', across(d))]
  transfers between devices with their start and end apart: 26 -> 16, of which waited for: 13 -> 9; matrix products, arithmetic and copies ran while one was open for 0% -> 0% of each run, Pallas kernels for 6% -> 14%
where the time goes in v2:
time: 209 us
  waiting for transfers between devices  121 us (58%)
  Pallas kernels  43.7 us (21%)
  starting transfers between devices  26.1 us (12%)
  local copies, waits for them, and re-layouts  15.5 us (7%)
    ppermute x3, waiting for transfers between devices, local(): lax.ppermute(pieces[d], 'cell', across(d))  48.3 us
    ppermute x1, waiting for transfers between devices, local(): lax.ppermute(first, 'cell', along(SHIFTS[1]))  34.9 us
    pallas_call x1, Pallas kernels, early(): pl.pallas_call(early_body, out_shape=[jax.ShapeDtypeStruct(((TRASH + 1) *...  16.7 us
    unnamed x34, local copies, waits for them, and re-layouts  15.5 us
    ppermute x3, waiting for transfers between devices, local(): lax.ppermute(mine, 'dp', dp_perm(dz))  14.8 us
    ppermute x3, waiting for transfers between devices, local(): mine = mine + lax.ppermute(quarters[dz], 'dp', dp_perm(dz))  12.2 us
    pallas_call x1, Pallas kernels, late(): pl.pallas_call(late_body, out_shape=[jax.ShapeDtypeStruct((NC * PIECE, D)...  9.26 us
    ppermute x1, waiting for transfers between devices, local(): far = lax.ppermute(held, 'cell', along(SHIFTS[3]))  8.52 us
  transfers between devices with their start and end apart: 16, of which 9 were waited for; matrix products, arithmetic and copies ran while one was open for 0% of the time, Pallas kernels for 14%

profile of v2, /device:TPU:1, one launch (start us, length us, event | category | flops | bytes accessed | tf_op | source)
XLA Modules:
  0.0 208.7 jit_solution(13131554707254451066)
XLA Ops:
  2.1 3.8 %collective-permute-start.2 = (s32[512]{0:T(512)S(1)}, s32[512]{0:T(512)S(1)}, u32[]{:S(2)}, u32[]{:S(2)}) collective-permute-start(s32[512]{0:T(512)S(1)} %pad_add_fusion.refs_0_), channel_id=1, source_target_pairs={{0,16},{1,5},{2,18},{3,7},{4,20},{5,1},{6,22},{7,3},{8,24},{9,13},... | collective-permute-start | bytes 6152 | tf_op jit(solution)/shard_map/ppermute | solution.py:423
  7.4 2.8 %copy-done = bf16[1,384,64,128]{3,2,1,0:T(8,128)(2,1)S(1)} copy-done((bf16[1,384,64,128]{3,2,1,0:T(8,128)(2,1)S(1)}, bf16[1,384,64,128]{3,2,1,0:T(8,128)(2,1)}, u32[]{:S(2)}) %copy-start) | copy-done | bytes 6291480
  10.8 7.3 %pack.1 = (bf16[192,64,128]{2,1,0:T(8,128)(2,1)S(1)}, bf16[192,64,128]{2,1,0:T(8,128)(2,1)S(1)}, bf16[192,64,128]{2,1,0:T(8,128)(2,1)S(1)}, bf16[192,64,128]{2,1,0:T(8,128)(2,1)}) custom-call(s32[4]{0:T(128)S(1)} %pad_add_fusion.1.pos, s32[32]{0:T(128)S(1)} %bitcast.8, bf16[384,64,128]{2,1,0:T(8,128)(2,1)S(1)} %bitcast.6), custom_call_target="tpu_custom_call" | custom-call | tf_op jit(solution)/shard_map/pack/pallas_call | solution.py:107
  20.4 2.3 %collective-permute-start.4 = (bf16[192,64,128]{2,1,0:T(8,128)(2,1)S(1)}, bf16[192,64,128]{2,1,0:T(8,128)(2,1)S(1)}, u32[]{:S(2)}, u32[]{:S(2)}) collective-permute-start(bf16[192,64,128]{2,1,0:T(8,128)(2,1)S(1)} %get-tuple-element.42), channel_id=1, source_target_pairs={{0,24},{1,7},{2,26},{3,1},{4,28},{5,3},{6,30},{7,5},{8,0},{9,15},{... | collective-permute-start | bytes 9437192 | tf_op jit(solution)/shard_map/ppermute | solution.py:426
  22.7 34.9 %collective-permute-done.3.refs_1_ = bf16[192,64,128]{2,1,0:T(8,128)(2,1)S(1)} collective-permute-done((bf16[192,64,128]{2,1,0:T(8,128)(2,1)S(1)}, bf16[192,64,128]{2,1,0:T(8,128)(2,1)S(1)}, u32[]{:S(2)}, u32[]{:S(2)}) %collective-permute-start.3) | collective-permute-done | bytes 3145760 | tf_op jit(solution)/shard_map/ppermute | solution.py:426
  61.2 5.7 %lists.1 = (s32[896]{0:T(1024)}, s32[8]{0:T(128)}, s32[256]{0:T(256)}) custom-call(s32[4]{0:T(128)} %copy-done.8, s32[512]{0:T(512)} %copy-done.13, s32[512]{0:T(512)} %copy-done.16, s32[512]{0:T(512)} %copy-done.15, s32[512]{0:T(512)} %copy-done.14), custom_call_target="tpu_custom_call" | custom-call | tf_op jit(solution)/shard_map/lists/pallas_call | solution.py:161
  68.8 1.9 copy-done.4
  70.7 1.9 copy-done.6
  73.9 16.7 %early.1 = (f32[16448,128]{1,0:T(8,128)S(1)}, f32[2056,128]{1,0:T(8,128)S(1)}, f32[2056,128]{1,0:T(8,128)S(1)}) custom-call(s32[896]{0:T(1024)S(1)} %copy-done.7, s32[8]{0:T(128)S(1)} %copy-done.10, bf16[192,64,128]{2,1,0:T(8,128)(2,1)S(1)} %copy-done.2, bf16[192,64,128]{2,1,0:T(8,128)(2,1)S(1)} %copy-done.4, bf16[192,64,128]{2,1,0:T(8,128)(2,1)S(1)} %copy-done.6), custom_call_target="tpu_custom_call" | custom-call | flops 2000000000 | bytes 20000000 | tf_op jit(solution)/shard_map/early/pallas_call | solution.py:230
  90.7 8.5 %collective-permute-done.5.blocks = bf16[192,64,128]{2,1,0:T(8,128)(2,1)} collective-permute-done((bf16[192,64,128]{2,1,0:T(8,128)(2,1)}, bf16[192,64,128]{2,1,0:T(8,128)(2,1)}, u32[]{:S(2)}, u32[]{:S(2)}) %collective-permute-start.5) | collective-permute-done | bytes 3145760 | tf_op jit(solution)/shard_map/ppermute | solution.py:428
  99.2 9.3 %late.1 = (f32[4288,128]{1,0:T(8,128)S(1)}, f32[4288,128]{1,0:T(8,128)S(1)}, f32[4288,128]{1,0:T(8,128)S(1)}, f32[4288,128]{1,0:T(8,128)S(1)}) custom-call(s32[896]{0:T(1024)S(1)} %copy-done.7, s32[8]{0:T(128)S(1)} %copy-done.10, s32[256]{0:T(256)S(1)} %copy-done.12, bf16[192,64,128]{2,1,0:T(8,128)(2,1)} %collective-permute-done.5.blocks, ...), custom_call_target="tpu_custom_call" | custom-call | flops 1000000000 | bytes 20000000 | tf_op jit(solution)/shard_map/late/pallas_call | solution.py:294
  109.1 3.4 %collective-permute-start.7 = (f32[4288,128]{1,0:T(8,128)S(1)}, f32[4288,128]{1,0:T(8,128)S(1)}, u32[]{:S(2)}, u32[]{:S(2)}) collective-permute-start(f32[4288,128]{1,0:T(8,128)S(1)} %get-tuple-element.52), channel_id=1, source_target_pairs={{0,4},{1,17},{2,6},{3,19},{4,0},{5,21},{6,2},{7,23},{8,12},{9,25},... | collective-permute-start | bytes 6586376 | tf_op jit(solution)/shard_map/ppermute | solution.py:431
  112.6 23.6 %collective-permute-done.6.refs_1_ = f32[4288,128]{1,0:T(8,128)S(1)} collective-permute-done((f32[4288,128]{1,0:T(8,128)S(1)}, f32[4288,128]{1,0:T(8,128)S(1)}, u32[]{:S(2)}, u32[]{:S(2)}) %collective-permute-start.6) | collective-permute-done | bytes 2195488 | tf_op jit(solution)/shard_map/ppermute | solution.py:431
  136.2 24.7 %collective-permute-done.7.refs_2_ = f32[4288,128]{1,0:T(8,128)S(1)} collective-permute-done((f32[4288,128]{1,0:T(8,128)S(1)}, f32[4288,128]{1,0:T(8,128)S(1)}, u32[]{:S(2)}, u32[]{:S(2)}) %collective-permute-start.7) | collective-permute-done | bytes 2195488 | tf_op jit(solution)/shard_map/ppermute | solution.py:431
  161.1 3.5 %collective-permute-start.9 = (f32[2144,128]{1,0:T(8,128)S(1)}, f32[2144,128]{1,0:T(8,128)S(1)}, u32[]{:S(2)}, u32[]{:S(2)}) collective-permute-start(f32[2144,128]{1,0:T(8,128)S(1)} %other_total.1), channel_id=1, source_target_pairs={{0,1},{1,0},{2,3},{3,2},{4,5},{5,4},{6,7},{7,6},{8,9},{9,8},{10,11... | collective-permute-start | bytes 3293192 | tf_op jit(solution)/shard_map/ppermute | solution.py:432
  164.6 2.4 %collective-permute-done.9.refs_4_ = f32[2144,128]{1,0:T(8,128)S(1)} collective-permute-done((f32[2144,128]{1,0:T(8,128)S(1)}, f32[2144,128]{1,0:T(8,128)S(1)}, u32[]{:S(2)}, u32[]{:S(2)}) %collective-permute-start.9) | collective-permute-done | bytes 1097760 | tf_op jit(solution)/shard_map/ppermute | solution.py:432
  168.0 4.0 %collective-permute-start.10 = (f32[536,128]{1,0:T(8,128)S(1)}, f32[536,128]{1,0:T(8,128)S(1)}, u32[]{:S(2)}, u32[]{:S(2)}) collective-permute-start(f32[536,128]{1,0:T(8,128)S(1)} %get-tuple-element.55), channel_id=1, source_target_pairs={{0,32},{32,64},{64,96},{96,0},{1,33},{33,65},{65,97},{97,1},{2,34}... | collective-permute-start | bytes 823304 | tf_op jit(solution)/shard_map/ppermute | solution.py:436
  172.0 2.9 %collective-permute-start.11 = (f32[536,128]{1,0:T(8,128)S(1)}, f32[536,128]{1,0:T(8,128)S(1)}, u32[]{:S(2)}, u32[]{:S(2)}) collective-permute-start(f32[536,128]{1,0:T(8,128)S(1)} %get-tuple-element.56), channel_id=1, source_target_pairs={{0,64},{32,96},{64,0},{96,32},{1,65},{33,97},{65,1},{97,33},{2,66}... | collective-permute-start | bytes 823304 | tf_op jit(solution)/shard_map/ppermute | solution.py:436
  174.8 5.5 %collective-permute-done.10 = f32[536,128]{1,0:T(8,128)S(1)} collective-permute-done((f32[536,128]{1,0:T(8,128)S(1)}, f32[536,128]{1,0:T(8,128)S(1)}, u32[]{:S(2)}, u32[]{:S(2)}) %collective-permute-start.10) | collective-permute-done | bytes 274464 | tf_op jit(solution)/shard_map/ppermute | solution.py:436
  180.3 6.7 %collective-permute-done.11 = f32[536,128]{1,0:T(8,128)S(1)} collective-permute-done((f32[536,128]{1,0:T(8,128)S(1)}, f32[536,128]{1,0:T(8,128)S(1)}, u32[]{:S(2)}, u32[]{:S(2)}) %collective-permute-start.11) | collective-permute-done | bytes 274464 | tf_op jit(solution)/shard_map/ppermute | solution.py:436
  187.1 2.7 %collective-permute-start.15 = (f32[536,128]{1,0:T(8,128)S(1)}, f32[536,128]{1,0:T(8,128)S(1)}, u32[]{:S(2)}, u32[]{:S(2)}) collective-permute-start(f32[536,128]{1,0:T(8,128)S(1)} %add_add_fusion.refs_0_), channel_id=1, source_target_pairs={{0,96},{32,0},{64,32},{96,64},{1,97},{33,1},{65,33},{97,65},{2,98}... | collective-permute-start | bytes 823304 | tf_op jit(solution)/shard_map/ppermute | solution.py:437
  190.4 10.5 %collective-permute-done.15.refs_3_ = f32[536,128]{1,0:T(8,128)S(1)} collective-permute-done((f32[536,128]{1,0:T(8,128)S(1)}, f32[536,128]{1,0:T(8,128)S(1)}, u32[]{:S(2)}, u32[]{:S(2)}) %collective-permute-start.15) | collective-permute-done | bytes 274464 | tf_op jit(solution)/shard_map/ppermute | solution.py:437
  201.0 4.3 %collective-permute-done.13.refs_1_ = f32[536,128]{1,0:T(8,128)S(1)} collective-permute-done((f32[536,128]{1,0:T(8,128)S(1)}, f32[536,128]{1,0:T(8,128)S(1)}, u32[]{:S(2)}, u32[]{:S(2)}) %collective-permute-start.13) | collective-permute-done | bytes 274464 | tf_op jit(solution)/shard_map/ppermute | solution.py:437
  205.2 3.5 %finish.1 = (f32[32,128]{1,0:T(8,128)}, f32[32,128,128]{2,1,0:T(8,128)}) custom-call(s32[4]{0:T(128)S(1)} %copy-done.9, f32[536,128]{1,0:T(8,128)S(1)} %add_add_fusion.refs_0_, f32[536,128]{1,0:T(8,128)S(1)} %collective-permute-done.13.refs_1_, f32[536,128]{1,0:T(8,128)S(1)} %collective-permute-done.14.refs_2_, f32[536,128]{1,0:T(8,128)S(1)} %collective-permute-done.15.refs_3_), custom_call_target="tpu_custom_call" | custom-call | tf_op jit(solution)/shard_map/finish/pallas_call | solution.py:406
  (54 shorter events, 15.3 us)
Async XLA Ops:
  2.1 16.1 %copy-start.13 = (s32[512]{0:T(512)}, s32[512]{0:T(512)S(1)}, u32[]{:S(2)}) copy-start(s32[512]{0:T(512)S(1)} %pad_add_fusion.refs_0_) | copy-start | bytes 6148
  2.1 17.8 %collective-permute-start.2 = (s32[512]{0:T(512)S(1)}, s32[512]{0:T(512)S(1)}, u32[]{:S(2)}, u32[]{:S(2)}) collective-permute-start(s32[512]{0:T(512)S(1)} %pad_add_fusion.refs_0_), channel_id=1, source_target_pairs={{0,16},{1,5},{2,18},{3,7},{4,20},{5,1},{6,22},{7,3},{8,24},{9,13},... | collective-permute-start | bytes 6152 | tf_op jit(solution)/shard_map/ppermute | solution.py:423
  5.8 14.1 %collective-permute-start.1 = (s32[512]{0:T(512)S(1)}, s32[512]{0:T(512)S(1)}, u32[]{:S(2)}, u32[]{:S(2)}) collective-permute-start(s32[512]{0:T(512)S(1)} %pad_add_fusion.refs_0_), channel_id=1, source_target_pairs={{0,24},{1,7},{2,26},{3,1},{4,28},{5,3},{6,30},{7,5},{8,0},{9,15},{... | collective-permute-start | bytes 6152 | tf_op jit(solution)/shard_map/ppermute | solution.py:423
  6.6 13.3 %collective-permute-start = (s32[512]{0:T(512)S(1)}, s32[512]{0:T(512)S(1)}, u32[]{:S(2)}, u32[]{:S(2)}) collective-permute-start(s32[512]{0:T(512)S(1)} %pad_add_fusion.refs_0_), channel_id=1, source_target_pairs={{0,8},{1,3},{2,10},{3,5},{4,12},{5,7},{6,14},{7,1},{8,16},{9,11},{... | collective-permute-start | bytes 6152 | tf_op jit(solution)/shard_map/ppermute | solution.py:423
  7.4 10.8 %copy-start.8 = (s32[4]{0:T(128)}, s32[4]{0:T(128)S(1)}, u32[]{:S(2)}) copy-start(s32[4]{0:T(128)S(1)} %pad_add_fusion.1.pos) | copy-start | bytes 52
  7.4 2.8 %copy-start = (bf16[1,384,64,128]{3,2,1,0:T(8,128)(2,1)S(1)}, bf16[1,384,64,128]{3,2,1,0:T(8,128)(2,1)}, u32[]{:S(2)}) copy-start(bf16[1,384,64,128]{3,2,1,0:T(8,128)(2,1)} %param.3) | copy-start | bytes 18874372
  19.9 41.3 %copy-start.14 = (s32[512]{0:T(512)}, s32[512]{0:T(512)S(1)}, u32[]{:S(2)}) copy-start(s32[512]{0:T(512)S(1)} %collective-permute-done.2.refs_3_) | copy-start | bytes 6148
  19.9 41.3 %copy-start.15 = (s32[512]{0:T(512)}, s32[512]{0:T(512)S(1)}, u32[]{:S(2)}) copy-start(s32[512]{0:T(512)S(1)} %collective-permute-done.1.refs_2_) | copy-start | bytes 6148
  19.9 41.3 %copy-start.16 = (s32[512]{0:T(512)}, s32[512]{0:T(512)S(1)}, u32[]{:S(2)}) copy-start(s32[512]{0:T(512)S(1)} %collective-permute-done.refs_1_) | copy-start | bytes 6148
  19.9 37.7 %collective-permute-start.3 = (bf16[192,64,128]{2,1,0:T(8,128)(2,1)S(1)}, bf16[192,64,128]{2,1,0:T(8,128)(2,1)S(1)}, u32[]{:S(2)}, u32[]{:S(2)}) collective-permute-start(bf16[192,64,128]{2,1,0:T(8,128)(2,1)S(1)} %get-tuple-element.41), channel_id=1, source_target_pairs={{0,8},{1,3},{2,10},{3,5},{4,12},{5,7},{6,14},{7,1},{8,16},{9,11},{... | collective-permute-start | bytes 9437192 | tf_op jit(solution)/shard_map/ppermute | solution.py:426
  20.4 38.9 %collective-permute-start.4 = (bf16[192,64,128]{2,1,0:T(8,128)(2,1)S(1)}, bf16[192,64,128]{2,1,0:T(8,128)(2,1)S(1)}, u32[]{:S(2)}, u32[]{:S(2)}) collective-permute-start(bf16[192,64,128]{2,1,0:T(8,128)(2,1)S(1)} %get-tuple-element.42), channel_id=1, source_target_pairs={{0,24},{1,7},{2,26},{3,1},{4,28},{5,3},{6,30},{7,5},{8,0},{9,15},{... | collective-permute-start | bytes 9437192 | tf_op jit(solution)/shard_map/ppermute | solution.py:426
  60.9 38.2 %collective-permute-start.5 = (bf16[192,64,128]{2,1,0:T(8,128)(2,1)}, bf16[192,64,128]{2,1,0:T(8,128)(2,1)}, u32[]{:S(2)}, u32[]{:S(2)}) collective-permute-start(bf16[192,64,128]{2,1,0:T(8,128)(2,1)} %get-tuple-element.43), channel_id=1, source_target_pairs={{0,16},{1,5},{2,18},{3,7},{4,20},{5,1},{6,22},{7,3},{8,24},{9,13},... | collective-permute-start | bytes 9437192 | tf_op jit(solution)/shard_map/ppermute | solution.py:428
  73.9 25.2 %copy-start.12 = (s32[256]{0:T(256)S(1)}, s32[256]{0:T(256)}, u32[]{:S(2)}) copy-start(s32[256]{0:T(256)} %get-tuple-element.38.tallies) | copy-start | bytes 3076
  108.5 27.7 %collective-permute-start.6 = (f32[4288,128]{1,0:T(8,128)S(1)}, f32[4288,128]{1,0:T(8,128)S(1)}, u32[]{:S(2)}, u32[]{:S(2)}) collective-permute-start(f32[4288,128]{1,0:T(8,128)S(1)} %get-tuple-element.51), channel_id=1, source_target_pairs={{0,2},{1,9},{2,4},{3,11},{4,6},{5,13},{6,0},{7,15},{8,10},{9,17},{... | collective-permute-start | bytes 6586376 | tf_op jit(solution)/shard_map/ppermute | solution.py:431
  109.1 51.7 %collective-permute-start.7 = (f32[4288,128]{1,0:T(8,128)S(1)}, f32[4288,128]{1,0:T(8,128)S(1)}, u32[]{:S(2)}, u32[]{:S(2)}) collective-permute-start(f32[4288,128]{1,0:T(8,128)S(1)} %get-tuple-element.52), channel_id=1, source_target_pairs={{0,4},{1,17},{2,6},{3,19},{4,0},{5,21},{6,2},{7,23},{8,12},{9,25},... | collective-permute-start | bytes 6586376 | tf_op jit(solution)/shard_map/ppermute | solution.py:431
  112.6 48.3 %collective-permute-start.8 = (f32[4288,128]{1,0:T(8,128)S(1)}, f32[4288,128]{1,0:T(8,128)S(1)}, u32[]{:S(2)}, u32[]{:S(2)}) collective-permute-start(f32[4288,128]{1,0:T(8,128)S(1)} %get-tuple-element.53), channel_id=1, source_target_pairs={{0,6},{1,25},{2,0},{3,27},{4,2},{5,29},{6,4},{7,31},{8,14},{9,1},{... | collective-permute-start | bytes 6586376 | tf_op jit(solution)/shard_map/ppermute | solution.py:431
  160.9 6.1 %copy-start.9 = (s32[4]{0:T(128)S(1)}, s32[4]{0:T(128)}, u32[]{:S(2)}) copy-start(s32[4]{0:T(128)} %copy-done.8) | copy-start | bytes 52
  161.1 5.9 %collective-permute-start.9 = (f32[2144,128]{1,0:T(8,128)S(1)}, f32[2144,128]{1,0:T(8,128)S(1)}, u32[]{:S(2)}, u32[]{:S(2)}) collective-permute-start(f32[2144,128]{1,0:T(8,128)S(1)} %other_total.1), channel_id=1, source_target_pairs={{0,1},{1,0},{2,3},{3,2},{4,5},{5,4},{6,7},{7,6},{8,9},{9,8},{10,11... | collective-permute-start | bytes 3293192 | tf_op jit(solution)/shard_map/ppermute | solution.py:432
  168.0 12.3 %collective-permute-start.10 = (f32[536,128]{1,0:T(8,128)S(1)}, f32[536,128]{1,0:T(8,128)S(1)}, u32[]{:S(2)}, u32[]{:S(2)}) collective-permute-start(f32[536,128]{1,0:T(8,128)S(1)} %get-tuple-element.55), channel_id=1, source_target_pairs={{0,32},{32,64},{64,96},{96,0},{1,33},{33,65},{65,97},{97,1},{2,34}... | collective-permute-start | bytes 823304 | tf_op jit(solution)/shard_map/ppermute | solution.py:436
  172.0 15.1 %collective-permute-start.11 = (f32[536,128]{1,0:T(8,128)S(1)}, f32[536,128]{1,0:T(8,128)S(1)}, u32[]{:S(2)}, u32[]{:S(2)}) collective-permute-start(f32[536,128]{1,0:T(8,128)S(1)} %get-tuple-element.56), channel_id=1, source_target_pairs={{0,64},{32,96},{64,0},{96,32},{1,65},{33,97},{65,1},{97,33},{2,66}... | collective-permute-start | bytes 823304 | tf_op jit(solution)/shard_map/ppermute | solution.py:436
  174.8 12.2 %collective-permute-start.12 = (f32[536,128]{1,0:T(8,128)S(1)}, f32[536,128]{1,0:T(8,128)S(1)}, u32[]{:S(2)}, u32[]{:S(2)}) collective-permute-start(f32[536,128]{1,0:T(8,128)S(1)} %get-tuple-element.57), channel_id=1, source_target_pairs={{0,96},{32,0},{64,32},{96,64},{1,97},{33,1},{65,33},{97,65},{2,98}... | collective-permute-start | bytes 823304 | tf_op jit(solution)/shard_map/ppermute | solution.py:436
  187.1 13.8 %collective-permute-start.15 = (f32[536,128]{1,0:T(8,128)S(1)}, f32[536,128]{1,0:T(8,128)S(1)}, u32[]{:S(2)}, u32[]{:S(2)}) collective-permute-start(f32[536,128]{1,0:T(8,128)S(1)} %add_add_fusion.refs_0_), channel_id=1, source_target_pairs={{0,96},{32,0},{64,32},{96,64},{1,97},{33,1},{65,33},{97,65},{2,98}... | collective-permute-start | bytes 823304 | tf_op jit(solution)/shard_map/ppermute | solution.py:437
  189.8 11.2 %collective-permute-start.14 = (f32[536,128]{1,0:T(8,128)S(1)}, f32[536,128]{1,0:T(8,128)S(1)}, u32[]{:S(2)}, u32[]{:S(2)}) collective-permute-start(f32[536,128]{1,0:T(8,128)S(1)} %add_add_fusion.refs_0_), channel_id=1, source_target_pairs={{0,64},{32,96},{64,0},{96,32},{1,65},{33,97},{65,1},{97,33},{2,66}... | collective-permute-start | bytes 823304 | tf_op jit(solution)/shard_map/ppermute | solution.py:437
  189.9 15.4 %collective-permute-start.13 = (f32[536,128]{1,0:T(8,128)S(1)}, f32[536,128]{1,0:T(8,128)S(1)}, u32[]{:S(2)}, u32[]{:S(2)}) collective-permute-start(f32[536,128]{1,0:T(8,128)S(1)} %add_add_fusion.refs_0_), channel_id=1, source_target_pairs={{0,32},{32,64},{64,96},{96,0},{1,33},{33,65},{65,97},{97,1},{2,34}... | collective-permute-start | bytes 823304 | tf_op jit(solution)/shard_map/ppermute | solution.py:437
  (9 other events, 12.7 us)

commit v3 on v2

v3 whole, which is shorter than its diff:
```python
import jax
import jax.numpy as jnp
from jax import lax
from jax.experimental import pallas as pl
from jax.experimental.pallas import tpu as pltpu
from jax.sharding import PartitionSpec as P

CELLS = 1024
NX = NY = NZ = 4
NC = 2
OWNERS = NX * NY * NC
CELL_DEV = CELLS // OWNERS
BLK = 384
ROWS = 64
D = 128
RUN = 24
SLOTS = NC * RUN
SHIFTS = (0, 1, 3, 2)
GROUPS = len(SHIFTS)
CHIP_CELLS = NC * CELL_DEV
LIST = 4 * GROUPS * SLOTS + 128
PAIR = 8
F32 = jnp.float32
I32 = jnp.int32
META = 512
UNITS = (((2, 0), (2, 1)), ((0, 0), (0, 1)), ((1, 1), (3, 0)), ((1, 0), (3, 1)))
PACKED = CELL_DEV * ROWS
PIECE = PACKED + 3 * CELL_DEV
QCELL = CELL_DEV // NZ
QPACKED = QCELL * ROWS
QPIECE = QPACKED + 3 * QCELL
VMEM_LIMIT = 16 * 1024 * 1024
LARGE_VMEM = 56 * 1024 * 1024
SMALL_VMEM = 6 * 1024 * 1024

SMEM_SPEC = pl.BlockSpec(memory_space=pltpu.SMEM)
VMEM_SPEC = pl.BlockSpec(memory_space=pltpu.VMEM)
HBM_SPEC = pl.BlockSpec(memory_space=pltpu.HBM)


def at(x, y, c):
    return (x * NY + y) * NC + c


def cell_perm(even, odd, dc=0):
    steps = (even, odd)
    return [
        (at(x, y, c), at((x + steps[c][0]) % NX, (y + steps[c][1]) % NY, c ^ dc))
        for x in range(NX)
        for y in range(NY)
        for c in range(NC)
    ]


def along(d):
    return cell_perm((d, 0), (0, d))


def across(d):
    return cell_perm((0, d), (d, 0))


SWAP = cell_perm((0, 0), (0, 0), 1)


def dp_perm(dz):
    return [(z, (z + dz) % NZ) for z in range(NZ)]


def place():
    me = lax.axis_index("cell")
    x, y, c = me // (NY * NC), (me // NC) % NY, me % NC
    first, second = jnp.where(c == 0, x, y), jnp.where(c == 0, y, x)
    return jnp.stack([first, second, c, lax.axis_index("dp")]).astype(I32)


def owner(c, first, second, oc):
    return jnp.where(c == 0, at(first, second, oc), at(second, first, oc))


def unit_owner(pos, d, rel, side):
    return owner(pos[2], lax.rem(pos[0] + d, 4), lax.rem(pos[1] + rel, 4), lax.rem(pos[2] + side, 2))


def gather_body(flows, pos, counts, vectors, *refs):
    outs = refs[: len(flows)]
    offsets, sems = refs[len(flows) :]
    total = jnp.int32(0)
    for o in range(OWNERS):
        offsets[o] = total
        total = total + counts[o]
    copies = []
    for out, (d, units) in zip(outs, flows):
        for i, (rel, side) in enumerate(units):
            o = unit_owner(pos, d, rel, side)
            start = jnp.minimum(offsets[o], BLK - RUN)
            copies.append(
                pltpu.make_async_copy(vectors.at[pl.ds(start, RUN)], out.at[pl.ds(i * RUN, RUN)], sems.at[len(copies)])
            )
            copies[-1].start()
    for copy in copies:
        copy.wait()


def gather_runs(flows, pos, counts, vectors, name, vmem):
    def body(*refs):
        gather_body(flows, *refs)

    return pl.pallas_call(
        body,
        out_shape=[jax.ShapeDtypeStruct((SLOTS, ROWS, D), vectors.dtype)] * len(flows),
        in_specs=[SMEM_SPEC, SMEM_SPEC, HBM_SPEC],
        out_specs=[VMEM_SPEC] * len(flows),
        scratch_shapes=[pltpu.SMEM((OWNERS,), I32), pltpu.SemaphoreType.DMA((NC * len(flows),))],
        compiler_params=pltpu.CompilerParams(vmem_limit_bytes=vmem),
        name=name,
    )(pos, counts, vectors)


def lists_body(pos, *refs):
    metas = refs[:GROUPS]
    lists, sizes, tallies, offsets = refs[GROUPS:]

    def clear(i, _):
        for u in range(8):
            tallies[i * 8 + u] = jnp.int32(0)
        return 0

    lax.fori_loop(0, 4 * CHIP_CELLS // 8, clear, 0)
    for g in range(GROUPS):
        total = jnp.int32(0)
        for o in range(OWNERS):
            offsets[g * OWNERS + o] = total
            total = total + metas[g][BLK + o]
    begin = jnp.int32(0)
    for group, units in enumerate(UNITS):
        for g in range(GROUPS):
            filled = begin
            for i, (rel, side) in enumerate(units):
                o = unit_owner(pos, 0, rel, side)
                n = metas[g][BLK + o]
                start = offsets[g * OWNERS + o]
                slot = i * RUN + start - jnp.minimum(start, BLK - RUN)
                base = (slot << 17) + i * ((PIECE // 8 << 7) + CELL_DEV)
                tally = group * CHIP_CELLS + i * CELL_DEV

                def add(j, f, g=g, start=start, base=base, tally=tally):
                    cell = metas[g][start + j]
                    lists[f + j] = base + (j << 17) + cell * ((ROWS // 8 << 7) + 1)
                    tallies[tally + cell] = tallies[tally + cell] + ROWS
                    return f

                lax.fori_loop(0, n, add, filled)
                filled = filled + n
            for j in range(PAIR):
                lists[filled + j] = jnp.int32((PACKED // 8 << 7) + CHIP_CELLS)
            segment = group * GROUPS + g
            sizes[2 * segment] = begin
            sizes[2 * segment + 1] = (filled - begin + PAIR - 1) // PAIR
            begin = begin + sizes[2 * segment + 1] * PAIR


def make_lists(pos, metas):
    return pl.pallas_call(
        lists_body,
        out_shape=[
            jax.ShapeDtypeStruct((LIST,), I32),
            jax.ShapeDtypeStruct((8 * GROUPS,), I32),
            jax.ShapeDtypeStruct((4 * CHIP_CELLS,), I32),
        ],
        in_specs=[SMEM_SPEC] * (1 + GROUPS),
        out_specs=[SMEM_SPEC] * 3,
        scratch_shapes=[pltpu.SMEM((GROUPS * OWNERS,), I32)],
        compiler_params=pltpu.CompilerParams(vmem_limit_bytes=SMALL_VMEM),
        name="lists",
    )(pos, *metas)


def add_blocks(segment, lists, sizes, buf, acc, acc_s, acc_q):
    begin, steps = sizes[2 * segment], sizes[2 * segment + 1]
    row = lax.broadcasted_iota(I32, (ROWS, D), 0)
    lane = lax.broadcasted_iota(I32, (ROWS, D), 1)
    upper = lane >= row
    contract = (((0,), (0,)), ((), ()))

    def step(i, _):
        done = []
        for u in range(PAIR):
            entry = lists[begin + i * PAIR + u]
            block = buf[entry >> 17]
            turned = jnp.concatenate([block[:, ROWS:], block[:, :ROWS]], axis=1)
            top = lax.dot_general(block[:, :ROWS], block, contract, preferred_element_type=F32)
            low = lax.dot_general(block[:, ROWS:], turned, contract, preferred_element_type=F32)
            wide = block.astype(F32)
            done.append(
                (
                    pl.multiple_of(((entry >> 7) & 1023) * 8, 8),
                    pl.multiple_of((entry & 127) * 8, 8),
                    jnp.where(upper, top, low),
                    jnp.sum(wide.reshape(8, 8, D), axis=0),
                    jnp.sum((wide * wide).reshape(8, 8, D), axis=0),
                )
            )
        for at_row, at_sum, gram, total, square in done:
            here, near = pl.ds(at_row, ROWS), pl.ds(at_sum, 8)
            acc[here, :] = acc[here, :] + gram
            acc_s[near, :] = acc_s[near, :] + total
            acc_q[near, :] = acc_q[near, :] + square
        return 0

    lax.fori_loop(0, steps, step, 0)


def gram_body(group, started, lists, sizes, tallies, *refs):
    blocks = refs[:GROUPS]
    starts = refs[GROUPS : GROUPS + started]
    outs = refs[GROUPS + started : GROUPS + started + 2]
    acc, acc_s, acc_q = refs[GROUPS + started + 2 :]

    def clear(i, _):
        rows = pl.ds(pl.multiple_of(i * ROWS, ROWS), ROWS)
        for u in range(2):
            value = starts[u][rows, :] if started else jnp.zeros((ROWS, D), F32)
            acc[pl.ds(pl.multiple_of(u * PIECE + i * ROWS, 8), ROWS), :] = value
        return 0

    lax.fori_loop(0, CELL_DEV, clear, 0)

    def clear_sums(i, _):
        acc_s[pl.ds(pl.multiple_of(i * 8, 8), 8), :] = jnp.zeros((8, D), F32)
        acc_q[pl.ds(pl.multiple_of(i * 8, 8), 8), :] = jnp.zeros((8, D), F32)
        return 0

    lax.fori_loop(0, CHIP_CELLS, clear_sums, 0)
    for g in range(GROUPS):
        add_blocks(group * GROUPS + g, lists, sizes, blocks[g], acc, acc_s, acc_q)

    def copy_out(i, _):
        rows = pl.ds(pl.multiple_of(i * ROWS, ROWS), ROWS)
        for u in range(2):
            outs[u][rows, :] = acc[pl.ds(pl.multiple_of(u * PIECE + i * ROWS, 8), ROWS), :]
        return 0

    lax.fori_loop(0, CELL_DEV, copy_out, 0)
    for u in range(2):
        for k, source in enumerate((acc_s, acc_q)):
            total = source[pl.ds(u * CELL_DEV * 8, CELL_DEV, stride=8), :]
            for j in range(1, 8):
                total = total + source[pl.ds(u * CELL_DEV * 8 + j, CELL_DEV, stride=8), :]
            rows = pl.ds(PACKED + k * CELL_DEV, CELL_DEV)
            outs[u][rows, :] = total + starts[u][rows, :] if started else total
        for j in range(CELL_DEV):
            count = jnp.full((1, D), tallies[group * CHIP_CELLS + u * CELL_DEV + j].astype(F32), F32)
            rows = pl.ds(PACKED + 2 * CELL_DEV + j, 1)
            outs[u][rows, :] = count + starts[u][rows, :] if started else count


def gram(group, lists, sizes, tallies, blocks, starts=()):
    def body(*refs):
        gram_body(group, len(starts), *refs)

    half = jax.ShapeDtypeStruct((PIECE, D), F32)
    return pl.pallas_call(
        body,
        out_shape=[half, half],
        in_specs=[SMEM_SPEC] * 3 + [VMEM_SPEC] * (GROUPS + len(starts)),
        out_specs=[VMEM_SPEC] * 2,
        scratch_shapes=[pltpu.VMEM((NC * PIECE, D), F32)] + [pltpu.VMEM(((CHIP_CELLS + 1) * 8, D), F32)] * 2,
        compiler_params=pltpu.CompilerParams(vmem_limit_bytes=SMALL_VMEM),
        cost_estimate=pl.CostEstimate(flops=10**9, bytes_accessed=10**7, transcendentals=0),
        name=f"gram{group}",
    )(lists, sizes, tallies, *blocks, *starts)


def total_body(*refs):
    def step(i, _):
        rows = pl.ds(pl.multiple_of(i * 32, 32), 32)
        value = refs[0][rows, :]
        for part in refs[1:-1]:
            value = value + part[rows, :]
        refs[-1][rows, :] = value
        return 0

    lax.fori_loop(0, PIECE // 32, step, 0)


def other_total(parts):
    return pl.pallas_call(
        total_body,
        out_shape=jax.ShapeDtypeStruct((PIECE, D), F32),
        in_specs=[VMEM_SPEC] * len(parts),
        out_specs=VMEM_SPEC,
        compiler_params=pltpu.CompilerParams(vmem_limit_bytes=SMALL_VMEM),
        name="other_total",
    )(*parts)


def join_body(pos, *refs):
    outs = refs[-NZ:]
    parts = refs[:-NZ]
    z = pos[3]

    def total(rows):
        value = parts[0][rows, :]
        for part in parts[1:]:
            value = value + part[rows, :]
        return value

    for dz in range(NZ):
        q = lax.rem(z + dz, NZ)

        def step(i, _, dz=dz, q=q):
            outs[dz][pl.ds(pl.multiple_of(i * ROWS, ROWS), ROWS), :] = total(
                pl.ds(pl.multiple_of(q * QPACKED + i * ROWS, ROWS), ROWS)
            )
            return 0

        lax.fori_loop(0, QCELL, step, 0)
        for k in range(3):
            outs[dz][pl.ds(QPACKED + k * QCELL, QCELL), :] = total(
                pl.ds(pl.multiple_of(PACKED + k * CELL_DEV + q * QCELL, QCELL), QCELL)
            )


def join(pos, parts):
    return pl.pallas_call(
        join_body,
        out_shape=[jax.ShapeDtypeStruct((QPIECE, D), F32)] * NZ,
        in_specs=[SMEM_SPEC] + [VMEM_SPEC] * len(parts),
        out_specs=[VMEM_SPEC] * NZ,
        compiler_params=pltpu.CompilerParams(vmem_limit_bytes=SMALL_VMEM),
        name="join",
    )(pos, *parts)


def finish_body(pos, *refs):
    parts = refs[:NZ]
    mean_out, cov_out = refs[NZ:]
    z = pos[3]
    row = lax.broadcasted_iota(I32, (ROWS, D), 0)
    lane = lax.broadcasted_iota(I32, (ROWS, D), 1)
    for dz in range(NZ):
        q = lax.rem(z + NZ - dz, NZ)
        part = parts[dz]
        sums = part[pl.ds(QPACKED, QCELL), :]
        counts = part[pl.ds(QPACKED + 2 * QCELL, QCELL), :]
        safe = jnp.maximum(counts, 1.0)
        mean = sums / safe
        inverse = 1.0 / safe
        mean_out[pl.ds(pl.multiple_of(q * QCELL, QCELL), QCELL), :] = mean
        scaled = jnp.transpose(jnp.concatenate([mean * counts] * (D // QCELL), axis=0))
        for j in range(QCELL):
            packed = part[pl.ds(j * ROWS, ROWS), :]
            diagonal = part[pl.ds(QPACKED + QCELL + j, 1), :]
            flipped = jnp.transpose(jnp.concatenate([packed, packed], axis=0))
            rolled = pltpu.roll(packed, ROWS, 1)
            high, low = flipped[:ROWS], flipped[ROWS:]
            top = jnp.where(lane >= row, packed, high)
            corner = jnp.where(lane - ROWS < row, rolled, jnp.where(lane - ROWS == row, diagonal, high))
            bottom = jnp.where(lane < ROWS, low, corner)
            full = jnp.concatenate([top, bottom], axis=0)
            outer = scaled[:, j : j + 1] * mean[j : j + 1, :]
            cov_out[q * QCELL + j] = (full - outer) * inverse[j : j + 1, :]


def finish(pos, parts):
    return pl.pallas_call(
        finish_body,
        out_shape=[
            jax.ShapeDtypeStruct((CELL_DEV, D), F32),
            jax.ShapeDtypeStruct((CELL_DEV, D, D), F32),
        ],
        in_specs=[SMEM_SPEC] + [VMEM_SPEC] * NZ,
        out_specs=[VMEM_SPEC, VMEM_SPEC],
        compiler_params=pltpu.CompilerParams(vmem_limit_bytes=VMEM_LIMIT),
        name="finish",
    )(pos, *parts)


def local(vectors, block_cells, dest_counts):
    pos = place()
    counts = dest_counts[0, 0]
    meta = jnp.concatenate([block_cells[0], counts, jnp.zeros((META - BLK - OWNERS,), I32)])
    metas = [meta] + [lax.ppermute(meta, "cell", along(d)) for d in SHIFTS[1:]]
    lists, sizes, tallies = make_lists(pos, metas)
    sent, got = [], []
    for group, units in enumerate(UNITS):
        turn = pos
        if group == 1:
            turn, *_ = lax.optimization_barrier((pos, *sent[0]))
        elif group > 1:
            turn, *_ = lax.optimization_barrier((pos, sizes, *got[group - 2][1:]))
        runs = gather_runs([(d, units) for d in SHIFTS], turn, counts, vectors[0], f"gather{group}", LARGE_VMEM if group == 0 else SMALL_VMEM)
        if group == 0:
            *_, r0, r1, r2, r3 = lax.optimization_barrier((*metas, *runs))
            runs = [r0, r1, r2, r3]
        sent.append(runs)
        got.append([runs[0]] + [lax.ppermute(run, "cell", along(d)) for d, run in zip(SHIFTS[1:], runs[1:])])

    def step(rel, piece):
        return lax.ppermute(piece, "cell", across(rel))

    fore, back = gram(0, lists, sizes, tallies, got[0])
    fore, back = step(1, fore), step(3, back)
    left, right = gram(2, lists, sizes, tallies, got[2])
    other1, own3 = step(1, left), step(3, right)
    left, right = gram(3, lists, sizes, tallies, got[3], (fore, back))
    own1, other3 = step(1, left), step(3, right)
    own, other = gram(1, lists, sizes, tallies, got[1], (own3, other1))
    swapped = lax.ppermute(other_total([other, other3]), "cell", SWAP)
    quarters = join(pos, [own, own1, swapped])
    mine = quarters[0]
    for dz in range(1, NZ):
        mine = mine + lax.ppermute(quarters[dz], "dp", dp_perm(dz))
    whole = [mine] + [lax.ppermute(mine, "dp", dp_perm(dz)) for dz in range(1, NZ)]
    return tuple(finish(pos, whole))


def solution(mesh):
    in_specs = (P("dp", "cell", None, None), P("dp", "cell"), P("dp", "cell", None))
    out_specs = (P("cell", None), P("cell", None, None))
    return jax.shard_map(local, mesh=mesh, in_specs=in_specs, out_specs=out_specs, check_vma=False)
```

time: 209 us -> 174 us (0.83)
  waiting for transfers between devices: 121 us -> 75.1 us
  starting transfers between devices: 26.1 us -> 43.5 us
  local copies, waits for them, and re-layouts: 15.5 us -> 0.02 us
  Pallas kernels: 43.7 us -> 50.8 us
    ppermute x7 -> x19, waiting for transfers between devices: 94.1 us -> 48 us  [the longest x12 38 us: local(): lax.ppermute(run, 'cell', along(d))]
    ppermute x7 -> x19, starting transfers between devices: 10.6 us -> 26.8 us  [the longest x12 12.8 us: local(): lax.ppermute(run, 'cell', along(d))]
    unnamed x34 -> x8, local copies, waits for them, and re-layouts: 15.5 us -> 0.01 us
    pallas_call x3 -> x8, Pallas kernels: 33.3 us -> 40 us  [the longest x4 28.4 us: gram(): pl.pallas_call(body, out_shape=[half, half], in_specs=[SMEM_SPEC] * 3 + [...]
  transfers between devices with their start and end apart: 16 -> 28, of which waited for: 9 -> 20; matrix products, arithmetic and copies ran while one was open for 0% -> 0% of each run, Pallas kernels for 14% -> 27%
where the time goes in v3:
time: 174 us; the launch traced here: 172 us
  waiting for transfers between devices  75.1 us (43%)
  Pallas kernels  50.8 us (29%)
  starting transfers between devices  43.5 us (25%)
  other arithmetic  2.15 us (1%)
    ppermute x12, waiting for transfers between devices, local(): lax.ppermute(run, 'cell', along(d))  38 us
    pallas_call x4, Pallas kernels, gram(): pl.pallas_call(body, out_shape=[half, half], in_specs=[SMEM_SPEC] * 3 + [...  28.4 us
    ppermute x3, waiting for transfers between devices, local(): lax.ppermute(mine, 'dp', dp_perm(dz))  15.1 us
    ppermute x12, starting transfers between devices, local(): lax.ppermute(run, 'cell', along(d))  12.8 us
    ppermute x3, waiting for transfers between devices, local(): mine = mine + lax.ppermute(quarters[dz], 'dp', dp_perm(dz))  11.9 us
    pallas_call x4, Pallas kernels, gather_runs(): pl.pallas_call(body, out_shape=[jax.ShapeDtypeStruct((SLOTS, ROWS, D), ve...  11.6 us
    ppermute x6, starting transfers between devices, step(): return lax.ppermute(piece, 'cell', across(rel))  8.45 us
    ppermute x3, starting transfers between devices, local(): mine = mine + lax.ppermute(quarters[dz], 'dp', dp_perm(dz))  8.16 us
  transfers between devices with their start and end apart: 28, of which 20 were waited for; matrix products, arithmetic and copies ran while one was open for 0% of the time, Pallas kernels for 27%

profile of v3, /device:TPU:1, one launch (start us, length us, event | category | flops | bytes accessed | tf_op | source)
XLA Modules:
  0.0 172.3 jit_solution(16953817094762010681)
XLA Ops:
  2.1 3.7 %collective-permute-start.2 = (s32[512]{0:T(512)S(1)}, s32[512]{0:T(512)S(1)}, u32[]{:S(2)}, u32[]{:S(2)}) collective-permute-start(s32[512]{0:T(512)S(1)} %pad_add_fusion.refs_0_), channel_id=1, source_target_pairs={{0,16},{1,5},{2,18},{3,7},{4,20},{5,1},{6,22},{7,3},{8,24},{9,13},... | collective-permute-start | bytes 6152 | tf_op jit(solution)/shard_map/ppermute | solution.py:384
  7.9 4.8 %gather0.1 = (bf16[48,64,128]{2,1,0:T(8,128)(2,1)}, bf16[48,64,128]{2,1,0:T(8,128)(2,1)}, bf16[48,64,128]{2,1,0:T(8,128)(2,1)}, bf16[48,64,128]{2,1,0:T(8,128)(2,1)}) custom-call(s32[4]{0:T(128)} %pad_add_fusion.1.pos.refs_0_, s32[32]{0:T(128)} %bitcast.11, bf16[384,64,128]{2,1,0:T(8,128)(2,1)} %bitcast.6), custom_call_target="tpu_custom_call" | custom-call | tf_op jit(solution)/shard_map/gather0/pallas_call | solution.py:109
  21.0 4.3 %collective-permute-done.6.refs_4_ = bf16[48,64,128]{2,1,0:T(8,128)(2,1)S(1)} collective-permute-done((bf16[48,64,128]{2,1,0:T(8,128)(2,1)}, bf16[48,64,128]{2,1,0:T(8,128)(2,1)S(1)}, u32[]{:S(2)}, u32[]{:S(2)}) %collective-permute-start.6) | collective-permute-done | bytes 786464 | tf_op jit(solution)/shard_map/ppermute | solution.py:398
  25.4 6.0 %lists.1 = (s32[896]{0:T(1024)S(1)}, s32[32]{0:T(128)S(1)}, s32[256]{0:T(256)S(1)}) custom-call(s32[4]{0:T(128)S(1)} %copy-done.1, s32[512]{0:T(512)S(1)} %pad_add_fusion.refs_0_, s32[512]{0:T(512)S(1)} %collective-permute-done.refs_1_, s32[512]{0:T(512)S(1)} %collective-permute-done.1.refs_2_, s32[512]{0:T(512)S(1)} %collective-permute-done.2.refs_3_), custom_call_target="tpu_custom_call" | custom-call | tf_op jit(solution)/shard_map/lists/pallas_call | solution.py:164
  39.3 2.9 %collective-permute-done.3.refs_4_ = bf16[48,64,128]{2,1,0:T(8,128)(2,1)S(1)} collective-permute-done((bf16[48,64,128]{2,1,0:T(8,128)(2,1)S(1)}, bf16[48,64,128]{2,1,0:T(8,128)(2,1)S(1)}, u32[]{:S(2)}, u32[]{:S(2)}) %collective-permute-start.3) | collective-permute-done | bytes 786464 | tf_op jit(solution)/shard_map/ppermute | solution.py:398
  42.2 6.5 %gram0.1 = (f32[2144,128]{1,0:T(8,128)S(1)}, f32[2144,128]{1,0:T(8,128)S(1)}) custom-call(s32[896]{0:T(1024)S(1)} %get-tuple-element.40.refs_0_, s32[32]{0:T(128)S(1)} %get-tuple-element.41.refs_1_, s32[256]{0:T(256)S(1)} %get-tuple-element.42.refs_2_, bf16[48,64,128]{2,1,0:T(8,128)(2,1)S(1)} %copy-done.3, ...), custom_call_target="tpu_custom_call" | custom-call | flops 1000000000 | bytes 10000000 | tf_op jit(solution)/shard_map/gram0/pallas_call | solution.py:263
  56.0 4.8 %collective-permute-done.9.refs_4_ = bf16[48,64,128]{2,1,0:T(8,128)(2,1)S(1)} collective-permute-done((bf16[48,64,128]{2,1,0:T(8,128)(2,1)S(1)}, bf16[48,64,128]{2,1,0:T(8,128)(2,1)S(1)}, u32[]{:S(2)}, u32[]{:S(2)}) %collective-permute-start.9) | collective-permute-done | bytes 786464 | tf_op jit(solution)/shard_map/ppermute | solution.py:398
  60.8 3.0 %collective-permute-start.15 = (bf16[48,64,128]{2,1,0:T(8,128)(2,1)S(1)}, bf16[48,64,128]{2,1,0:T(8,128)(2,1)S(1)}, u32[]{:S(2)}, u32[]{:S(2)}) collective-permute-start(bf16[48,64,128]{2,1,0:T(8,128)(2,1)S(1)} %get-tuple-element.67), channel_id=1, source_target_pairs={{0,24},{1,7},{2,26},{3,1},{4,28},{5,3},{6,30},{7,5},{8,0},{9,15},{... | collective-permute-start | bytes 2359304 | tf_op jit(solution)/shard_map/ppermute | solution.py:398
  63.8 13.3 %collective-permute-done.11.refs_6_ = bf16[48,64,128]{2,1,0:T(8,128)(2,1)S(1)} collective-permute-done((bf16[48,64,128]{2,1,0:T(8,128)(2,1)S(1)}, bf16[48,64,128]{2,1,0:T(8,128)(2,1)S(1)}, u32[]{:S(2)}, u32[]{:S(2)}) %collective-permute-start.11) | collective-permute-done | bytes 786464 | tf_op jit(solution)/shard_map/ppermute | solution.py:398
  78.1 7.2 %gram2.1 = (f32[2144,128]{1,0:T(8,128)S(1)}, f32[2144,128]{1,0:T(8,128)S(1)}) custom-call(s32[896]{0:T(1024)S(1)} %get-tuple-element.40.refs_0_, s32[32]{0:T(128)S(1)} %get-tuple-element.41.refs_1_, s32[256]{0:T(256)S(1)} %get-tuple-element.42.refs_2_, bf16[48,64,128]{2,1,0:T(8,128)(2,1)S(1)} %get-tuple-element.57.refs_3_, ...), custom_call_target="tpu_custom_call" | custom-call | flops 1000000000 | bytes 10000000 | tf_op jit(solution)/shard_map/gram2/pallas_call | solution.py:263
  90.1 3.8 %collective-permute-done.15.refs_5_ = bf16[48,64,128]{2,1,0:T(8,128)(2,1)S(1)} collective-permute-done((bf16[48,64,128]{2,1,0:T(8,128)(2,1)S(1)}, bf16[48,64,128]{2,1,0:T(8,128)(2,1)S(1)}, u32[]{:S(2)}, u32[]{:S(2)}) %collective-permute-start.15) | collective-permute-done | bytes 786464 | tf_op jit(solution)/shard_map/ppermute | solution.py:398
  97.1 7.5 %gram3.1 = (f32[2144,128]{1,0:T(8,128)S(1)}, f32[2144,128]{1,0:T(8,128)S(1)}) custom-call(s32[896]{0:T(1024)S(1)} %get-tuple-element.40.refs_0_, s32[32]{0:T(128)S(1)} %get-tuple-element.41.refs_1_, s32[256]{0:T(256)S(1)} %get-tuple-element.42.refs_2_, bf16[48,64,128]{2,1,0:T(8,128)(2,1)S(1)} %get-tuple-element.65.refs_3_, ...), custom_call_target="tpu_custom_call" | custom-call | flops 1000000000 | bytes 10000000 | tf_op jit(solution)/shard_map/gram3/pallas_call | solution.py:263
  106.1 3.2 %collective-permute-done.12.refs_7_ = f32[2144,128]{1,0:T(8,128)S(1)} collective-permute-done((f32[2144,128]{1,0:T(8,128)S(1)}, f32[2144,128]{1,0:T(8,128)S(1)}, u32[]{:S(2)}, u32[]{:S(2)}) %collective-permute-start.12) | collective-permute-done | bytes 1097760 | tf_op jit(solution)/shard_map/ppermute | solution.py:401
  110.1 7.3 %gram1.1 = (f32[2144,128]{1,0:T(8,128)S(1)}, f32[2144,128]{1,0:T(8,128)S(1)}) custom-call(s32[896]{0:T(1024)S(1)} %get-tuple-element.40.refs_0_, s32[32]{0:T(128)S(1)} %get-tuple-element.41.refs_1_, s32[256]{0:T(256)S(1)} %get-tuple-element.42.refs_2_, bf16[48,64,128]{2,1,0:T(8,128)(2,1)S(1)} %get-tuple-element.52.refs_3_, ...), custom_call_target="tpu_custom_call" | custom-call | flops 1000000000 | bytes 10000000 | tf_op jit(solution)/shard_map/gram1/pallas_call | solution.py:263
  117.4 3.6 %collective-permute-done.20.refs_1_ = f32[2144,128]{1,0:T(8,128)S(1)} collective-permute-done((f32[2144,128]{1,0:T(8,128)S(1)}, f32[2144,128]{1,0:T(8,128)S(1)}, u32[]{:S(2)}, u32[]{:S(2)}) %collective-permute-start.20) | collective-permute-done | bytes 1097760 | tf_op jit(solution)/shard_map/ppermute | solution.py:401
  121.4 5.5 %collective-permute-start.21 = (f32[2144,128]{1,0:T(8,128)S(1)}, f32[2144,128]{1,0:T(8,128)S(1)}, u32[]{:S(2)}, u32[]{:S(2)}) collective-permute-start(f32[2144,128]{1,0:T(8,128)S(1)} %other_total.1), channel_id=1, source_target_pairs={{0,1},{1,0},{2,3},{3,2},{4,5},{5,4},{6,7},{7,6},{8,9},{9,8},{10,11... | collective-permute-start | bytes 3293192 | tf_op jit(solution)/shard_map/ppermute | solution.py:410
  130.1 4.5 %collective-permute-start.22 = (f32[536,128]{1,0:T(8,128)S(1)}, f32[536,128]{1,0:T(8,128)S(1)}, u32[]{:S(2)}, u32[]{:S(2)}) collective-permute-start(f32[536,128]{1,0:T(8,128)S(1)} %get-tuple-element.75), channel_id=1, source_target_pairs={{0,32},{32,64},{64,96},{96,0},{1,33},{33,65},{65,97},{97,1},{2,34}... | collective-permute-start | bytes 823304 | tf_op jit(solution)/shard_map/ppermute | solution.py:414
  134.6 3.4 %collective-permute-start.23 = (f32[536,128]{1,0:T(8,128)S(1)}, f32[536,128]{1,0:T(8,128)S(1)}, u32[]{:S(2)}, u32[]{:S(2)}) collective-permute-start(f32[536,128]{1,0:T(8,128)S(1)} %get-tuple-element.76), channel_id=1, source_target_pairs={{0,64},{32,96},{64,0},{96,32},{1,65},{33,97},{65,1},{97,33},{2,66}... | collective-permute-start | bytes 823304 | tf_op jit(solution)/shard_map/ppermute | solution.py:414
  138.3 5.2 %collective-permute-done.22 = f32[536,128]{1,0:T(8,128)S(1)} collective-permute-done((f32[536,128]{1,0:T(8,128)S(1)}, f32[536,128]{1,0:T(8,128)S(1)}, u32[]{:S(2)}, u32[]{:S(2)}) %collective-permute-start.22) | collective-permute-done | bytes 274464 | tf_op jit(solution)/shard_map/ppermute | solution.py:414
  143.5 6.7 %collective-permute-done.23 = f32[536,128]{1,0:T(8,128)S(1)} collective-permute-done((f32[536,128]{1,0:T(8,128)S(1)}, f32[536,128]{1,0:T(8,128)S(1)}, u32[]{:S(2)}, u32[]{:S(2)}) %collective-permute-start.23) | collective-permute-done | bytes 274464 | tf_op jit(solution)/shard_map/ppermute | solution.py:414
  150.3 2.7 %collective-permute-start.27 = (f32[536,128]{1,0:T(8,128)S(1)}, f32[536,128]{1,0:T(8,128)S(1)}, u32[]{:S(2)}, u32[]{:S(2)}) collective-permute-start(f32[536,128]{1,0:T(8,128)S(1)} %add_add_fusion.refs_0_), channel_id=1, source_target_pairs={{0,96},{32,0},{64,32},{96,64},{1,97},{33,1},{65,33},{97,65},{2,98}... | collective-permute-start | bytes 823304 | tf_op jit(solution)/shard_map/ppermute | solution.py:415
  153.7 6.2 %collective-permute-done.27.refs_3_ = f32[536,128]{1,0:T(8,128)S(1)} collective-permute-done((f32[536,128]{1,0:T(8,128)S(1)}, f32[536,128]{1,0:T(8,128)S(1)}, u32[]{:S(2)}, u32[]{:S(2)}) %collective-permute-start.27) | collective-permute-done | bytes 274464 | tf_op jit(solution)/shard_map/ppermute | solution.py:415
  161.8 7.0 %collective-permute-done.25.refs_1_ = f32[536,128]{1,0:T(8,128)S(1)} collective-permute-done((f32[536,128]{1,0:T(8,128)S(1)}, f32[536,128]{1,0:T(8,128)S(1)}, u32[]{:S(2)}, u32[]{:S(2)}) %collective-permute-start.25) | collective-permute-done | bytes 274464 | tf_op jit(solution)/shard_map/ppermute | solution.py:415
  168.8 3.5 %finish.1 = (f32[32,128]{1,0:T(8,128)}, f32[32,128,128]{2,1,0:T(8,128)}) custom-call(s32[4]{0:T(128)S(1)} %copy-done.1, f32[536,128]{1,0:T(8,128)S(1)} %add_add_fusion.refs_0_, f32[536,128]{1,0:T(8,128)S(1)} %collective-permute-done.25.refs_1_, f32[536,128]{1,0:T(8,128)S(1)} %collective-permute-done.26.refs_2_, f32[536,128]{1,0:T(8,128)S(1)} %collective-permute-done.27.refs_3_), custom_call_target="tpu_custom_call" | custom-call | tf_op jit(solution)/shard_map/finish/pallas_call | solution.py:367
  (57 shorter events, 45.0 us)
Async XLA Ops:
  2.1 10.6 %collective-permute-start.2 = (s32[512]{0:T(512)S(1)}, s32[512]{0:T(512)S(1)}, u32[]{:S(2)}, u32[]{:S(2)}) collective-permute-start(s32[512]{0:T(512)S(1)} %pad_add_fusion.refs_0_), channel_id=1, source_target_pairs={{0,16},{1,5},{2,18},{3,7},{4,20},{5,1},{6,22},{7,3},{8,24},{9,13},... | collective-permute-start | bytes 6152 | tf_op jit(solution)/shard_map/ppermute | solution.py:384
  12.7 12.6 %collective-permute-start.6 = (bf16[48,64,128]{2,1,0:T(8,128)(2,1)}, bf16[48,64,128]{2,1,0:T(8,128)(2,1)S(1)}, u32[]{:S(2)}, u32[]{:S(2)}) collective-permute-start(bf16[48,64,128]{2,1,0:T(8,128)(2,1)} %get-tuple-element.48), channel_id=1, source_target_pairs={{0,8},{1,3},{2,10},{3,5},{4,12},{5,7},{6,14},{7,1},{8,16},{9,11},{... | collective-permute-start | bytes 2359304 | tf_op jit(solution)/shard_map/ppermute | solution.py:398
  13.2 20.0 %collective-permute-start.7 = (bf16[48,64,128]{2,1,0:T(8,128)(2,1)}, bf16[48,64,128]{2,1,0:T(8,128)(2,1)S(1)}, u32[]{:S(2)}, u32[]{:S(2)}) collective-permute-start(bf16[48,64,128]{2,1,0:T(8,128)(2,1)} %get-tuple-element.49), channel_id=1, source_target_pairs={{0,24},{1,7},{2,26},{3,1},{4,28},{5,3},{6,30},{7,5},{8,0},{9,15},{... | collective-permute-start | bytes 2359304 | tf_op jit(solution)/shard_map/ppermute | solution.py:398
  15.5 18.8 %collective-permute-start.8 = (bf16[48,64,128]{2,1,0:T(8,128)(2,1)}, bf16[48,64,128]{2,1,0:T(8,128)(2,1)S(1)}, u32[]{:S(2)}, u32[]{:S(2)}) collective-permute-start(bf16[48,64,128]{2,1,0:T(8,128)(2,1)} %get-tuple-element.50), channel_id=1, source_target_pairs={{0,16},{1,5},{2,18},{3,7},{4,20},{5,1},{6,22},{7,3},{8,24},{9,13},... | collective-permute-start | bytes 2359304 | tf_op jit(solution)/shard_map/ppermute | solution.py:398
  18.3 23.9 %collective-permute-start.3 = (bf16[48,64,128]{2,1,0:T(8,128)(2,1)S(1)}, bf16[48,64,128]{2,1,0:T(8,128)(2,1)S(1)}, u32[]{:S(2)}, u32[]{:S(2)}) collective-permute-start(bf16[48,64,128]{2,1,0:T(8,128)(2,1)S(1)} %get-tuple-element.53), channel_id=1, source_target_pairs={{0,8},{1,3},{2,10},{3,5},{4,12},{5,7},{6,14},{7,1},{8,16},{9,11},{... | collective-permute-start | bytes 2359304 | tf_op jit(solution)/shard_map/ppermute | solution.py:398
  19.2 30.7 %collective-permute-start.4 = (bf16[48,64,128]{2,1,0:T(8,128)(2,1)S(1)}, bf16[48,64,128]{2,1,0:T(8,128)(2,1)S(1)}, u32[]{:S(2)}, u32[]{:S(2)}) collective-permute-start(bf16[48,64,128]{2,1,0:T(8,128)(2,1)S(1)} %get-tuple-element.54), channel_id=1, source_target_pairs={{0,24},{1,7},{2,26},{3,1},{4,28},{5,3},{6,30},{7,5},{8,0},{9,15},{... | collective-permute-start | bytes 2359304 | tf_op jit(solution)/shard_map/ppermute | solution.py:398
  25.3 25.9 %collective-permute-start.5 = (bf16[48,64,128]{2,1,0:T(8,128)(2,1)S(1)}, bf16[48,64,128]{2,1,0:T(8,128)(2,1)S(1)}, u32[]{:S(2)}, u32[]{:S(2)}) collective-permute-start(bf16[48,64,128]{2,1,0:T(8,128)(2,1)S(1)} %get-tuple-element.55), channel_id=1, source_target_pairs={{0,16},{1,5},{2,18},{3,7},{4,20},{5,1},{6,22},{7,3},{8,24},{9,13},... | collective-permute-start | bytes 2359304 | tf_op jit(solution)/shard_map/ppermute | solution.py:398
  36.6 24.2 %collective-permute-start.9 = (bf16[48,64,128]{2,1,0:T(8,128)(2,1)S(1)}, bf16[48,64,128]{2,1,0:T(8,128)(2,1)S(1)}, u32[]{:S(2)}, u32[]{:S(2)}) collective-permute-start(bf16[48,64,128]{2,1,0:T(8,128)(2,1)S(1)} %get-tuple-element.58), channel_id=1, source_target_pairs={{0,8},{1,3},{2,10},{3,5},{4,12},{5,7},{6,14},{7,1},{8,16},{9,11},{... | collective-permute-start | bytes 2359304 | tf_op jit(solution)/shard_map/ppermute | solution.py:398
  37.5 23.3 %collective-permute-start.10 = (bf16[48,64,128]{2,1,0:T(8,128)(2,1)S(1)}, bf16[48,64,128]{2,1,0:T(8,128)(2,1)S(1)}, u32[]{:S(2)}, u32[]{:S(2)}) collective-permute-start(bf16[48,64,128]{2,1,0:T(8,128)(2,1)S(1)} %get-tuple-element.59), channel_id=1, source_target_pairs={{0,24},{1,7},{2,26},{3,1},{4,28},{5,3},{6,30},{7,5},{8,0},{9,15},{... | collective-permute-start | bytes 2359304 | tf_op jit(solution)/shard_map/ppermute | solution.py:398
  42.2 34.8 %collective-permute-start.11 = (bf16[48,64,128]{2,1,0:T(8,128)(2,1)S(1)}, bf16[48,64,128]{2,1,0:T(8,128)(2,1)S(1)}, u32[]{:S(2)}, u32[]{:S(2)}) collective-permute-start(bf16[48,64,128]{2,1,0:T(8,128)(2,1)S(1)} %get-tuple-element.60), channel_id=1, source_target_pairs={{0,16},{1,5},{2,18},{3,7},{4,20},{5,1},{6,22},{7,3},{8,24},{9,13},... | collective-permute-start | bytes 2359304 | tf_op jit(solution)/shard_map/ppermute | solution.py:398
  49.9 47.2 %collective-permute-start.17 = (f32[2144,128]{1,0:T(8,128)S(1)}, f32[2144,128]{1,0:T(8,128)S(1)}, u32[]{:S(2)}, u32[]{:S(2)}) collective-permute-start(f32[2144,128]{1,0:T(8,128)S(1)} %get-tuple-element.69), channel_id=1, source_target_pairs={{0,2},{1,9},{2,4},{3,11},{4,6},{5,13},{6,0},{7,15},{8,10},{9,17},{... | collective-permute-start | bytes 3293192 | tf_op jit(solution)/shard_map/ppermute | solution.py:401
  51.2 45.8 %collective-permute-start.18 = (f32[2144,128]{1,0:T(8,128)S(1)}, f32[2144,128]{1,0:T(8,128)S(1)}, u32[]{:S(2)}, u32[]{:S(2)}) collective-permute-start(f32[2144,128]{1,0:T(8,128)S(1)} %get-tuple-element.70), channel_id=1, source_target_pairs={{0,6},{1,25},{2,0},{3,27},{4,2},{5,29},{6,4},{7,31},{8,14},{9,1},{... | collective-permute-start | bytes 3293192 | tf_op jit(solution)/shard_map/ppermute | solution.py:401
  60.8 26.9 %collective-permute-start.14 = (bf16[48,64,128]{2,1,0:T(8,128)(2,1)S(1)}, bf16[48,64,128]{2,1,0:T(8,128)(2,1)S(1)}, u32[]{:S(2)}, u32[]{:S(2)}) collective-permute-start(bf16[48,64,128]{2,1,0:T(8,128)(2,1)S(1)} %get-tuple-element.66), channel_id=1, source_target_pairs={{0,8},{1,3},{2,10},{3,5},{4,12},{5,7},{6,14},{7,1},{8,16},{9,11},{... | collective-permute-start | bytes 2359304 | tf_op jit(solution)/shard_map/ppermute | solution.py:398
  60.8 33.2 %collective-permute-start.15 = (bf16[48,64,128]{2,1,0:T(8,128)(2,1)S(1)}, bf16[48,64,128]{2,1,0:T(8,128)(2,1)S(1)}, u32[]{:S(2)}, u32[]{:S(2)}) collective-permute-start(bf16[48,64,128]{2,1,0:T(8,128)(2,1)S(1)} %get-tuple-element.67), channel_id=1, source_target_pairs={{0,24},{1,7},{2,26},{3,1},{4,28},{5,3},{6,30},{7,5},{8,0},{9,15},{... | collective-permute-start | bytes 2359304 | tf_op jit(solution)/shard_map/ppermute | solution.py:398
  77.0 20.0 %collective-permute-start.16 = (bf16[48,64,128]{2,1,0:T(8,128)(2,1)S(1)}, bf16[48,64,128]{2,1,0:T(8,128)(2,1)S(1)}, u32[]{:S(2)}, u32[]{:S(2)}) collective-permute-start(bf16[48,64,128]{2,1,0:T(8,128)(2,1)S(1)} %get-tuple-element.68), channel_id=1, source_target_pairs={{0,16},{1,5},{2,18},{3,7},{4,20},{5,1},{6,22},{7,3},{8,24},{9,13},... | collective-permute-start | bytes 2359304 | tf_op jit(solution)/shard_map/ppermute | solution.py:398
  87.7 21.5 %collective-permute-start.12 = (f32[2144,128]{1,0:T(8,128)S(1)}, f32[2144,128]{1,0:T(8,128)S(1)}, u32[]{:S(2)}, u32[]{:S(2)}) collective-permute-start(f32[2144,128]{1,0:T(8,128)S(1)} %get-tuple-element.61), channel_id=1, source_target_pairs={{0,6},{1,25},{2,0},{3,27},{4,2},{5,29},{6,4},{7,31},{8,14},{9,1},{... | collective-permute-start | bytes 3293192 | tf_op jit(solution)/shard_map/ppermute | solution.py:401
  94.0 16.1 %collective-permute-start.13 = (f32[2144,128]{1,0:T(8,128)S(1)}, f32[2144,128]{1,0:T(8,128)S(1)}, u32[]{:S(2)}, u32[]{:S(2)}) collective-permute-start(f32[2144,128]{1,0:T(8,128)S(1)} %get-tuple-element.62), channel_id=1, source_target_pairs={{0,2},{1,9},{2,4},{3,11},{4,6},{5,13},{6,0},{7,15},{8,10},{9,17},{... | collective-permute-start | bytes 3293192 | tf_op jit(solution)/shard_map/ppermute | solution.py:401
  104.5 16.5 %collective-permute-start.20 = (f32[2144,128]{1,0:T(8,128)S(1)}, f32[2144,128]{1,0:T(8,128)S(1)}, u32[]{:S(2)}, u32[]{:S(2)}) collective-permute-start(f32[2144,128]{1,0:T(8,128)S(1)} %get-tuple-element.73), channel_id=1, source_target_pairs={{0,6},{1,25},{2,0},{3,27},{4,2},{5,29},{6,4},{7,31},{8,14},{9,1},{... | collective-permute-start | bytes 3293192 | tf_op jit(solution)/shard_map/ppermute | solution.py:401
  105.6 21.3 %collective-permute-start.19 = (f32[2144,128]{1,0:T(8,128)S(1)}, f32[2144,128]{1,0:T(8,128)S(1)}, u32[]{:S(2)}, u32[]{:S(2)}) collective-permute-start(f32[2144,128]{1,0:T(8,128)S(1)} %get-tuple-element.71), channel_id=1, source_target_pairs={{0,2},{1,9},{2,4},{3,11},{4,6},{5,13},{6,0},{7,15},{8,10},{9,17},{... | collective-permute-start | bytes 3293192 | tf_op jit(solution)/shard_map/ppermute | solution.py:401
  130.1 13.4 %collective-permute-start.22 = (f32[536,128]{1,0:T(8,128)S(1)}, f32[536,128]{1,0:T(8,128)S(1)}, u32[]{:S(2)}, u32[]{:S(2)}) collective-permute-start(f32[536,128]{1,0:T(8,128)S(1)} %get-tuple-element.75), channel_id=1, source_target_pairs={{0,32},{32,64},{64,96},{96,0},{1,33},{33,65},{65,97},{97,1},{2,34}... | collective-permute-start | bytes 823304 | tf_op jit(solution)/shard_map/ppermute | solution.py:414
  134.6 15.6 %collective-permute-start.23 = (f32[536,128]{1,0:T(8,128)S(1)}, f32[536,128]{1,0:T(8,128)S(1)}, u32[]{:S(2)}, u32[]{:S(2)}) collective-permute-start(f32[536,128]{1,0:T(8,128)S(1)} %get-tuple-element.76), channel_id=1, source_target_pairs={{0,64},{32,96},{64,0},{96,32},{1,65},{33,97},{65,1},{97,33},{2,66}... | collective-permute-start | bytes 823304 | tf_op jit(solution)/shard_map/ppermute | solution.py:414
  138.0 12.2 %collective-permute-start.24 = (f32[536,128]{1,0:T(8,128)S(1)}, f32[536,128]{1,0:T(8,128)S(1)}, u32[]{:S(2)}, u32[]{:S(2)}) collective-permute-start(f32[536,128]{1,0:T(8,128)S(1)} %get-tuple-element.77), channel_id=1, source_target_pairs={{0,96},{32,0},{64,32},{96,64},{1,97},{33,1},{65,33},{97,65},{2,98}... | collective-permute-start | bytes 823304 | tf_op jit(solution)/shard_map/ppermute | solution.py:414
  150.3 9.6 %collective-permute-start.27 = (f32[536,128]{1,0:T(8,128)S(1)}, f32[536,128]{1,0:T(8,128)S(1)}, u32[]{:S(2)}, u32[]{:S(2)}) collective-permute-start(f32[536,128]{1,0:T(8,128)S(1)} %add_add_fusion.refs_0_), channel_id=1, source_target_pairs={{0,96},{32,0},{64,32},{96,64},{1,97},{33,1},{65,33},{97,65},{2,98}... | collective-permute-start | bytes 823304 | tf_op jit(solution)/shard_map/ppermute | solution.py:415
  153.7 15.1 %collective-permute-start.25 = (f32[536,128]{1,0:T(8,128)S(1)}, f32[536,128]{1,0:T(8,128)S(1)}, u32[]{:S(2)}, u32[]{:S(2)}) collective-permute-start(f32[536,128]{1,0:T(8,128)S(1)} %add_add_fusion.refs_0_), channel_id=1, source_target_pairs={{0,32},{32,64},{64,96},{96,0},{1,33},{33,65},{65,97},{97,1},{2,34}... | collective-permute-start | bytes 823304 | tf_op jit(solution)/shard_map/ppermute | solution.py:415
  (8 other events, 61.8 us)

commit v4 on v3

--- a/solution.py
+++ b/solution.py
@@ -16,13 +16,14 @@
 RUN = 24
 SLOTS = NC * RUN
 SHIFTS = (0, 1, 3, 2)
+COPIES = 1
 GROUPS = len(SHIFTS)
 CHIP_CELLS = NC * CELL_DEV
 LIST = 4 * GROUPS * SLOTS + 128
 PAIR = 8
 F32 = jnp.float32
 I32 = jnp.int32
-META = 512
+HEAD = 16
 UNITS = (((2, 0), (2, 1)), ((0, 0), (0, 1)), ((1, 1), (3, 0)), ((1, 0), (3, 1)))
 PACKED = CELL_DEV * ROWS
 PIECE = PACKED + 3 * CELL_DEV
@@ -82,44 +83,65 @@
     return owner(pos[2], lax.rem(pos[0] + d, 4), lax.rem(pos[1] + rel, 4), lax.rem(pos[2] + side, 2))
 
 
-def gather_body(flows, pos, counts, vectors, *refs):
+def gather_body(flows, head, pos, counts, vectors, *refs):
+    header, refs = (refs[:2], refs[2:]) if head else ((), refs)
     outs = refs[: len(flows)]
-    offsets, sems = refs[len(flows) :]
+    offsets, sems = refs[len(flows) : len(flows) + 2]
     total = jnp.int32(0)
     for o in range(OWNERS):
         offsets[o] = total
         total = total + counts[o]
     copies = []
+    rows = RUN * ROWS // COPIES
     for out, (d, units) in zip(outs, flows):
         for i, (rel, side) in enumerate(units):
-            o = unit_owner(pos, d, rel, side)
-            start = jnp.minimum(offsets[o], BLK - RUN)
-            copies.append(
-                pltpu.make_async_copy(vectors.at[pl.ds(start, RUN)], out.at[pl.ds(i * RUN, RUN)], sems.at[len(copies)])
-            )
-            copies[-1].start()
+            start = jnp.minimum(offsets[unit_owner(pos, d, rel, side)], BLK - RUN)
+            for part in range(COPIES):
+                copies.append(
+                    pltpu.make_async_copy(
+                        vectors.at[pl.ds(pl.multiple_of(start * ROWS + part * rows, ROWS), rows)],
+                        out.at[pl.ds((i * COPIES + part) * rows, rows)],
+                        sems.at[len(copies)],
+                    )
+                )
+                copies[-1].start()
+    if head:
+        cells, count_row = header
+        text = refs[-1]
+        text[...] = jnp.zeros((HEAD, D), F32)
+        for i in range(BLK // D):
+            text[i : i + 1, :] = cells[:, i * D : (i + 1) * D].astype(F32)
+        text[BLK // D : BLK // D + 1, :OWNERS] = count_row[...].astype(F32)
+        for out in outs:
+            out[pl.ds(SLOTS * ROWS, HEAD), :] = text[...].astype(out.dtype)
     for copy in copies:
         copy.wait()
 
 
-def gather_runs(flows, pos, counts, vectors, name, vmem):
+def gather_runs(flows, pos, counts, vectors, name, header=()):
     def body(*refs):
-        gather_body(flows, *refs)
-
+        gather_body(flows, bool(header), *refs)
+
+    rows = SLOTS * ROWS + (HEAD if header else 0)
     return pl.pallas_call(
         body,
-        out_shape=[jax.ShapeDtypeStruct((SLOTS, ROWS, D), vectors.dtype)] * len(flows),
-        in_specs=[SMEM_SPEC, SMEM_SPEC, HBM_SPEC],
+        out_shape=[jax.ShapeDtypeStruct((rows, D), vectors.dtype)] * len(flows),
+        in_specs=[SMEM_SPEC, SMEM_SPEC, HBM_SPEC] + [VMEM_SPEC] * len(header),
         out_specs=[VMEM_SPEC] * len(flows),
-        scratch_shapes=[pltpu.SMEM((OWNERS,), I32), pltpu.SemaphoreType.DMA((NC * len(flows),))],
-        compiler_params=pltpu.CompilerParams(vmem_limit_bytes=vmem),
+        scratch_shapes=[pltpu.SMEM((OWNERS,), I32), pltpu.SemaphoreType.DMA((2 * COPIES * len(flows),))]
+        + ([pltpu.VMEM((HEAD, D), F32)] if header else []),
+        compiler_params=pltpu.CompilerParams(vmem_limit_bytes=LARGE_VMEM if header else SMALL_VMEM),
         name=name,
-    )(pos, counts, vectors)
-
-
-def lists_body(pos, *refs):
-    metas = refs[:GROUPS]
-    lists, sizes, tallies, offsets = refs[GROUPS:]
+    )(pos, counts, vectors, *header)
+
+
+def lists_body(pos, own_cells, own_counts, *refs):
+    heads = refs[: GROUPS - 1]
+    lists, sizes, tallies, offsets, text, metas, sem = refs[GROUPS - 1 :]
+    for g, head in enumerate(heads):
+        text[pl.ds(g * 8, 8), :] = head[...].astype(F32)[:8].astype(I32)
+    copy = pltpu.make_async_copy(text, metas, sem.at[0])
+    copy.start()
 
     def clear(i, _):
         for u in range(8):
@@ -127,25 +149,33 @@
         return 0
 
     lax.fori_loop(0, 4 * CHIP_CELLS // 8, clear, 0)
+    copy.wait()
+
+    def count_of(g, o):
+        return own_counts[o] if g == 0 else metas[(g - 1) * 8 + BLK // D, o]
+
+    def cell_of(g, i):
+        return own_cells[i] if g == 0 else metas[(g - 1) * 8 + (i >> 7), i & (D - 1)]
+
     for g in range(GROUPS):
         total = jnp.int32(0)
         for o in range(OWNERS):
             offsets[g * OWNERS + o] = total
-            total = total + metas[g][BLK + o]
+            total = total + count_of(g, o)
     begin = jnp.int32(0)
     for group, units in enumerate(UNITS):
         for g in range(GROUPS):
             filled = begin
             for i, (rel, side) in enumerate(units):
                 o = unit_owner(pos, 0, rel, side)
-                n = metas[g][BLK + o]
+                n = count_of(g, o)
                 start = offsets[g * OWNERS + o]
                 slot = i * RUN + start - jnp.minimum(start, BLK - RUN)
                 base = (slot << 17) + i * ((PIECE // 8 << 7) + CELL_DEV)
                 tally = group * CHIP_CELLS + i * CELL_DEV
 
                 def add(j, f, g=g, start=start, base=base, tally=tally):
-                    cell = metas[g][start + j]
+                    cell = cell_of(g, start + j)
                     lists[f + j] = base + (j << 17) + cell * ((ROWS // 8 << 7) + 1)
                     tallies[tally + cell] = tallies[tally + cell] + ROWS
                     return f
@@ -160,7 +190,8 @@
             begin = begin + sizes[2 * segment + 1] * PAIR
 
 
-def make_lists(pos, metas):
+def make_lists(pos, own_cells, own_counts, arrived):
+    head = pl.BlockSpec((HEAD, D), lambda i: (SLOTS * ROWS // HEAD, 0))
     return pl.pallas_call(
         lists_body,
         out_shape=[
@@ -168,12 +199,18 @@
             jax.ShapeDtypeStruct((8 * GROUPS,), I32),
             jax.ShapeDtypeStruct((4 * CHIP_CELLS,), I32),
         ],
-        in_specs=[SMEM_SPEC] * (1 + GROUPS),
+        grid=(1,),
+        in_specs=[SMEM_SPEC] * 3 + [head] * (GROUPS - 1),
         out_specs=[SMEM_SPEC] * 3,
-        scratch_shapes=[pltpu.SMEM((GROUPS * OWNERS,), I32)],
+        scratch_shapes=[
+            pltpu.SMEM((GROUPS * OWNERS,), I32),
+            pltpu.VMEM(((GROUPS - 1) * 8, D), I32),
+            pltpu.SMEM(((GROUPS - 1) * 8, D), I32),
+            pltpu.SemaphoreType.DMA((1,)),
+        ],
         compiler_params=pltpu.CompilerParams(vmem_limit_bytes=SMALL_VMEM),
         name="lists",
-    )(pos, *metas)
+    )(pos, own_cells, own_counts, *arrived)
 
 
 def add_blocks(segment, lists, sizes, buf, acc, acc_s, acc_q):
@@ -187,7 +224,7 @@
         done = []
         for u in range(PAIR):
             entry = lists[begin + i * PAIR + u]
-            block = buf[entry >> 17]
+            block = buf[pl.ds(pl.multiple_of((entry >> 17) * ROWS, ROWS), ROWS), :]
             turned = jnp.concatenate([block[:, ROWS:], block[:, :ROWS]], axis=1)
             top = lax.dot_general(block[:, :ROWS], block, contract, preferred_element_type=F32)
             low = lax.dot_general(block[:, ROWS:], turned, contract, preferred_element_type=F32)
@@ -213,14 +250,20 @@
 
 def gram_body(group, started, lists, sizes, tallies, *refs):
     blocks = refs[:GROUPS]
-    starts = refs[GROUPS : GROUPS + started]
-    outs = refs[GROUPS + started : GROUPS + started + 2]
-    acc, acc_s, acc_q = refs[GROUPS + started + 2 :]
+    first, second = started
+    starts = (refs[GROUPS : GROUPS + first], refs[GROUPS + first : GROUPS + first + second])
+    outs = refs[GROUPS + first + second :][:2]
+    acc, acc_s, acc_q = refs[GROUPS + first + second + 2 :]
+
+    def add_starts(value, u, rows):
+        for start in starts[u]:
+            value = value + start[rows, :]
+        return value
 
     def clear(i, _):
         rows = pl.ds(pl.multiple_of(i * ROWS, ROWS), ROWS)
         for u in range(2):
-            value = starts[u][rows, :] if started else jnp.zeros((ROWS, D), F32)
+            value = add_starts(jnp.zeros((ROWS, D), F32), u, rows)
             acc[pl.ds(pl.multiple_of(u * PIECE + i * ROWS, 8), ROWS), :] = value
         return 0
 
@@ -248,28 +291,28 @@
             for j in range(1, 8):
                 total = total + source[pl.ds(u * CELL_DEV * 8 + j, CELL_DEV, stride=8), :]
             rows = pl.ds(PACKED + k * CELL_DEV, CELL_DEV)
-            outs[u][rows, :] = total + starts[u][rows, :] if started else total
+            outs[u][rows, :] = add_starts(total, u, rows)
         for j in range(CELL_DEV):
             count = jnp.full((1, D), tallies[group * CHIP_CELLS + u * CELL_DEV + j].astype(F32), F32)
             rows = pl.ds(PACKED + 2 * CELL_DEV + j, 1)
-            outs[u][rows, :] = count + starts[u][rows, :] if started else count
-
-
-def gram(group, lists, sizes, tallies, blocks, starts=()):
+            outs[u][rows, :] = add_starts(count, u, rows)
+
+
+def gram(group, lists, sizes, tallies, blocks, first=(), second=()):
     def body(*refs):
-        gram_body(group, len(starts), *refs)
+        gram_body(group, (len(first), len(second)), *refs)
 
     half = jax.ShapeDtypeStruct((PIECE, D), F32)
     return pl.pallas_call(
         body,
         out_shape=[half, half],
-        in_specs=[SMEM_SPEC] * 3 + [VMEM_SPEC] * (GROUPS + len(starts)),
+        in_specs=[SMEM_SPEC] * 3 + [VMEM_SPEC] * (GROUPS + len(first) + len(second)),
         out_specs=[VMEM_SPEC] * 2,
         scratch_shapes=[pltpu.VMEM((NC * PIECE, D), F32)] + [pltpu.VMEM(((CHIP_CELLS + 1) * 8, D), F32)] * 2,
         compiler_params=pltpu.CompilerParams(vmem_limit_bytes=SMALL_VMEM),
         cost_estimate=pl.CostEstimate(flops=10**9, bytes_accessed=10**7, transcendentals=0),
         name=f"gram{group}",
-    )(lists, sizes, tallies, *blocks, *starts)
+    )(lists, sizes, tallies, *blocks, *first, *second)
 
 
 def total_body(*refs):
@@ -379,23 +422,26 @@
 
 def local(vectors, block_cells, dest_counts):
     pos = place()
-    counts = dest_counts[0, 0]
-    meta = jnp.concatenate([block_cells[0], counts, jnp.zeros((META - BLK - OWNERS,), I32)])
-    metas = [meta] + [lax.ppermute(meta, "cell", along(d)) for d in SHIFTS[1:]]
-    lists, sizes, tallies = make_lists(pos, metas)
+    counts, cells = dest_counts[0, 0], block_cells[0]
+    rows = vectors.reshape(BLK * ROWS, D)
     sent, got = [], []
     for group, units in enumerate(UNITS):
-        turn = pos
-        if group == 1:
+        turn, flows, header = pos, [(d, units) for d in SHIFTS], ()
+        if group == 0:
+            flows, header = flows[1:], (block_cells, dest_counts[0])
+        elif group == 1:
             turn, *_ = lax.optimization_barrier((pos, *sent[0]))
-        elif group > 1:
-            turn, *_ = lax.optimization_barrier((pos, sizes, *got[group - 2][1:]))
-        runs = gather_runs([(d, units) for d in SHIFTS], turn, counts, vectors[0], f"gather{group}", LARGE_VMEM if group == 0 else SMALL_VMEM)
-        if group == 0:
-            *_, r0, r1, r2, r3 = lax.optimization_barrier((*metas, *runs))
-            runs = [r0, r1, r2, r3]
+            flows = flows[1:]
+        else:
+            if group == 2:
+                lists, sizes, tallies = make_lists(pos, cells, counts, got[0])
+            turn, *_ = lax.optimization_barrier((pos, sizes, *got[group - 2][-3:]))
+            flows = [(0, UNITS[group - 2])] + flows
+        runs = gather_runs(flows, turn, counts, rows, f"gather{group}", header)
         sent.append(runs)
-        got.append([runs[0]] + [lax.ppermute(run, "cell", along(d)) for d, run in zip(SHIFTS[1:], runs[1:])])
+        if group > 1:
+            got[group - 2].insert(0, runs[0])
+        got.append(list(runs[1:-3]) + [lax.ppermute(run, "cell", along(d)) for d, run in zip(SHIFTS[1:], runs[-3:])])
 
     def step(rel, piece):
         return lax.ppermute(piece, "cell", across(rel))
@@ -404,9 +450,9 @@
     fore, back = step(1, fore), step(3, back)
     left, right = gram(2, lists, sizes, tallies, got[2])
     other1, own3 = step(1, left), step(3, right)
-    left, right = gram(3, lists, sizes, tallies, got[3], (fore, back))
+    left, right = gram(3, lists, sizes, tallies, got[3], (fore,), (back,))
     own1, other3 = step(1, left), step(3, right)
-    own, other = gram(1, lists, sizes, tallies, got[1], (own3, other1))
+    own, other = gram(1, lists, sizes, tallies, got[1], (own3,), (other1,))
     swapped = lax.ppermute(other_total([other, other3]), "cell", SWAP)
     quarters = join(pos, [own, own1, swapped])
     mine = quarters[0]

time: 174 us -> 165 us (0.948)
  waiting for transfers between devices: 75.1 us -> 56.2 us
  local copies, waits for them, and re-layouts: 0.02 us -> 5.58 us
  Pallas kernels: 50.8 us -> 54.9 us
  starting transfers between devices: 43.5 us -> 46 us
    ppermute x12, waiting for transfers between devices: 38 us -> 20.6 us  [local(): lax.ppermute(run, 'cell', along(d))]
    ppermute x12, starting transfers between devices: 12.8 us -> 24.9 us  [local(): lax.ppermute(run, 'cell', along(d))]
    unnamed x8 -> x12, local copies, waits for them, and re-layouts: 0.01 us -> 5.58 us
    ppermute x3 -> x0, starting transfers between devices: 5.21 us -> none  [local(): metas = [meta] + [lax.ppermute(meta, 'cell', along(d)) for d in SHIFTS[1:]]]
    ppermute x6, starting transfers between devices: 8.45 us -> 4.91 us  [step(): return lax.ppermute(piece, 'cell', across(rel))]
    ppermute x3, waiting for transfers between devices: 15.1 us -> 11.8 us  [local(): lax.ppermute(mine, 'dp', dp_perm(dz))]
    ppermute x3, starting transfers between devices: 8.16 us -> 5.7 us  [local(): mine = mine + lax.ppermute(quarters[dz], 'dp', dp_perm(dz))]
    ppermute x6, waiting for transfers between devices: 7.67 us -> 9.67 us  [step(): return lax.ppermute(piece, 'cell', across(rel))]
  transfers between devices with their start and end apart: 28 -> 25, of which waited for: 20 -> 13; matrix products, arithmetic and copies ran while one was open for 0% -> 0% of each run, Pallas kernels for 27% -> 28%
where the time goes in v4:
time: 165 us; the launch traced here: 164 us
  waiting for transfers between devices  56.2 us (34%)
  Pallas kernels  54.9 us (33%)
  starting transfers between devices  46 us (28%)
  local copies, waits for them, and re-layouts  5.58 us (3%)
    pallas_call x4, Pallas kernels, gram(): pl.pallas_call(body, out_shape=[half, half], in_specs=[SMEM_SPEC] * 3 + [...  29.8 us
    ppermute x12, starting transfers between devices, local(): lax.ppermute(run, 'cell', along(d))  24.9 us
    ppermute x12, waiting for transfers between devices, local(): lax.ppermute(run, 'cell', along(d))  20.6 us
    pallas_call x4, Pallas kernels, gather_runs(): pl.pallas_call(body, out_shape=[jax.ShapeDtypeStruct((rows, D), vectors.d...  13 us
    ppermute x3, waiting for transfers between devices, local(): lax.ppermute(mine, 'dp', dp_perm(dz))  11.8 us
    ppermute x3, waiting for transfers between devices, local(): mine = mine + lax.ppermute(quarters[dz], 'dp', dp_perm(dz))  11.7 us
    ppermute x6, waiting for transfers between devices, step(): return lax.ppermute(piece, 'cell', across(rel))  9.67 us
    pallas_call x1, Pallas kernels, make_lists(): pl.pallas_call(lists_body, out_shape=[jax.ShapeDtypeStruct((LIST,), I32),...  7.39 us
  transfers between devices with their start and end apart: 25, of which 13 were waited for; matrix products, arithmetic and copies ran while one was open for 0% of the time, Pallas kernels for 28%

profile of v4, /device:TPU:1, one launch (start us, length us, event | category | flops | bytes accessed | tf_op | source)
XLA Modules:
  0.0 164.2 jit_solution(15551265400518676678)
XLA Ops:
  1.3 4.3 %gather0.1 = (bf16[3088,128]{1,0:T(8,128)(2,1)}, bf16[3088,128]{1,0:T(8,128)(2,1)}, bf16[3088,128]{1,0:T(8,128)(2,1)}) custom-call(s32[4]{0:T(128)} %pad_add_fusion.refs_0_.pos, s32[32]{0:T(128)} %bitcast.11, bf16[24576,128]{1,0:T(8,128)(2,1)} %bitcast.7, s32[1,384]{1,0:T(1,128)} %refs_3_.1, s32[1,32]{1,0:T(1,128)} %bitcast.12), custom_call_target="tpu_custom_call" | custom-call | tf_op jit(solution)/shard_map/gather0/pallas_call | solution.py:126
  10.9 3.2 %gather1.1 = (bf16[3072,128]{1,0:T(8,128)(2,1)}, bf16[3072,128]{1,0:T(8,128)(2,1)}, bf16[3072,128]{1,0:T(8,128)(2,1)}) custom-call(s32[4]{0:T(128)S(1)} %copy-done.3, s32[32]{0:T(128)S(1)} %bitcast.13, bf16[24576,128]{1,0:T(8,128)(2,1)S(1)} %bitcast.8), custom_call_target="tpu_custom_call" | custom-call | tf_op jit(solution)/shard_map/gather1/pallas_call | solution.py:126
  19.2 10.2 %collective-permute-start.5 = (bf16[3072,128]{1,0:T(8,128)(2,1)}, bf16[3072,128]{1,0:T(8,128)(2,1)}, u32[]{:S(2)}, u32[]{:S(2)}) collective-permute-start(bf16[3072,128]{1,0:T(8,128)(2,1)} %get-tuple-element.45), channel_id=1, source_target_pairs={{0,16},{1,5},{2,18},{3,7},{4,20},{5,1},{6,22},{7,3},{8,24},{9,13},... | collective-permute-start | bytes 2359304 | tf_op jit(solution)/shard_map/ppermute | solution.py:444
  29.4 7.4 %lists.1 = (s32[896]{0:T(1024)S(1)}, s32[32]{0:T(128)S(1)}, s32[256]{0:T(256)S(1)}) custom-call(s32[4]{0:T(128)S(1)} %copy-done.3, s32[384]{0:T(512)S(1)} %reduce.own_cells, s32[32]{0:T(128)S(1)} %bitcast.14, bf16[3088,128]{1,0:T(8,128)(2,1)S(1)} %collective-permute-done.refs_0_.refs_4_, bf16[3088,128]{1,0:T(8,128)(2,1)S(1)} %collective-permute-done.1.refs_1_.refs_5_, ...), custom_call_target="tpu_custom_call" | custom-call | tf_op jit(solution)/shard_map/lists/pallas_call | solution.py:195
  36.8 2.8 %copy-done.1 = bf16[1,384,64,128]{3,2,1,0:T(8,128)(2,1)S(1)} copy-done((bf16[1,384,64,128]{3,2,1,0:T(8,128)(2,1)S(1)}, bf16[1,384,64,128]{3,2,1,0:T(8,128)(2,1)}, u32[]{:S(2)}) %copy-start.1) | copy-done | bytes 6291480
  39.6 2.7 %gather2.1 = (bf16[3072,128]{1,0:T(8,128)(2,1)S(1)}, bf16[3072,128]{1,0:T(8,128)(2,1)S(1)}, bf16[3072,128]{1,0:T(8,128)(2,1)S(1)}, bf16[3072,128]{1,0:T(8,128)(2,1)S(1)}, bf16[3072,128]{1,0:T(8,128)(2,1)S(1)}) custom-call(s32[4]{0:T(128)S(1)} %copy-done.3, s32[32]{0:T(128)S(1)} %bitcast.15, bf16[24576,128]{1,0:T(8,128)(2,1)S(1)} %bitcast.9), custom_call_target="tpu_custom_call" | custom-call | tf_op jit(solution)/shard_map/gather2/pallas_call | solution.py:126
  45.5 8.2 %gram0.1 = (f32[2144,128]{1,0:T(8,128)S(1)}, f32[2144,128]{1,0:T(8,128)S(1)}) custom-call(s32[896]{0:T(1024)S(1)} %get-tuple-element.39.refs_0_, s32[32]{0:T(128)S(1)} %get-tuple-element.40.refs_1_, s32[256]{0:T(256)S(1)} %get-tuple-element.41.refs_2_, bf16[3072,128]{1,0:T(8,128)(2,1)S(1)} %get-tuple-element.60.refs_3_, ...), custom_call_target="tpu_custom_call" | custom-call | flops 1000000000 | bytes 10000000 | tf_op jit(solution)/shard_map/gram0/pallas_call | solution.py:306
  56.4 2.8 %copy-done.2 = bf16[1,384,64,128]{3,2,1,0:T(8,128)(2,1)S(1)} copy-done((bf16[1,384,64,128]{3,2,1,0:T(8,128)(2,1)S(1)}, bf16[1,384,64,128]{3,2,1,0:T(8,128)(2,1)}, u32[]{:S(2)}) %copy-start.2) | copy-done | bytes 6291480
  59.2 2.7 %gather3.1 = (bf16[3072,128]{1,0:T(8,128)(2,1)S(1)}, bf16[3072,128]{1,0:T(8,128)(2,1)S(1)}, bf16[3072,128]{1,0:T(8,128)(2,1)S(1)}, bf16[3072,128]{1,0:T(8,128)(2,1)S(1)}, bf16[3072,128]{1,0:T(8,128)(2,1)S(1)}) custom-call(s32[4]{0:T(128)S(1)} %copy-done.3, s32[32]{0:T(128)S(1)} %bitcast.16, bf16[24576,128]{1,0:T(8,128)(2,1)S(1)} %bitcast.10), custom_call_target="tpu_custom_call" | custom-call | tf_op jit(solution)/shard_map/gather3/pallas_call | solution.py:126
  63.7 3.4 %collective-permute-start.12 = (bf16[3072,128]{1,0:T(8,128)(2,1)S(1)}, bf16[3072,128]{1,0:T(8,128)(2,1)S(1)}, u32[]{:S(2)}, u32[]{:S(2)}) collective-permute-start(bf16[3072,128]{1,0:T(8,128)(2,1)S(1)} %get-tuple-element.58), channel_id=1, source_target_pairs={{0,24},{1,7},{2,26},{3,1},{4,28},{5,3},{6,30},{7,5},{8,0},{9,15},{... | collective-permute-start | bytes 2359304 | tf_op jit(solution)/shard_map/ppermute | solution.py:444
  67.1 8.4 %gram2.1 = (f32[2144,128]{1,0:T(8,128)S(1)}, f32[2144,128]{1,0:T(8,128)S(1)}) custom-call(s32[896]{0:T(1024)S(1)} %get-tuple-element.39.refs_0_, s32[32]{0:T(128)S(1)} %get-tuple-element.40.refs_1_, s32[256]{0:T(256)S(1)} %get-tuple-element.41.refs_2_, bf16[3072,128]{1,0:T(8,128)(2,1)S(1)} %get-tuple-element.49.refs_3_, ...), custom_call_target="tpu_custom_call" | custom-call | flops 1000000000 | bytes 10000000 | tf_op jit(solution)/shard_map/gram2/pallas_call | solution.py:306
  75.5 7.4 %collective-permute-done.11.refs_4_ = bf16[3072,128]{1,0:T(8,128)(2,1)S(1)} collective-permute-done((bf16[3072,128]{1,0:T(8,128)(2,1)S(1)}, bf16[3072,128]{1,0:T(8,128)(2,1)S(1)}, u32[]{:S(2)}, u32[]{:S(2)}) %collective-permute-start.11) | collective-permute-done | bytes 786464 | tf_op jit(solution)/shard_map/ppermute | solution.py:444
  82.9 8.1 %collective-permute-done.12.refs_5_ = bf16[3072,128]{1,0:T(8,128)(2,1)S(1)} collective-permute-done((bf16[3072,128]{1,0:T(8,128)(2,1)S(1)}, bf16[3072,128]{1,0:T(8,128)(2,1)S(1)}, u32[]{:S(2)}, u32[]{:S(2)}) %collective-permute-start.12) | collective-permute-done | bytes 786464 | tf_op jit(solution)/shard_map/ppermute | solution.py:444
  92.2 7.1 %gram3.1 = (f32[2144,128]{1,0:T(8,128)S(1)}, f32[2144,128]{1,0:T(8,128)S(1)}) custom-call(s32[896]{0:T(1024)S(1)} %get-tuple-element.39.refs_0_, s32[32]{0:T(128)S(1)} %get-tuple-element.40.refs_1_, s32[256]{0:T(256)S(1)} %get-tuple-element.41.refs_2_, bf16[3072,128]{1,0:T(8,128)(2,1)S(1)} %get-tuple-element.56.refs_3_, ...), custom_call_target="tpu_custom_call" | custom-call | flops 1000000000 | bytes 10000000 | tf_op jit(solution)/shard_map/gram3/pallas_call | solution.py:306
  101.5 3.0 %collective-permute-done.10.refs_8_ = f32[2144,128]{1,0:T(8,128)S(1)} collective-permute-done((f32[2144,128]{1,0:T(8,128)S(1)}, f32[2144,128]{1,0:T(8,128)S(1)}, u32[]{:S(2)}, u32[]{:S(2)}) %collective-permute-start.10) | collective-permute-done | bytes 1097760 | tf_op jit(solution)/shard_map/ppermute | solution.py:447
  105.5 6.1 %gram1.1 = (f32[2144,128]{1,0:T(8,128)S(1)}, f32[2144,128]{1,0:T(8,128)S(1)}) custom-call(s32[896]{0:T(1024)S(1)} %get-tuple-element.39.refs_0_, s32[32]{0:T(128)S(1)} %get-tuple-element.40.refs_1_, s32[256]{0:T(256)S(1)} %get-tuple-element.41.refs_2_, bf16[3072,128]{1,0:T(8,128)(2,1)S(1)} %get-tuple-element.47.refs_3_, ...), custom_call_target="tpu_custom_call" | custom-call | flops 1000000000 | bytes 10000000 | tf_op jit(solution)/shard_map/gram1/pallas_call | solution.py:306
  111.7 5.6 %collective-permute-done.17.refs_1_ = f32[2144,128]{1,0:T(8,128)S(1)} collective-permute-done((f32[2144,128]{1,0:T(8,128)S(1)}, f32[2144,128]{1,0:T(8,128)S(1)}, u32[]{:S(2)}, u32[]{:S(2)}) %collective-permute-start.17) | collective-permute-done | bytes 1097760 | tf_op jit(solution)/shard_map/ppermute | solution.py:447
  117.7 6.4 %collective-permute-start.18 = (f32[2144,128]{1,0:T(8,128)S(1)}, f32[2144,128]{1,0:T(8,128)S(1)}, u32[]{:S(2)}, u32[]{:S(2)}) collective-permute-start(f32[2144,128]{1,0:T(8,128)S(1)} %other_total.1), channel_id=1, source_target_pairs={{0,1},{1,0},{2,3},{3,2},{4,5},{5,4},{6,7},{7,6},{8,9},{9,8},{10,11... | collective-permute-start | bytes 3293192 | tf_op jit(solution)/shard_map/ppermute | solution.py:456
  129.4 3.0 %collective-permute-start.20 = (f32[536,128]{1,0:T(8,128)S(1)}, f32[536,128]{1,0:T(8,128)S(1)}, u32[]{:S(2)}, u32[]{:S(2)}) collective-permute-start(f32[536,128]{1,0:T(8,128)S(1)} %get-tuple-element.68), channel_id=1, source_target_pairs={{0,64},{32,96},{64,0},{96,32},{1,65},{33,97},{65,1},{97,33},{2,66}... | collective-permute-start | bytes 823304 | tf_op jit(solution)/shard_map/ppermute | solution.py:460
  133.0 5.0 %collective-permute-done.19 = f32[536,128]{1,0:T(8,128)S(1)} collective-permute-done((f32[536,128]{1,0:T(8,128)S(1)}, f32[536,128]{1,0:T(8,128)S(1)}, u32[]{:S(2)}, u32[]{:S(2)}) %collective-permute-start.19) | collective-permute-done | bytes 274464 | tf_op jit(solution)/shard_map/ppermute | solution.py:460
  137.9 6.7 %collective-permute-done.20 = f32[536,128]{1,0:T(8,128)S(1)} collective-permute-done((f32[536,128]{1,0:T(8,128)S(1)}, f32[536,128]{1,0:T(8,128)S(1)}, u32[]{:S(2)}, u32[]{:S(2)}) %collective-permute-start.20) | collective-permute-done | bytes 274464 | tf_op jit(solution)/shard_map/ppermute | solution.py:460
  148.9 4.0 %collective-permute-done.22.refs_1_ = f32[536,128]{1,0:T(8,128)S(1)} collective-permute-done((f32[536,128]{1,0:T(8,128)S(1)}, f32[536,128]{1,0:T(8,128)S(1)}, u32[]{:S(2)}, u32[]{:S(2)}) %collective-permute-start.22) | collective-permute-done | bytes 274464 | tf_op jit(solution)/shard_map/ppermute | solution.py:461
  152.9 7.8 %collective-permute-done.23.refs_2_ = f32[536,128]{1,0:T(8,128)S(1)} collective-permute-done((f32[536,128]{1,0:T(8,128)S(1)}, f32[536,128]{1,0:T(8,128)S(1)}, u32[]{:S(2)}, u32[]{:S(2)}) %collective-permute-start.23) | collective-permute-done | bytes 274464 | tf_op jit(solution)/shard_map/ppermute | solution.py:461
  160.7 3.5 %finish.1 = (f32[32,128]{1,0:T(8,128)}, f32[32,128,128]{2,1,0:T(8,128)}) custom-call(s32[4]{0:T(128)S(1)} %copy-done.3, f32[536,128]{1,0:T(8,128)S(1)} %add_add_fusion.refs_0_, f32[536,128]{1,0:T(8,128)S(1)} %collective-permute-done.22.refs_1_, f32[536,128]{1,0:T(8,128)S(1)} %collective-permute-done.23.refs_2_, f32[536,128]{1,0:T(8,128)S(1)} %collective-permute-done.24.refs_3_), custom_call_target="tpu_custom_call" | custom-call | tf_op jit(solution)/shard_map/finish/pallas_call | solution.py:410
  (53 shorter events, 33.3 us)
Async XLA Ops:
  5.6 13.6 %collective-permute-start = (bf16[3088,128]{1,0:T(8,128)(2,1)}, bf16[3088,128]{1,0:T(8,128)(2,1)S(1)}, u32[]{:S(2)}, u32[]{:S(2)}) collective-permute-start(bf16[3088,128]{1,0:T(8,128)(2,1)} %get-tuple-element.36), channel_id=1, source_target_pairs={{0,8},{1,3},{2,10},{3,5},{4,12},{5,7},{6,14},{7,1},{8,16},{9,11},{... | collective-permute-start | bytes 2371592 | tf_op jit(solution)/shard_map/ppermute | solution.py:444
  7.8 21.6 %collective-permute-start.1 = (bf16[3088,128]{1,0:T(8,128)(2,1)}, bf16[3088,128]{1,0:T(8,128)(2,1)S(1)}, u32[]{:S(2)}, u32[]{:S(2)}) collective-permute-start(bf16[3088,128]{1,0:T(8,128)(2,1)} %get-tuple-element.37), channel_id=1, source_target_pairs={{0,24},{1,7},{2,26},{3,1},{4,28},{5,3},{6,30},{7,5},{8,0},{9,15},{... | collective-permute-start | bytes 2371592 | tf_op jit(solution)/shard_map/ppermute | solution.py:444
  9.3 20.1 %collective-permute-start.2 = (bf16[3088,128]{1,0:T(8,128)(2,1)}, bf16[3088,128]{1,0:T(8,128)(2,1)}, u32[]{:S(2)}, u32[]{:S(2)}) collective-permute-start(bf16[3088,128]{1,0:T(8,128)(2,1)} %get-tuple-element.38), channel_id=1, source_target_pairs={{0,16},{1,5},{2,18},{3,7},{4,20},{5,1},{6,22},{7,3},{8,24},{9,13},... | collective-permute-start | bytes 2371592 | tf_op jit(solution)/shard_map/ppermute | solution.py:444
  14.1 30.9 %collective-permute-start.3 = (bf16[3072,128]{1,0:T(8,128)(2,1)}, bf16[3072,128]{1,0:T(8,128)(2,1)S(1)}, u32[]{:S(2)}, u32[]{:S(2)}) collective-permute-start(bf16[3072,128]{1,0:T(8,128)(2,1)} %get-tuple-element.43), channel_id=1, source_target_pairs={{0,8},{1,3},{2,10},{3,5},{4,12},{5,7},{6,14},{7,1},{8,16},{9,11},{... | collective-permute-start | bytes 2359304 | tf_op jit(solution)/shard_map/ppermute | solution.py:444
  14.6 39.1 %collective-permute-start.4 = (bf16[3072,128]{1,0:T(8,128)(2,1)}, bf16[3072,128]{1,0:T(8,128)(2,1)}, u32[]{:S(2)}, u32[]{:S(2)}) collective-permute-start(bf16[3072,128]{1,0:T(8,128)(2,1)} %get-tuple-element.44), channel_id=1, source_target_pairs={{0,24},{1,7},{2,26},{3,1},{4,28},{5,3},{6,30},{7,5},{8,0},{9,15},{... | collective-permute-start | bytes 2359304 | tf_op jit(solution)/shard_map/ppermute | solution.py:444
  19.2 34.6 %collective-permute-start.5 = (bf16[3072,128]{1,0:T(8,128)(2,1)}, bf16[3072,128]{1,0:T(8,128)(2,1)}, u32[]{:S(2)}, u32[]{:S(2)}) collective-permute-start(bf16[3072,128]{1,0:T(8,128)(2,1)} %get-tuple-element.45), channel_id=1, source_target_pairs={{0,16},{1,5},{2,18},{3,7},{4,20},{5,1},{6,22},{7,3},{8,24},{9,13},... | collective-permute-start | bytes 2359304 | tf_op jit(solution)/shard_map/ppermute | solution.py:444
  42.3 19.6 %collective-permute-start.6 = (bf16[3072,128]{1,0:T(8,128)(2,1)S(1)}, bf16[3072,128]{1,0:T(8,128)(2,1)S(1)}, u32[]{:S(2)}, u32[]{:S(2)}) collective-permute-start(bf16[3072,128]{1,0:T(8,128)(2,1)S(1)} %get-tuple-element.50), channel_id=1, source_target_pairs={{0,8},{1,3},{2,10},{3,5},{4,12},{5,7},{6,14},{7,1},{8,16},{9,11},{... | collective-permute-start | bytes 2359304 | tf_op jit(solution)/shard_map/ppermute | solution.py:444
  42.4 21.3 %collective-permute-start.7 = (bf16[3072,128]{1,0:T(8,128)(2,1)S(1)}, bf16[3072,128]{1,0:T(8,128)(2,1)S(1)}, u32[]{:S(2)}, u32[]{:S(2)}) collective-permute-start(bf16[3072,128]{1,0:T(8,128)(2,1)S(1)} %get-tuple-element.51), channel_id=1, source_target_pairs={{0,24},{1,7},{2,26},{3,1},{4,28},{5,3},{6,30},{7,5},{8,0},{9,15},{... | collective-permute-start | bytes 2359304 | tf_op jit(solution)/shard_map/ppermute | solution.py:444
  45.1 22.0 %collective-permute-start.8 = (bf16[3072,128]{1,0:T(8,128)(2,1)S(1)}, bf16[3072,128]{1,0:T(8,128)(2,1)S(1)}, u32[]{:S(2)}, u32[]{:S(2)}) collective-permute-start(bf16[3072,128]{1,0:T(8,128)(2,1)S(1)} %get-tuple-element.52), channel_id=1, source_target_pairs={{0,16},{1,5},{2,18},{3,7},{4,20},{5,1},{6,22},{7,3},{8,24},{9,13},... | collective-permute-start | bytes 2359304 | tf_op jit(solution)/shard_map/ppermute | solution.py:444
  53.7 38.5 %collective-permute-start.14 = (f32[2144,128]{1,0:T(8,128)S(1)}, f32[2144,128]{1,0:T(8,128)S(1)}, u32[]{:S(2)}, u32[]{:S(2)}) collective-permute-start(f32[2144,128]{1,0:T(8,128)S(1)} %get-tuple-element.61), channel_id=1, source_target_pairs={{0,2},{1,9},{2,4},{3,11},{4,6},{5,13},{6,0},{7,15},{8,10},{9,17},{... | collective-permute-start | bytes 3293192 | tf_op jit(solution)/shard_map/ppermute | solution.py:447
  53.8 38.4 %collective-permute-start.15 = (f32[2144,128]{1,0:T(8,128)S(1)}, f32[2144,128]{1,0:T(8,128)S(1)}, u32[]{:S(2)}, u32[]{:S(2)}) collective-permute-start(f32[2144,128]{1,0:T(8,128)S(1)} %get-tuple-element.62), channel_id=1, source_target_pairs={{0,6},{1,25},{2,0},{3,27},{4,2},{5,29},{6,4},{7,31},{8,14},{9,1},{... | collective-permute-start | bytes 3293192 | tf_op jit(solution)/shard_map/ppermute | solution.py:447
  61.9 21.0 %collective-permute-start.11 = (bf16[3072,128]{1,0:T(8,128)(2,1)S(1)}, bf16[3072,128]{1,0:T(8,128)(2,1)S(1)}, u32[]{:S(2)}, u32[]{:S(2)}) collective-permute-start(bf16[3072,128]{1,0:T(8,128)(2,1)S(1)} %get-tuple-element.57), channel_id=1, source_target_pairs={{0,8},{1,3},{2,10},{3,5},{4,12},{5,7},{6,14},{7,1},{8,16},{9,11},{... | collective-permute-start | bytes 2359304 | tf_op jit(solution)/shard_map/ppermute | solution.py:444
  63.7 27.4 %collective-permute-start.12 = (bf16[3072,128]{1,0:T(8,128)(2,1)S(1)}, bf16[3072,128]{1,0:T(8,128)(2,1)S(1)}, u32[]{:S(2)}, u32[]{:S(2)}) collective-permute-start(bf16[3072,128]{1,0:T(8,128)(2,1)S(1)} %get-tuple-element.58), channel_id=1, source_target_pairs={{0,24},{1,7},{2,26},{3,1},{4,28},{5,3},{6,30},{7,5},{8,0},{9,15},{... | collective-permute-start | bytes 2359304 | tf_op jit(solution)/shard_map/ppermute | solution.py:444
  67.1 25.1 %collective-permute-start.13 = (bf16[3072,128]{1,0:T(8,128)(2,1)S(1)}, bf16[3072,128]{1,0:T(8,128)(2,1)S(1)}, u32[]{:S(2)}, u32[]{:S(2)}) collective-permute-start(bf16[3072,128]{1,0:T(8,128)(2,1)S(1)} %get-tuple-element.59), channel_id=1, source_target_pairs={{0,16},{1,5},{2,18},{3,7},{4,20},{5,1},{6,22},{7,3},{8,24},{9,13},... | collective-permute-start | bytes 2359304 | tf_op jit(solution)/shard_map/ppermute | solution.py:444
  82.9 21.6 %collective-permute-start.10 = (f32[2144,128]{1,0:T(8,128)S(1)}, f32[2144,128]{1,0:T(8,128)S(1)}, u32[]{:S(2)}, u32[]{:S(2)}) collective-permute-start(f32[2144,128]{1,0:T(8,128)S(1)} %get-tuple-element.54), channel_id=1, source_target_pairs={{0,2},{1,9},{2,4},{3,11},{4,6},{5,13},{6,0},{7,15},{8,10},{9,17},{... | collective-permute-start | bytes 3293192 | tf_op jit(solution)/shard_map/ppermute | solution.py:447
  91.1 14.5 %collective-permute-start.9 = (f32[2144,128]{1,0:T(8,128)S(1)}, f32[2144,128]{1,0:T(8,128)S(1)}, u32[]{:S(2)}, u32[]{:S(2)}) collective-permute-start(f32[2144,128]{1,0:T(8,128)S(1)} %get-tuple-element.53), channel_id=1, source_target_pairs={{0,6},{1,25},{2,0},{3,27},{4,2},{5,29},{6,4},{7,31},{8,14},{9,1},{... | collective-permute-start | bytes 3293192 | tf_op jit(solution)/shard_map/ppermute | solution.py:447
  99.3 18.0 %collective-permute-start.17 = (f32[2144,128]{1,0:T(8,128)S(1)}, f32[2144,128]{1,0:T(8,128)S(1)}, u32[]{:S(2)}, u32[]{:S(2)}) collective-permute-start(f32[2144,128]{1,0:T(8,128)S(1)} %get-tuple-element.65), channel_id=1, source_target_pairs={{0,6},{1,25},{2,0},{3,27},{4,2},{5,29},{6,4},{7,31},{8,14},{9,1},{... | collective-permute-start | bytes 3293192 | tf_op jit(solution)/shard_map/ppermute | solution.py:447
  101.0 23.1 %collective-permute-start.16 = (f32[2144,128]{1,0:T(8,128)S(1)}, f32[2144,128]{1,0:T(8,128)S(1)}, u32[]{:S(2)}, u32[]{:S(2)}) collective-permute-start(f32[2144,128]{1,0:T(8,128)S(1)} %get-tuple-element.63), channel_id=1, source_target_pairs={{0,2},{1,9},{2,4},{3,11},{4,6},{5,13},{6,0},{7,15},{8,10},{9,17},{... | collective-permute-start | bytes 3293192 | tf_op jit(solution)/shard_map/ppermute | solution.py:447
  117.7 8.8 %collective-permute-start.18 = (f32[2144,128]{1,0:T(8,128)S(1)}, f32[2144,128]{1,0:T(8,128)S(1)}, u32[]{:S(2)}, u32[]{:S(2)}) collective-permute-start(f32[2144,128]{1,0:T(8,128)S(1)} %other_total.1), channel_id=1, source_target_pairs={{0,1},{1,0},{2,3},{3,2},{4,5},{5,4},{6,7},{7,6},{8,9},{9,8},{10,11... | collective-permute-start | bytes 3293192 | tf_op jit(solution)/shard_map/ppermute | solution.py:456
  127.3 10.7 %collective-permute-start.19 = (f32[536,128]{1,0:T(8,128)S(1)}, f32[536,128]{1,0:T(8,128)S(1)}, u32[]{:S(2)}, u32[]{:S(2)}) collective-permute-start(f32[536,128]{1,0:T(8,128)S(1)} %get-tuple-element.67), channel_id=1, source_target_pairs={{0,32},{32,64},{64,96},{96,0},{1,33},{33,65},{65,97},{97,1},{2,34}... | collective-permute-start | bytes 823304 | tf_op jit(solution)/shard_map/ppermute | solution.py:460
  129.4 15.2 %collective-permute-start.20 = (f32[536,128]{1,0:T(8,128)S(1)}, f32[536,128]{1,0:T(8,128)S(1)}, u32[]{:S(2)}, u32[]{:S(2)}) collective-permute-start(f32[536,128]{1,0:T(8,128)S(1)} %get-tuple-element.68), channel_id=1, source_target_pairs={{0,64},{32,96},{64,0},{96,32},{1,65},{33,97},{65,1},{97,33},{2,66}... | collective-permute-start | bytes 823304 | tf_op jit(solution)/shard_map/ppermute | solution.py:460
  132.5 12.2 %collective-permute-start.21 = (f32[536,128]{1,0:T(8,128)S(1)}, f32[536,128]{1,0:T(8,128)S(1)}, u32[]{:S(2)}, u32[]{:S(2)}) collective-permute-start(f32[536,128]{1,0:T(8,128)S(1)} %get-tuple-element.69), channel_id=1, source_target_pairs={{0,96},{32,0},{64,32},{96,64},{1,97},{33,1},{65,33},{97,65},{2,98}... | collective-permute-start | bytes 823304 | tf_op jit(solution)/shard_map/ppermute | solution.py:460
  146.4 14.3 %collective-permute-start.23 = (f32[536,128]{1,0:T(8,128)S(1)}, f32[536,128]{1,0:T(8,128)S(1)}, u32[]{:S(2)}, u32[]{:S(2)}) collective-permute-start(f32[536,128]{1,0:T(8,128)S(1)} %add_add_fusion.refs_0_), channel_id=1, source_target_pairs={{0,64},{32,96},{64,0},{96,32},{1,65},{33,97},{65,1},{97,33},{2,66}... | collective-permute-start | bytes 823304 | tf_op jit(solution)/shard_map/ppermute | solution.py:461
  148.6 12.1 %collective-permute-start.24 = (f32[536,128]{1,0:T(8,128)S(1)}, f32[536,128]{1,0:T(8,128)S(1)}, u32[]{:S(2)}, u32[]{:S(2)}) collective-permute-start(f32[536,128]{1,0:T(8,128)S(1)} %add_add_fusion.refs_0_), channel_id=1, source_target_pairs={{0,96},{32,0},{64,32},{96,64},{1,97},{33,1},{65,33},{97,65},{2,98}... | collective-permute-start | bytes 823304 | tf_op jit(solution)/shard_map/ppermute | solution.py:461
  (7 other events, 62.7 us)

commit v5 on v4

--- a/solution.py
+++ b/solution.py
@@ -248,12 +248,11 @@
     lax.fori_loop(0, steps, step, 0)
 
 
-def gram_body(group, started, lists, sizes, tallies, *refs):
-    blocks = refs[:GROUPS]
+def gram_body(group, members, counted, quartered, started, pos, lists, sizes, tallies, *refs):
+    blocks, refs = refs[: len(members)], refs[len(members) :]
     first, second = started
-    starts = (refs[GROUPS : GROUPS + first], refs[GROUPS + first : GROUPS + first + second])
-    outs = refs[GROUPS + first + second :][:2]
-    acc, acc_s, acc_q = refs[GROUPS + first + second + 2 :]
+    starts = (refs[:first], refs[first : first + second])
+    outs, (acc, acc_s, acc_q) = refs[first + second : -3], refs[-3:]
 
     def add_starts(value, u, rows):
         for start in starts[u]:
@@ -275,44 +274,67 @@
         return 0
 
     lax.fori_loop(0, CHIP_CELLS, clear_sums, 0)
-    for g in range(GROUPS):
-        add_blocks(group * GROUPS + g, lists, sizes, blocks[g], acc, acc_s, acc_q)
-
-    def copy_out(i, _):
-        rows = pl.ds(pl.multiple_of(i * ROWS, ROWS), ROWS)
-        for u in range(2):
-            outs[u][rows, :] = acc[pl.ds(pl.multiple_of(u * PIECE + i * ROWS, 8), ROWS), :]
-        return 0
-
-    lax.fori_loop(0, CELL_DEV, copy_out, 0)
+    for g, member in zip(members, blocks):
+        add_blocks(group * GROUPS + g, lists, sizes, member, acc, acc_s, acc_q)
     for u in range(2):
+        base = u * PIECE
         for k, source in enumerate((acc_s, acc_q)):
             total = source[pl.ds(u * CELL_DEV * 8, CELL_DEV, stride=8), :]
             for j in range(1, 8):
                 total = total + source[pl.ds(u * CELL_DEV * 8 + j, CELL_DEV, stride=8), :]
-            rows = pl.ds(PACKED + k * CELL_DEV, CELL_DEV)
-            outs[u][rows, :] = add_starts(total, u, rows)
+            rows = PACKED + k * CELL_DEV
+            acc[pl.ds(base + rows, CELL_DEV), :] = add_starts(total, u, pl.ds(rows, CELL_DEV))
         for j in range(CELL_DEV):
-            count = jnp.full((1, D), tallies[group * CHIP_CELLS + u * CELL_DEV + j].astype(F32), F32)
-            rows = pl.ds(PACKED + 2 * CELL_DEV + j, 1)
-            outs[u][rows, :] = add_starts(count, u, rows)
-
-
-def gram(group, lists, sizes, tallies, blocks, first=(), second=()):
+            count = jnp.zeros((1, D), F32)
+            if counted:
+                count = jnp.full((1, D), tallies[group * CHIP_CELLS + u * CELL_DEV + j].astype(F32), F32)
+            rows = PACKED + 2 * CELL_DEV + j
+            acc[pl.ds(base + rows, 1), :] = add_starts(count, u, pl.ds(rows, 1))
+    if not quartered:
+
+        def copy_out(i, _):
+            for u in range(2):
+                outs[u][pl.ds(pl.multiple_of(i * 32, 32), 32), :] = acc[
+                    pl.ds(pl.multiple_of(u * PIECE + i * 32, 32), 32), :
+                ]
+            return 0
+
+        lax.fori_loop(0, PIECE // 32, copy_out, 0)
+        return
+    for dz in range(NZ):
+        q = lax.rem(pos[3] + dz, NZ)
+        for u in range(2):
+
+            def copy_quarter(i, _, dz=dz, q=q, u=u):
+                outs[dz][pl.ds(pl.multiple_of(u * QPIECE + i * ROWS, 8), ROWS), :] = acc[
+                    pl.ds(pl.multiple_of(u * PIECE + q * QPACKED + i * ROWS, 8), ROWS), :
+                ]
+                return 0
+
+            lax.fori_loop(0, QCELL, copy_quarter, 0)
+            for k in range(3):
+                outs[dz][pl.ds(u * QPIECE + QPACKED + k * QCELL, QCELL), :] = acc[
+                    pl.ds(pl.multiple_of(u * PIECE + PACKED + k * CELL_DEV + q * QCELL, QCELL), QCELL), :
+                ]
+
+
+def gram(group, pos, lists, sizes, tallies, blocks, first=(), second=(), members=(0, 1, 2, 3), counted=True, quartered=False):
     def body(*refs):
-        gram_body(group, (len(first), len(second)), *refs)
+        gram_body(group, members, counted, quartered, (len(first), len(second)), *refs)
 
     half = jax.ShapeDtypeStruct((PIECE, D), F32)
+    quarter = jax.ShapeDtypeStruct((2 * QPIECE, D), F32)
+    outs = [quarter] * NZ if quartered else [half] * 2
     return pl.pallas_call(
         body,
-        out_shape=[half, half],
-        in_specs=[SMEM_SPEC] * 3 + [VMEM_SPEC] * (GROUPS + len(first) + len(second)),
-        out_specs=[VMEM_SPEC] * 2,
+        out_shape=outs,
+        in_specs=[SMEM_SPEC] * 4 + [VMEM_SPEC] * (len(members) + len(first) + len(second)),
+        out_specs=[VMEM_SPEC] * len(outs),
         scratch_shapes=[pltpu.VMEM((NC * PIECE, D), F32)] + [pltpu.VMEM(((CHIP_CELLS + 1) * 8, D), F32)] * 2,
         compiler_params=pltpu.CompilerParams(vmem_limit_bytes=SMALL_VMEM),
         cost_estimate=pl.CostEstimate(flops=10**9, bytes_accessed=10**7, transcendentals=0),
-        name=f"gram{group}",
-    )(lists, sizes, tallies, *blocks, *first, *second)
+        name=f"gram{group}" + ("" if counted else "b"),
+    )(pos, lists, sizes, tallies, *(blocks[g] for g in members), *first, *second)
 
 
 def total_body(*refs):
@@ -338,9 +360,9 @@
     )(*parts)
 
 
-def join_body(pos, *refs):
-    outs = refs[-NZ:]
-    parts = refs[:-NZ]
+def join_body(extra, pos, *refs):
+    outs, parts = refs[-NZ:], refs[:-NZ]
+    parts, extras = parts[: len(parts) - extra], parts[len(parts) - extra :]
     z = pos[3]
 
     def total(rows):
@@ -352,28 +374,38 @@
     for dz in range(NZ):
         q = lax.rem(z + dz, NZ)
 
-        def step(i, _, dz=dz, q=q):
-            outs[dz][pl.ds(pl.multiple_of(i * ROWS, ROWS), ROWS), :] = total(
-                pl.ds(pl.multiple_of(q * QPACKED + i * ROWS, ROWS), ROWS)
+        def put(rows, value, dz=dz):
+            for more in extras if dz == 0 else ():
+                value = value + more[rows, :]
+            outs[dz][rows, :] = value
+
+        def step(i, _, q=q, put=put):
+            put(
+                pl.ds(pl.multiple_of(i * ROWS, ROWS), ROWS),
+                total(pl.ds(pl.multiple_of(q * QPACKED + i * ROWS, ROWS), ROWS)),
             )
             return 0
 
         lax.fori_loop(0, QCELL, step, 0)
         for k in range(3):
-            outs[dz][pl.ds(QPACKED + k * QCELL, QCELL), :] = total(
-                pl.ds(pl.multiple_of(PACKED + k * CELL_DEV + q * QCELL, QCELL), QCELL)
+            put(
+                pl.ds(QPACKED + k * QCELL, QCELL),
+                total(pl.ds(pl.multiple_of(PACKED + k * CELL_DEV + q * QCELL, QCELL), QCELL)),
             )
 
 
-def join(pos, parts):
+def join(pos, parts, extras=()):
+    def body(*refs):
+        join_body(len(extras), *refs)
+
     return pl.pallas_call(
-        join_body,
+        body,
         out_shape=[jax.ShapeDtypeStruct((QPIECE, D), F32)] * NZ,
-        in_specs=[SMEM_SPEC] + [VMEM_SPEC] * len(parts),
+        in_specs=[SMEM_SPEC] + [VMEM_SPEC] * (len(parts) + len(extras)),
         out_specs=[VMEM_SPEC] * NZ,
         compiler_params=pltpu.CompilerParams(vmem_limit_bytes=SMALL_VMEM),
         name="join",
-    )(pos, *parts)
+    )(pos, *parts, *extras)
 
 
 def finish_body(pos, *refs):
@@ -446,13 +478,17 @@
     def step(rel, piece):
         return lax.ppermute(piece, "cell", across(rel))
 
-    fore, back = gram(0, lists, sizes, tallies, got[0])
+    def grams(group, *rest, **options):
+        return gram(group, pos, lists, sizes, tallies, got[group], *rest, **options)
+
+    fore, back = grams(0)
     fore, back = step(1, fore), step(3, back)
-    left, right = gram(2, lists, sizes, tallies, got[2])
+    left, right = grams(2)
     other1, own3 = step(1, left), step(3, right)
-    left, right = gram(3, lists, sizes, tallies, got[3], (fore,), (back,))
+    left, right = grams(3, (fore,), (back,), members=(0, 1))
+    left, right = grams(3, (left,), (right,), members=(2, 3), counted=False)
     own1, other3 = step(1, left), step(3, right)
-    own, other = gram(1, lists, sizes, tallies, got[1], (own3,), (other1,))
+    own, other = grams(1, (own3,), (other1,))
     swapped = lax.ppermute(other_total([other, other3]), "cell", SWAP)
     quarters = join(pos, [own, own1, swapped])
     mine = quarters[0]

time: 165 us -> 164 us (level)
  waiting for transfers between devices: 56.2 us -> 52.5 us
  Pallas kernels: 54.9 us -> 57.7 us
    ppermute x6, waiting for transfers between devices: 9.67 us -> 4.6 us  [step(): return lax.ppermute(piece, 'cell', across(rel))]
    ppermute x1, starting transfers between devices: 6.4 us -> 3.15 us  [local(): swapped = lax.ppermute(other_total([other, other3]), 'cell', SWAP)]
    ppermute x6, starting transfers between devices: 4.91 us -> 7.89 us  [step(): return lax.ppermute(piece, 'cell', across(rel))]
    pallas_call x5 -> x6, Pallas kernels: 30.6 us -> 33.3 us  [the longest x5 32.5 us: gram(): pl.pallas_call(body, out_shape=outs, in_specs=[SMEM_SPEC] * 4 + [VMEM_SPE...]
    ppermute x12, waiting for transfers between devices: 20.6 us -> 22.9 us  [local(): lax.ppermute(run, 'cell', along(d))]
  transfers between devices with their start and end apart: 25 -> 25, of which waited for: 13 -> 13; matrix products, arithmetic and copies ran while one was open for 0% -> 0% of each run, Pallas kernels for 28% -> 30%
where the time goes in v5:
time: 164 us; the launch traced here: 162 us
  Pallas kernels  57.7 us (35%)
  waiting for transfers between devices  52.5 us (32%)
  starting transfers between devices  44.8 us (27%)
  local copies, waits for them, and re-layouts  5.58 us (3%)
    pallas_call x5, Pallas kernels, gram(): pl.pallas_call(body, out_shape=outs, in_specs=[SMEM_SPEC] * 4 + [VMEM_SPE...  32.5 us
    ppermute x12, starting transfers between devices, local(): lax.ppermute(run, 'cell', along(d))  24.5 us
    ppermute x12, waiting for transfers between devices, local(): lax.ppermute(run, 'cell', along(d))  22.9 us
    pallas_call x4, Pallas kernels, gather_runs(): pl.pallas_call(body, out_shape=[jax.ShapeDtypeStruct((rows, D), vectors.d...  13 us
    ppermute x3, waiting for transfers between devices, local(): lax.ppermute(mine, 'dp', dp_perm(dz))  11.9 us
    ppermute x3, waiting for transfers between devices, local(): mine = mine + lax.ppermute(quarters[dz], 'dp', dp_perm(dz))  10.8 us
    ppermute x6, starting transfers between devices, step(): return lax.ppermute(piece, 'cell', across(rel))  7.89 us
    pallas_call x1, Pallas kernels, make_lists(): pl.pallas_call(lists_body, out_shape=[jax.ShapeDtypeStruct((LIST,), I32),...  7.49 us
  transfers between devices with their start and end apart: 25, of which 13 were waited for; matrix products, arithmetic and copies ran while one was open for 0% of the time, Pallas kernels for 30%

profile of v5, /device:TPU:1, one launch (start us, length us, event | category | flops | bytes accessed | tf_op | source)
XLA Modules:
  0.0 162.2 jit_solution(14658138192721759663)
XLA Ops:
  1.4 4.3 %gather0.1 = (bf16[3088,128]{1,0:T(8,128)(2,1)}, bf16[3088,128]{1,0:T(8,128)(2,1)}, bf16[3088,128]{1,0:T(8,128)(2,1)}) custom-call(s32[4]{0:T(128)} %pad_add_fusion.refs_0_.pos, s32[32]{0:T(128)} %bitcast.11, bf16[24576,128]{1,0:T(8,128)(2,1)} %bitcast.7, s32[1,384]{1,0:T(1,128)} %refs_3_.1, s32[1,32]{1,0:T(1,128)} %bitcast.12), custom_call_target="tpu_custom_call" | custom-call | tf_op jit(solution)/shard_map/gather0/pallas_call | solution.py:126
  11.0 3.3 %gather1.1 = (bf16[3072,128]{1,0:T(8,128)(2,1)}, bf16[3072,128]{1,0:T(8,128)(2,1)}, bf16[3072,128]{1,0:T(8,128)(2,1)}) custom-call(s32[4]{0:T(128)S(1)} %copy-done.3, s32[32]{0:T(128)S(1)} %bitcast.13, bf16[24576,128]{1,0:T(8,128)(2,1)S(1)} %bitcast.8), custom_call_target="tpu_custom_call" | custom-call | tf_op jit(solution)/shard_map/gather1/pallas_call | solution.py:126
  19.3 10.2 %collective-permute-start.5 = (bf16[3072,128]{1,0:T(8,128)(2,1)}, bf16[3072,128]{1,0:T(8,128)(2,1)}, u32[]{:S(2)}, u32[]{:S(2)}) collective-permute-start(bf16[3072,128]{1,0:T(8,128)(2,1)} %get-tuple-element.47), channel_id=1, source_target_pairs={{0,16},{1,5},{2,18},{3,7},{4,20},{5,1},{6,22},{7,3},{8,24},{9,13},... | collective-permute-start | bytes 2359304 | tf_op jit(solution)/shard_map/ppermute | solution.py:476
  29.5 7.5 %lists.1 = (s32[896]{0:T(1024)S(1)}, s32[32]{0:T(128)S(1)}, s32[256]{0:T(256)S(1)}) custom-call(s32[4]{0:T(128)S(1)} %copy-done.3, s32[384]{0:T(512)S(1)} %reduce.own_cells, s32[32]{0:T(128)S(1)} %bitcast.14, bf16[3088,128]{1,0:T(8,128)(2,1)S(1)} %collective-permute-done.refs_0_.refs_5_, bf16[3088,128]{1,0:T(8,128)(2,1)S(1)} %collective-permute-done.1.refs_1_.refs_6_, ...), custom_call_target="tpu_custom_call" | custom-call | tf_op jit(solution)/shard_map/lists/pallas_call | solution.py:195
  37.0 2.8 %copy-done.1 = bf16[1,384,64,128]{3,2,1,0:T(8,128)(2,1)S(1)} copy-done((bf16[1,384,64,128]{3,2,1,0:T(8,128)(2,1)S(1)}, bf16[1,384,64,128]{3,2,1,0:T(8,128)(2,1)}, u32[]{:S(2)}) %copy-start.1) | copy-done | bytes 6291480
  39.8 2.7 %gather2.1 = (bf16[3072,128]{1,0:T(8,128)(2,1)S(1)}, bf16[3072,128]{1,0:T(8,128)(2,1)S(1)}, bf16[3072,128]{1,0:T(8,128)(2,1)S(1)}, bf16[3072,128]{1,0:T(8,128)(2,1)S(1)}, bf16[3072,128]{1,0:T(8,128)(2,1)S(1)}) custom-call(s32[4]{0:T(128)S(1)} %copy-done.3, s32[32]{0:T(128)S(1)} %bitcast.15, bf16[24576,128]{1,0:T(8,128)(2,1)S(1)} %bitcast.9), custom_call_target="tpu_custom_call" | custom-call | tf_op jit(solution)/shard_map/gather2/pallas_call | solution.py:126
  42.6 2.7 %collective-permute-start.7 = (bf16[3072,128]{1,0:T(8,128)(2,1)S(1)}, bf16[3072,128]{1,0:T(8,128)(2,1)S(1)}, u32[]{:S(2)}, u32[]{:S(2)}) collective-permute-start(bf16[3072,128]{1,0:T(8,128)(2,1)S(1)} %get-tuple-element.53), channel_id=1, source_target_pairs={{0,24},{1,7},{2,26},{3,1},{4,28},{5,3},{6,30},{7,5},{8,0},{9,15},{... | collective-permute-start | bytes 2359304 | tf_op jit(solution)/shard_map/ppermute | solution.py:476
  45.3 7.9 %gram0.1 = (f32[2144,128]{1,0:T(8,128)S(1)}, f32[2144,128]{1,0:T(8,128)S(1)}) custom-call(s32[4]{0:T(128)S(1)} %copy-done.3, s32[896]{0:T(1024)S(1)} %get-tuple-element.41.refs_1_, s32[32]{0:T(128)S(1)} %get-tuple-element.42.refs_2_, s32[256]{0:T(256)S(1)} %get-tuple-element.43.refs_3_, bf16[3072,128]{1,0:T(8,128)(2,1)S(1)} %get-tuple-element.62.refs_4_, ...), custom_call_target="tpu_custom_call" | custom-call | flops 1000000000 | bytes 10000000 | tf_op jit(solution)/shard_map/gram0/pallas_call | solution.py:328
  56.0 2.8 %copy-done.2 = bf16[1,384,64,128]{3,2,1,0:T(8,128)(2,1)S(1)} copy-done((bf16[1,384,64,128]{3,2,1,0:T(8,128)(2,1)S(1)}, bf16[1,384,64,128]{3,2,1,0:T(8,128)(2,1)}, u32[]{:S(2)}) %copy-start.2) | copy-done | bytes 6291480
  58.8 2.7 %gather3.1 = (bf16[3072,128]{1,0:T(8,128)(2,1)S(1)}, bf16[3072,128]{1,0:T(8,128)(2,1)S(1)}, bf16[3072,128]{1,0:T(8,128)(2,1)S(1)}, bf16[3072,128]{1,0:T(8,128)(2,1)S(1)}, bf16[3072,128]{1,0:T(8,128)(2,1)S(1)}) custom-call(s32[4]{0:T(128)S(1)} %copy-done.3, s32[32]{0:T(128)S(1)} %bitcast.16, bf16[24576,128]{1,0:T(8,128)(2,1)S(1)} %bitcast.10), custom_call_target="tpu_custom_call" | custom-call | tf_op jit(solution)/shard_map/gather3/pallas_call | solution.py:126
  63.7 3.6 %collective-permute-start.11 = (bf16[3072,128]{1,0:T(8,128)(2,1)S(1)}, bf16[3072,128]{1,0:T(8,128)(2,1)S(1)}, u32[]{:S(2)}, u32[]{:S(2)}) collective-permute-start(bf16[3072,128]{1,0:T(8,128)(2,1)S(1)} %get-tuple-element.58), channel_id=1, source_target_pairs={{0,24},{1,7},{2,26},{3,1},{4,28},{5,3},{6,30},{7,5},{8,0},{9,15},{... | collective-permute-start | bytes 2359304 | tf_op jit(solution)/shard_map/ppermute | solution.py:476
  67.3 6.3 %gram2.1 = (f32[2144,128]{1,0:T(8,128)S(1)}, f32[2144,128]{1,0:T(8,128)S(1)}) custom-call(s32[4]{0:T(128)S(1)} %copy-done.3, s32[896]{0:T(1024)S(1)} %get-tuple-element.41.refs_1_, s32[32]{0:T(128)S(1)} %get-tuple-element.42.refs_2_, s32[256]{0:T(256)S(1)} %get-tuple-element.43.refs_3_, bf16[3072,128]{1,0:T(8,128)(2,1)S(1)} %get-tuple-element.51.refs_4_, ...), custom_call_target="tpu_custom_call" | custom-call | flops 1000000000 | bytes 10000000 | tf_op jit(solution)/shard_map/gram2/pallas_call | solution.py:328
  73.6 18.3 %collective-permute-done.13.refs_5_ = bf16[3072,128]{1,0:T(8,128)(2,1)S(1)} collective-permute-done((bf16[3072,128]{1,0:T(8,128)(2,1)S(1)}, bf16[3072,128]{1,0:T(8,128)(2,1)S(1)}, u32[]{:S(2)}, u32[]{:S(2)}) %collective-permute-start.13) | collective-permute-done | bytes 786464 | tf_op jit(solution)/shard_map/ppermute | solution.py:476
  94.6 2.9 %gram3.1 = (f32[2144,128]{1,0:T(8,128)S(1)}, f32[2144,128]{1,0:T(8,128)S(1)}) custom-call(s32[4]{0:T(128)S(1)} %copy-done.3, s32[896]{0:T(1024)S(1)} %get-tuple-element.41.refs_1_, s32[32]{0:T(128)S(1)} %get-tuple-element.42.refs_2_, s32[256]{0:T(256)S(1)} %get-tuple-element.43.refs_3_, bf16[3072,128]{1,0:T(8,128)(2,1)S(1)} %get-tuple-element.60.refs_4_, ...), custom_call_target="tpu_custom_call" | custom-call | flops 1000000000 | bytes 10000000 | tf_op jit(solution)/shard_map/gram3/pallas_call | solution.py:328
  97.5 4.9 %gram3b.1 = (f32[2144,128]{1,0:T(8,128)S(1)}, f32[2144,128]{1,0:T(8,128)S(1)}) custom-call(s32[4]{0:T(128)S(1)} %copy-done.3, s32[896]{0:T(1024)S(1)} %get-tuple-element.41.refs_1_, s32[32]{0:T(128)S(1)} %get-tuple-element.42.refs_2_, s32[256]{0:T(256)S(1)} %get-tuple-element.43.refs_3_, bf16[3072,128]{1,0:T(8,128)(2,1)S(1)} %collective-permute-done.11.refs_4_, ...), custom_call_target="tpu_custom_call" | custom-call | flops 1000000000 | bytes 10000000 | tf_op jit(solution)/shard_map/gram3b/pallas_call | solution.py:328
  108.2 10.5 %gram1.1 = (f32[2144,128]{1,0:T(8,128)S(1)}, f32[2144,128]{1,0:T(8,128)S(1)}) custom-call(s32[4]{0:T(128)S(1)} %copy-done.3, s32[896]{0:T(1024)S(1)} %get-tuple-element.41.refs_1_, s32[32]{0:T(128)S(1)} %get-tuple-element.42.refs_2_, s32[256]{0:T(256)S(1)} %get-tuple-element.43.refs_3_, bf16[3072,128]{1,0:T(8,128)(2,1)S(1)} %get-tuple-element.49.refs_4_, ...), custom_call_target="tpu_custom_call" | custom-call | flops 1000000000 | bytes 10000000 | tf_op jit(solution)/shard_map/gram1/pallas_call | solution.py:328
  120.3 3.1 %collective-permute-start.18 = (f32[2144,128]{1,0:T(8,128)S(1)}, f32[2144,128]{1,0:T(8,128)S(1)}, u32[]{:S(2)}, u32[]{:S(2)}) collective-permute-start(f32[2144,128]{1,0:T(8,128)S(1)} %other_total.1), channel_id=1, source_target_pairs={{0,1},{1,0},{2,3},{3,2},{4,5},{5,4},{6,7},{7,6},{8,9},{9,8},{10,11... | collective-permute-start | bytes 3293192 | tf_op jit(solution)/shard_map/ppermute | solution.py:492
  127.0 3.1 %collective-permute-start.20 = (f32[536,128]{1,0:T(8,128)S(1)}, f32[536,128]{1,0:T(8,128)S(1)}, u32[]{:S(2)}, u32[]{:S(2)}) collective-permute-start(f32[536,128]{1,0:T(8,128)S(1)} %get-tuple-element.72), channel_id=1, source_target_pairs={{0,64},{32,96},{64,0},{96,32},{1,65},{33,97},{65,1},{97,33},{2,66}... | collective-permute-start | bytes 823304 | tf_op jit(solution)/shard_map/ppermute | solution.py:496
  131.5 4.2 %collective-permute-done.19 = f32[536,128]{1,0:T(8,128)S(1)} collective-permute-done((f32[536,128]{1,0:T(8,128)S(1)}, f32[536,128]{1,0:T(8,128)S(1)}, u32[]{:S(2)}, u32[]{:S(2)}) %collective-permute-start.19) | collective-permute-done | bytes 274464 | tf_op jit(solution)/shard_map/ppermute | solution.py:496
  135.8 6.5 %collective-permute-done.20 = f32[536,128]{1,0:T(8,128)S(1)} collective-permute-done((f32[536,128]{1,0:T(8,128)S(1)}, f32[536,128]{1,0:T(8,128)S(1)}, u32[]{:S(2)}, u32[]{:S(2)}) %collective-permute-start.20) | collective-permute-done | bytes 274464 | tf_op jit(solution)/shard_map/ppermute | solution.py:496
  143.9 2.8 %collective-permute-start.23 = (f32[536,128]{1,0:T(8,128)S(1)}, f32[536,128]{1,0:T(8,128)S(1)}, u32[]{:S(2)}, u32[]{:S(2)}) collective-permute-start(f32[536,128]{1,0:T(8,128)S(1)} %add_add_fusion.refs_0_), channel_id=1, source_target_pairs={{0,64},{32,96},{64,0},{96,32},{1,65},{33,97},{65,1},{97,33},{2,66}... | collective-permute-start | bytes 823304 | tf_op jit(solution)/shard_map/ppermute | solution.py:497
  146.8 4.4 %collective-permute-done.22.refs_1_ = f32[536,128]{1,0:T(8,128)S(1)} collective-permute-done((f32[536,128]{1,0:T(8,128)S(1)}, f32[536,128]{1,0:T(8,128)S(1)}, u32[]{:S(2)}, u32[]{:S(2)}) %collective-permute-start.22) | collective-permute-done | bytes 274464 | tf_op jit(solution)/shard_map/ppermute | solution.py:497
  151.2 7.5 %collective-permute-done.23.refs_2_ = f32[536,128]{1,0:T(8,128)S(1)} collective-permute-done((f32[536,128]{1,0:T(8,128)S(1)}, f32[536,128]{1,0:T(8,128)S(1)}, u32[]{:S(2)}, u32[]{:S(2)}) %collective-permute-start.23) | collective-permute-done | bytes 274464 | tf_op jit(solution)/shard_map/ppermute | solution.py:497
  158.7 3.5 %finish.1 = (f32[32,128]{1,0:T(8,128)}, f32[32,128,128]{2,1,0:T(8,128)}) custom-call(s32[4]{0:T(128)S(1)} %copy-done.3, f32[536,128]{1,0:T(8,128)S(1)} %add_add_fusion.refs_0_, f32[536,128]{1,0:T(8,128)S(1)} %collective-permute-done.22.refs_1_, f32[536,128]{1,0:T(8,128)S(1)} %collective-permute-done.23.refs_2_, f32[536,128]{1,0:T(8,128)S(1)} %collective-permute-done.24.refs_3_), custom_call_target="tpu_custom_call" | custom-call | tf_op jit(solution)/shard_map/finish/pallas_call | solution.py:442
  (54 shorter events, 32.8 us)
Async XLA Ops:
  5.7 13.6 %collective-permute-start = (bf16[3088,128]{1,0:T(8,128)(2,1)}, bf16[3088,128]{1,0:T(8,128)(2,1)S(1)}, u32[]{:S(2)}, u32[]{:S(2)}) collective-permute-start(bf16[3088,128]{1,0:T(8,128)(2,1)} %get-tuple-element.38), channel_id=1, source_target_pairs={{0,8},{1,3},{2,10},{3,5},{4,12},{5,7},{6,14},{7,1},{8,16},{9,11},{... | collective-permute-start | bytes 2371592 | tf_op jit(solution)/shard_map/ppermute | solution.py:476
  7.9 21.6 %collective-permute-start.1 = (bf16[3088,128]{1,0:T(8,128)(2,1)}, bf16[3088,128]{1,0:T(8,128)(2,1)S(1)}, u32[]{:S(2)}, u32[]{:S(2)}) collective-permute-start(bf16[3088,128]{1,0:T(8,128)(2,1)} %get-tuple-element.39), channel_id=1, source_target_pairs={{0,24},{1,7},{2,26},{3,1},{4,28},{5,3},{6,30},{7,5},{8,0},{9,15},{... | collective-permute-start | bytes 2371592 | tf_op jit(solution)/shard_map/ppermute | solution.py:476
  9.4 20.1 %collective-permute-start.2 = (bf16[3088,128]{1,0:T(8,128)(2,1)}, bf16[3088,128]{1,0:T(8,128)(2,1)}, u32[]{:S(2)}, u32[]{:S(2)}) collective-permute-start(bf16[3088,128]{1,0:T(8,128)(2,1)} %get-tuple-element.40), channel_id=1, source_target_pairs={{0,16},{1,5},{2,18},{3,7},{4,20},{5,1},{6,22},{7,3},{8,24},{9,13},... | collective-permute-start | bytes 2371592 | tf_op jit(solution)/shard_map/ppermute | solution.py:476
  14.2 31.0 %collective-permute-start.3 = (bf16[3072,128]{1,0:T(8,128)(2,1)}, bf16[3072,128]{1,0:T(8,128)(2,1)S(1)}, u32[]{:S(2)}, u32[]{:S(2)}) collective-permute-start(bf16[3072,128]{1,0:T(8,128)(2,1)} %get-tuple-element.45), channel_id=1, source_target_pairs={{0,8},{1,3},{2,10},{3,5},{4,12},{5,7},{6,14},{7,1},{8,16},{9,11},{... | collective-permute-start | bytes 2359304 | tf_op jit(solution)/shard_map/ppermute | solution.py:476
  14.7 38.5 %collective-permute-start.4 = (bf16[3072,128]{1,0:T(8,128)(2,1)}, bf16[3072,128]{1,0:T(8,128)(2,1)}, u32[]{:S(2)}, u32[]{:S(2)}) collective-permute-start(bf16[3072,128]{1,0:T(8,128)(2,1)} %get-tuple-element.46), channel_id=1, source_target_pairs={{0,24},{1,7},{2,26},{3,1},{4,28},{5,3},{6,30},{7,5},{8,0},{9,15},{... | collective-permute-start | bytes 2359304 | tf_op jit(solution)/shard_map/ppermute | solution.py:476
  19.3 35.6 %collective-permute-start.5 = (bf16[3072,128]{1,0:T(8,128)(2,1)}, bf16[3072,128]{1,0:T(8,128)(2,1)}, u32[]{:S(2)}, u32[]{:S(2)}) collective-permute-start(bf16[3072,128]{1,0:T(8,128)(2,1)} %get-tuple-element.47), channel_id=1, source_target_pairs={{0,16},{1,5},{2,18},{3,7},{4,20},{5,1},{6,22},{7,3},{8,24},{9,13},... | collective-permute-start | bytes 2359304 | tf_op jit(solution)/shard_map/ppermute | solution.py:476
  42.5 20.1 %collective-permute-start.6 = (bf16[3072,128]{1,0:T(8,128)(2,1)S(1)}, bf16[3072,128]{1,0:T(8,128)(2,1)S(1)}, u32[]{:S(2)}, u32[]{:S(2)}) collective-permute-start(bf16[3072,128]{1,0:T(8,128)(2,1)S(1)} %get-tuple-element.52), channel_id=1, source_target_pairs={{0,8},{1,3},{2,10},{3,5},{4,12},{5,7},{6,14},{7,1},{8,16},{9,11},{... | collective-permute-start | bytes 2359304 | tf_op jit(solution)/shard_map/ppermute | solution.py:476
  42.6 21.1 %collective-permute-start.7 = (bf16[3072,128]{1,0:T(8,128)(2,1)S(1)}, bf16[3072,128]{1,0:T(8,128)(2,1)S(1)}, u32[]{:S(2)}, u32[]{:S(2)}) collective-permute-start(bf16[3072,128]{1,0:T(8,128)(2,1)S(1)} %get-tuple-element.53), channel_id=1, source_target_pairs={{0,24},{1,7},{2,26},{3,1},{4,28},{5,3},{6,30},{7,5},{8,0},{9,15},{... | collective-permute-start | bytes 2359304 | tf_op jit(solution)/shard_map/ppermute | solution.py:476
  45.3 22.0 %collective-permute-start.8 = (bf16[3072,128]{1,0:T(8,128)(2,1)S(1)}, bf16[3072,128]{1,0:T(8,128)(2,1)S(1)}, u32[]{:S(2)}, u32[]{:S(2)}) collective-permute-start(bf16[3072,128]{1,0:T(8,128)(2,1)S(1)} %get-tuple-element.54), channel_id=1, source_target_pairs={{0,16},{1,5},{2,18},{3,7},{4,20},{5,1},{6,22},{7,3},{8,24},{9,13},... | collective-permute-start | bytes 2359304 | tf_op jit(solution)/shard_map/ppermute | solution.py:476
  53.2 40.5 %collective-permute-start.14 = (f32[2144,128]{1,0:T(8,128)S(1)}, f32[2144,128]{1,0:T(8,128)S(1)}, u32[]{:S(2)}, u32[]{:S(2)}) collective-permute-start(f32[2144,128]{1,0:T(8,128)S(1)} %get-tuple-element.63), channel_id=1, source_target_pairs={{0,2},{1,9},{2,4},{3,11},{4,6},{5,13},{6,0},{7,15},{8,10},{9,17},{... | collective-permute-start | bytes 3293192 | tf_op jit(solution)/shard_map/ppermute | solution.py:479
  54.9 39.7 %collective-permute-start.15 = (f32[2144,128]{1,0:T(8,128)S(1)}, f32[2144,128]{1,0:T(8,128)S(1)}, u32[]{:S(2)}, u32[]{:S(2)}) collective-permute-start(f32[2144,128]{1,0:T(8,128)S(1)} %get-tuple-element.64), channel_id=1, source_target_pairs={{0,6},{1,25},{2,0},{3,27},{4,2},{5,29},{6,4},{7,31},{8,14},{9,1},{... | collective-permute-start | bytes 3293192 | tf_op jit(solution)/shard_map/ppermute | solution.py:479
  62.6 29.3 %collective-permute-start.13 = (bf16[3072,128]{1,0:T(8,128)(2,1)S(1)}, bf16[3072,128]{1,0:T(8,128)(2,1)S(1)}, u32[]{:S(2)}, u32[]{:S(2)}) collective-permute-start(bf16[3072,128]{1,0:T(8,128)(2,1)S(1)} %get-tuple-element.61), channel_id=1, source_target_pairs={{0,8},{1,3},{2,10},{3,5},{4,12},{5,7},{6,14},{7,1},{8,16},{9,11},{... | collective-permute-start | bytes 2359304 | tf_op jit(solution)/shard_map/ppermute | solution.py:476
  63.7 33.7 %collective-permute-start.11 = (bf16[3072,128]{1,0:T(8,128)(2,1)S(1)}, bf16[3072,128]{1,0:T(8,128)(2,1)S(1)}, u32[]{:S(2)}, u32[]{:S(2)}) collective-permute-start(bf16[3072,128]{1,0:T(8,128)(2,1)S(1)} %get-tuple-element.58), channel_id=1, source_target_pairs={{0,24},{1,7},{2,26},{3,1},{4,28},{5,3},{6,30},{7,5},{8,0},{9,15},{... | collective-permute-start | bytes 2359304 | tf_op jit(solution)/shard_map/ppermute | solution.py:476
  67.3 30.2 %collective-permute-start.12 = (bf16[3072,128]{1,0:T(8,128)(2,1)S(1)}, bf16[3072,128]{1,0:T(8,128)(2,1)S(1)}, u32[]{:S(2)}, u32[]{:S(2)}) collective-permute-start(bf16[3072,128]{1,0:T(8,128)(2,1)S(1)} %get-tuple-element.59), channel_id=1, source_target_pairs={{0,16},{1,5},{2,18},{3,7},{4,20},{5,1},{6,22},{7,3},{8,24},{9,13},... | collective-permute-start | bytes 2359304 | tf_op jit(solution)/shard_map/ppermute | solution.py:476
  91.9 15.7 %collective-permute-start.10 = (f32[2144,128]{1,0:T(8,128)S(1)}, f32[2144,128]{1,0:T(8,128)S(1)}, u32[]{:S(2)}, u32[]{:S(2)}) collective-permute-start(f32[2144,128]{1,0:T(8,128)S(1)} %get-tuple-element.56), channel_id=1, source_target_pairs={{0,2},{1,9},{2,4},{3,11},{4,6},{5,13},{6,0},{7,15},{8,10},{9,17},{... | collective-permute-start | bytes 3293192 | tf_op jit(solution)/shard_map/ppermute | solution.py:479
  93.7 14.5 %collective-permute-start.9 = (f32[2144,128]{1,0:T(8,128)S(1)}, f32[2144,128]{1,0:T(8,128)S(1)}, u32[]{:S(2)}, u32[]{:S(2)}) collective-permute-start(f32[2144,128]{1,0:T(8,128)S(1)} %get-tuple-element.55), channel_id=1, source_target_pairs={{0,6},{1,25},{2,0},{3,27},{4,2},{5,29},{6,4},{7,31},{8,14},{9,1},{... | collective-permute-start | bytes 3293192 | tf_op jit(solution)/shard_map/ppermute | solution.py:479
  102.4 17.5 %collective-permute-start.17 = (f32[2144,128]{1,0:T(8,128)S(1)}, f32[2144,128]{1,0:T(8,128)S(1)}, u32[]{:S(2)}, u32[]{:S(2)}) collective-permute-start(f32[2144,128]{1,0:T(8,128)S(1)} %get-tuple-element.69), channel_id=1, source_target_pairs={{0,6},{1,25},{2,0},{3,27},{4,2},{5,29},{6,4},{7,31},{8,14},{9,1},{... | collective-permute-start | bytes 3293192 | tf_op jit(solution)/shard_map/ppermute | solution.py:479
  103.7 19.8 %collective-permute-start.16 = (f32[2144,128]{1,0:T(8,128)S(1)}, f32[2144,128]{1,0:T(8,128)S(1)}, u32[]{:S(2)}, u32[]{:S(2)}) collective-permute-start(f32[2144,128]{1,0:T(8,128)S(1)} %get-tuple-element.67), channel_id=1, source_target_pairs={{0,2},{1,9},{2,4},{3,11},{4,6},{5,13},{6,0},{7,15},{8,10},{9,17},{... | collective-permute-start | bytes 3293192 | tf_op jit(solution)/shard_map/ppermute | solution.py:479
  126.7 9.1 %collective-permute-start.19 = (f32[536,128]{1,0:T(8,128)S(1)}, f32[536,128]{1,0:T(8,128)S(1)}, u32[]{:S(2)}, u32[]{:S(2)}) collective-permute-start(f32[536,128]{1,0:T(8,128)S(1)} %get-tuple-element.71), channel_id=1, source_target_pairs={{0,32},{32,64},{64,96},{96,0},{1,33},{33,65},{65,97},{97,1},{2,34}... | collective-permute-start | bytes 823304 | tf_op jit(solution)/shard_map/ppermute | solution.py:496
  127.0 15.3 %collective-permute-start.20 = (f32[536,128]{1,0:T(8,128)S(1)}, f32[536,128]{1,0:T(8,128)S(1)}, u32[]{:S(2)}, u32[]{:S(2)}) collective-permute-start(f32[536,128]{1,0:T(8,128)S(1)} %get-tuple-element.72), channel_id=1, source_target_pairs={{0,64},{32,96},{64,0},{96,32},{1,65},{33,97},{65,1},{97,33},{2,66}... | collective-permute-start | bytes 823304 | tf_op jit(solution)/shard_map/ppermute | solution.py:496
  130.1 12.2 %collective-permute-start.21 = (f32[536,128]{1,0:T(8,128)S(1)}, f32[536,128]{1,0:T(8,128)S(1)}, u32[]{:S(2)}, u32[]{:S(2)}) collective-permute-start(f32[536,128]{1,0:T(8,128)S(1)} %get-tuple-element.73), channel_id=1, source_target_pairs={{0,96},{32,0},{64,32},{96,64},{1,97},{33,1},{65,33},{97,65},{2,98}... | collective-permute-start | bytes 823304 | tf_op jit(solution)/shard_map/ppermute | solution.py:496
  142.4 8.8 %collective-permute-start.22 = (f32[536,128]{1,0:T(8,128)S(1)}, f32[536,128]{1,0:T(8,128)S(1)}, u32[]{:S(2)}, u32[]{:S(2)}) collective-permute-start(f32[536,128]{1,0:T(8,128)S(1)} %add_add_fusion.refs_0_), channel_id=1, source_target_pairs={{0,32},{32,64},{64,96},{96,0},{1,33},{33,65},{65,97},{97,1},{2,34}... | collective-permute-start | bytes 823304 | tf_op jit(solution)/shard_map/ppermute | solution.py:497
  143.9 14.8 %collective-permute-start.23 = (f32[536,128]{1,0:T(8,128)S(1)}, f32[536,128]{1,0:T(8,128)S(1)}, u32[]{:S(2)}, u32[]{:S(2)}) collective-permute-start(f32[536,128]{1,0:T(8,128)S(1)} %add_add_fusion.refs_0_), channel_id=1, source_target_pairs={{0,64},{32,96},{64,0},{96,32},{1,65},{33,97},{65,1},{97,33},{2,66}... | collective-permute-start | bytes 823304 | tf_op jit(solution)/shard_map/ppermute | solution.py:497
  146.7 12.1 %collective-permute-start.24 = (f32[536,128]{1,0:T(8,128)S(1)}, f32[536,128]{1,0:T(8,128)S(1)}, u32[]{:S(2)}, u32[]{:S(2)}) collective-permute-start(f32[536,128]{1,0:T(8,128)S(1)} %add_add_fusion.refs_0_), channel_id=1, source_target_pairs={{0,96},{32,0},{64,32},{96,64},{1,97},{33,1},{65,33},{97,65},{2,98}... | collective-permute-start | bytes 823304 | tf_op jit(solution)/shard_map/ppermute | solution.py:497
  (7 other events, 60.0 us)

commit v6 on v5

--- a/solution.py
+++ b/solution.py
@@ -25,11 +25,11 @@
 I32 = jnp.int32
 HEAD = 16
 UNITS = (((2, 0), (2, 1)), ((0, 0), (0, 1)), ((1, 1), (3, 0)), ((1, 0), (3, 1)))
-PACKED = CELL_DEV * ROWS
-PIECE = PACKED + 3 * CELL_DEV
+PACKED = (CELL_DEV - 1) * ROWS
+PIECE = PACKED + 2 * CELL_DEV
 QCELL = CELL_DEV // NZ
 QPACKED = QCELL * ROWS
-QPIECE = QPACKED + 3 * QCELL
+QPIECE = QPACKED + 2 * QCELL
 VMEM_LIMIT = 16 * 1024 * 1024
 LARGE_VMEM = 56 * 1024 * 1024
 SMALL_VMEM = 6 * 1024 * 1024
@@ -248,7 +248,7 @@
     lax.fori_loop(0, steps, step, 0)
 
 
-def gram_body(group, members, counted, quartered, started, pos, lists, sizes, tallies, *refs):
+def gram_body(group, members, counted, started, lists, sizes, tallies, *refs):
     blocks, refs = refs[: len(members)], refs[len(members) :]
     first, second = started
     starts = (refs[:first], refs[first : first + second])
@@ -266,7 +266,7 @@
             acc[pl.ds(pl.multiple_of(u * PIECE + i * ROWS, 8), ROWS), :] = value
         return 0
 
-    lax.fori_loop(0, CELL_DEV, clear, 0)
+    lax.fori_loop(0, PACKED // ROWS, clear, 0)
 
     def clear_sums(i, _):
         acc_s[pl.ds(pl.multiple_of(i * 8, 8), 8), :] = jnp.zeros((8, D), F32)
@@ -276,65 +276,51 @@
     lax.fori_loop(0, CHIP_CELLS, clear_sums, 0)
     for g, member in zip(members, blocks):
         add_blocks(group * GROUPS + g, lists, sizes, member, acc, acc_s, acc_q)
+    lane = lax.broadcasted_iota(I32, (CELL_DEV, D), 1)
     for u in range(2):
-        base = u * PIECE
-        for k, source in enumerate((acc_s, acc_q)):
+        totals = []
+        for source in (acc_s, acc_q):
             total = source[pl.ds(u * CELL_DEV * 8, CELL_DEV, stride=8), :]
             for j in range(1, 8):
                 total = total + source[pl.ds(u * CELL_DEV * 8 + j, CELL_DEV, stride=8), :]
+            totals.append(total)
+        count = jnp.zeros((CELL_DEV, D), F32)
+        if counted:
+            for j in range(CELL_DEV):
+                value = tallies[group * CHIP_CELLS + u * CELL_DEV + j].astype(F32)
+                acc_s[pl.ds(u * CELL_DEV * 8 + j, 1), :] = jnp.full((1, D), value, F32)
+            count = acc_s[pl.ds(u * CELL_DEV * 8, CELL_DEV), :]
+        totals[1] = jnp.where(lane < ROWS, count, totals[1])
+        for k, total in enumerate(totals):
             rows = PACKED + k * CELL_DEV
-            acc[pl.ds(base + rows, CELL_DEV), :] = add_starts(total, u, pl.ds(rows, CELL_DEV))
-        for j in range(CELL_DEV):
-            count = jnp.zeros((1, D), F32)
-            if counted:
-                count = jnp.full((1, D), tallies[group * CHIP_CELLS + u * CELL_DEV + j].astype(F32), F32)
-            rows = PACKED + 2 * CELL_DEV + j
-            acc[pl.ds(base + rows, 1), :] = add_starts(count, u, pl.ds(rows, 1))
-    if not quartered:
-
-        def copy_out(i, _):
-            for u in range(2):
-                outs[u][pl.ds(pl.multiple_of(i * 32, 32), 32), :] = acc[
-                    pl.ds(pl.multiple_of(u * PIECE + i * 32, 32), 32), :
-                ]
-            return 0
-
-        lax.fori_loop(0, PIECE // 32, copy_out, 0)
-        return
-    for dz in range(NZ):
-        q = lax.rem(pos[3] + dz, NZ)
+            acc[pl.ds(u * PIECE + rows, CELL_DEV), :] = add_starts(total, u, pl.ds(rows, CELL_DEV))
+
+    def copy_out(i, _):
         for u in range(2):
-
-            def copy_quarter(i, _, dz=dz, q=q, u=u):
-                outs[dz][pl.ds(pl.multiple_of(u * QPIECE + i * ROWS, 8), ROWS), :] = acc[
-                    pl.ds(pl.multiple_of(u * PIECE + q * QPACKED + i * ROWS, 8), ROWS), :
-                ]
-                return 0
-
-            lax.fori_loop(0, QCELL, copy_quarter, 0)
-            for k in range(3):
-                outs[dz][pl.ds(u * QPIECE + QPACKED + k * QCELL, QCELL), :] = acc[
-                    pl.ds(pl.multiple_of(u * PIECE + PACKED + k * CELL_DEV + q * QCELL, QCELL), QCELL), :
-                ]
-
-
-def gram(group, pos, lists, sizes, tallies, blocks, first=(), second=(), members=(0, 1, 2, 3), counted=True, quartered=False):
+            outs[u][pl.ds(pl.multiple_of(i * 32, 32), 32), :] = acc[
+                pl.ds(pl.multiple_of(u * PIECE + i * 32, 32), 32), :
+            ]
+        return 0
+
+    lax.fori_loop(0, PIECE // 32, copy_out, 0)
+
+
+def gram(group, lists, sizes, tallies, blocks, first=(), second=(), members=(0, 1, 2, 3), counted=True):
     def body(*refs):
-        gram_body(group, members, counted, quartered, (len(first), len(second)), *refs)
+        gram_body(group, members, counted, (len(first), len(second)), *refs)
 
     half = jax.ShapeDtypeStruct((PIECE, D), F32)
-    quarter = jax.ShapeDtypeStruct((2 * QPIECE, D), F32)
-    outs = [quarter] * NZ if quartered else [half] * 2
+    outs = [half] * 2
     return pl.pallas_call(
         body,
         out_shape=outs,
-        in_specs=[SMEM_SPEC] * 4 + [VMEM_SPEC] * (len(members) + len(first) + len(second)),
+        in_specs=[SMEM_SPEC] * 3 + [VMEM_SPEC] * (len(members) + len(first) + len(second)),
         out_specs=[VMEM_SPEC] * len(outs),
         scratch_shapes=[pltpu.VMEM((NC * PIECE, D), F32)] + [pltpu.VMEM(((CHIP_CELLS + 1) * 8, D), F32)] * 2,
         compiler_params=pltpu.CompilerParams(vmem_limit_bytes=SMALL_VMEM),
         cost_estimate=pl.CostEstimate(flops=10**9, bytes_accessed=10**7, transcendentals=0),
         name=f"gram{group}" + ("" if counted else "b"),
-    )(pos, lists, sizes, tallies, *(blocks[g] for g in members), *first, *second)
+    )(lists, sizes, tallies, *(blocks[g] for g in members), *first, *second)
 
 
 def total_body(*refs):
@@ -360,9 +346,8 @@
     )(*parts)
 
 
-def join_body(extra, pos, *refs):
+def join_body(pos, *refs):
     outs, parts = refs[-NZ:], refs[:-NZ]
-    parts, extras = parts[: len(parts) - extra], parts[len(parts) - extra :]
     z = pos[3]
 
     def total(rows):
@@ -375,8 +360,6 @@
         q = lax.rem(z + dz, NZ)
 
         def put(rows, value, dz=dz):
-            for more in extras if dz == 0 else ():
-                value = value + more[rows, :]
             outs[dz][rows, :] = value
 
         def step(i, _, q=q, put=put):
@@ -387,25 +370,22 @@
             return 0
 
         lax.fori_loop(0, QCELL, step, 0)
-        for k in range(3):
+        for k in range(2):
             put(
                 pl.ds(QPACKED + k * QCELL, QCELL),
                 total(pl.ds(pl.multiple_of(PACKED + k * CELL_DEV + q * QCELL, QCELL), QCELL)),
             )
 
 
-def join(pos, parts, extras=()):
-    def body(*refs):
-        join_body(len(extras), *refs)
-
-    return pl.pallas_call(
-        body,
+def join(pos, parts):
+    return pl.pallas_call(
+        join_body,
         out_shape=[jax.ShapeDtypeStruct((QPIECE, D), F32)] * NZ,
-        in_specs=[SMEM_SPEC] + [VMEM_SPEC] * (len(parts) + len(extras)),
+        in_specs=[SMEM_SPEC] + [VMEM_SPEC] * len(parts),
         out_specs=[VMEM_SPEC] * NZ,
         compiler_params=pltpu.CompilerParams(vmem_limit_bytes=SMALL_VMEM),
         name="join",
-    )(pos, *parts, *extras)
+    )(pos, *parts)
 
 
 def finish_body(pos, *refs):
@@ -418,10 +398,10 @@
         q = lax.rem(z + NZ - dz, NZ)
         part = parts[dz]
         sums = part[pl.ds(QPACKED, QCELL), :]
-        counts = part[pl.ds(QPACKED + 2 * QCELL, QCELL), :]
+        counts = jnp.broadcast_to(part[pl.ds(QPACKED + QCELL, QCELL), :][:, :1], (QCELL, D))
         safe = jnp.maximum(counts, 1.0)
         mean = sums / safe
-        inverse = 1.0 / safe
+        inverse = jnp.where(counts > 0.0, 1.0 / safe, 0.0)
         mean_out[pl.ds(pl.multiple_of(q * QCELL, QCELL), QCELL), :] = mean
         scaled = jnp.transpose(jnp.concatenate([mean * counts] * (D // QCELL), axis=0))
         for j in range(QCELL):
@@ -455,7 +435,7 @@
 def local(vectors, block_cells, dest_counts):
     pos = place()
     counts, cells = dest_counts[0, 0], block_cells[0]
-    rows = vectors.reshape(BLK * ROWS, D)
+    rows = pltpu.with_memory_space_constraint(vectors.reshape(BLK * ROWS, D), pltpu.HBM)
     sent, got = [], []
     for group, units in enumerate(UNITS):
         turn, flows, header = pos, [(d, units) for d in SHIFTS], ()
@@ -479,7 +459,7 @@
         return lax.ppermute(piece, "cell", across(rel))
 
     def grams(group, *rest, **options):
-        return gram(group, pos, lists, sizes, tallies, got[group], *rest, **options)
+        return gram(group, lists, sizes, tallies, got[group], *rest, **options)
 
     fore, back = grams(0)
     fore, back = step(1, fore), step(3, back)

time: 164 us -> 161 us (0.982)
  starting transfers between devices: 44.8 us -> 50.8 us
  local copies, waits for them, and re-layouts: 5.58 us -> 0.01 us
  Pallas kernels: 57.7 us -> 55.6 us
    unnamed x12 -> x6, local copies, waits for them, and re-layouts: 5.58 us -> 0.01 us
    ppermute x12, waiting for transfers between devices: 22.9 us -> 19.7 us  [local(): lax.ppermute(run, 'cell', along(d))]
    ppermute x6, starting transfers between devices: 7.89 us -> 10.9 us  [step(): return lax.ppermute(piece, 'cell', across(rel))]
    ppermute x6, waiting for transfers between devices: 4.6 us -> 7.02 us  [step(): return lax.ppermute(piece, 'cell', across(rel))]
    pallas_call x6, Pallas kernels: 33.3 us -> 30.9 us  [the longest x5 30.1 us: gram(): pl.pallas_call(body, out_shape=outs, in_specs=[SMEM_SPEC] * 3 + [VMEM_SPE...]
    ppermute x1, starting transfers between devices: 3.15 us -> 5.17 us  [local(): swapped = lax.ppermute(other_total([other, other3]), 'cell', SWAP)]
  transfers between devices with their start and end apart: 25 -> 25, of which waited for: 13 -> 11; matrix products, arithmetic and copies ran while one was open for 0% -> 0% of each run, Pallas kernels for 30% -> 29%
where the time goes in v6:
time: 161 us; the launch traced here: 159 us
  Pallas kernels  55.6 us (35%)
  waiting for transfers between devices  51.5 us (32%)
  starting transfers between devices  50.8 us (32%)
    pallas_call x5, Pallas kernels, gram(): pl.pallas_call(body, out_shape=outs, in_specs=[SMEM_SPEC] * 3 + [VMEM_SPE...  30.1 us
    ppermute x12, starting transfers between devices, local(): lax.ppermute(run, 'cell', along(d))  23.7 us
    ppermute x12, waiting for transfers between devices, local(): lax.ppermute(run, 'cell', along(d))  19.7 us
    pallas_call x4, Pallas kernels, gather_runs(): pl.pallas_call(body, out_shape=[jax.ShapeDtypeStruct((rows, D), vectors.d...  13.1 us
    ppermute x3, waiting for transfers between devices, local(): lax.ppermute(mine, 'dp', dp_perm(dz))  11.5 us
    ppermute x3, waiting for transfers between devices, local(): mine = mine + lax.ppermute(quarters[dz], 'dp', dp_perm(dz))  11 us
    ppermute x6, starting transfers between devices, step(): return lax.ppermute(piece, 'cell', across(rel))  10.9 us
    pallas_call x1, Pallas kernels, make_lists(): pl.pallas_call(lists_body, out_shape=[jax.ShapeDtypeStruct((LIST,), I32),...  7.09 us
  transfers between devices with their start and end apart: 25, of which 11 were waited for; matrix products, arithmetic and copies ran while one was open for 0% of the time, Pallas kernels for 29%

profile of v6, /device:TPU:1, one launch (start us, length us, event | category | flops | bytes accessed | tf_op | source)
XLA Modules:
  0.0 159.5 jit_solution(66978345001263824)
XLA Ops:
  1.3 3.9 %gather0.1 = (bf16[3088,128]{1,0:T(8,128)(2,1)}, bf16[3088,128]{1,0:T(8,128)(2,1)}, bf16[3088,128]{1,0:T(8,128)(2,1)}) custom-call(s32[4]{0:T(128)} %pad_add_fusion.refs_0_.pos, s32[32]{0:T(128)} %bitcast.7, bf16[24576,128]{1,0:T(8,128)(2,1)} %bitcast.13, s32[1,384]{1,0:T(1,128)} %refs_3_.1, s32[1,32]{1,0:T(1,128)} %bitcast.8), custom_call_target="tpu_custom_call" | custom-call | tf_op jit(solution)/shard_map/gather0/pallas_call | solution.py:126
  10.6 3.6 %gather1.1 = (bf16[3072,128]{1,0:T(8,128)(2,1)}, bf16[3072,128]{1,0:T(8,128)(2,1)}, bf16[3072,128]{1,0:T(8,128)(2,1)}) custom-call(s32[4]{0:T(128)S(1)} %copy-done, s32[32]{0:T(128)S(1)} %bitcast.9, bf16[24576,128]{1,0:T(8,128)(2,1)} %bitcast.14), custom_call_target="tpu_custom_call" | custom-call | tf_op jit(solution)/shard_map/gather1/pallas_call | solution.py:126
  18.9 10.0 %collective-permute-start.5 = (bf16[3072,128]{1,0:T(8,128)(2,1)}, bf16[3072,128]{1,0:T(8,128)(2,1)}, u32[]{:S(2)}, u32[]{:S(2)}) collective-permute-start(bf16[3072,128]{1,0:T(8,128)(2,1)} %get-tuple-element.47), channel_id=1, source_target_pairs={{0,16},{1,5},{2,18},{3,7},{4,20},{5,1},{6,22},{7,3},{8,24},{9,13},... | collective-permute-start | bytes 2359304 | tf_op jit(solution)/shard_map/ppermute | solution.py:456
  29.0 7.1 %lists.1 = (s32[896]{0:T(1024)S(1)}, s32[32]{0:T(128)S(1)}, s32[256]{0:T(256)S(1)}) custom-call(s32[4]{0:T(128)S(1)} %copy-done, s32[384]{0:T(512)S(1)} %reduce.own_cells, s32[32]{0:T(128)S(1)} %bitcast.10, bf16[3088,128]{1,0:T(8,128)(2,1)S(1)} %collective-permute-done.refs_0_.refs_4_, bf16[3088,128]{1,0:T(8,128)(2,1)S(1)} %collective-permute-done.1.refs_1_.refs_5_, ...), custom_call_target="tpu_custom_call" | custom-call | tf_op jit(solution)/shard_map/lists/pallas_call | solution.py:195
  36.1 2.8 %gather2.1 = (bf16[3072,128]{1,0:T(8,128)(2,1)S(1)}, bf16[3072,128]{1,0:T(8,128)(2,1)S(1)}, bf16[3072,128]{1,0:T(8,128)(2,1)S(1)}, bf16[3072,128]{1,0:T(8,128)(2,1)S(1)}, bf16[3072,128]{1,0:T(8,128)(2,1)S(1)}) custom-call(s32[4]{0:T(128)S(1)} %copy-done, s32[32]{0:T(128)S(1)} %bitcast.11, bf16[24576,128]{1,0:T(8,128)(2,1)} %bitcast.15), custom_call_target="tpu_custom_call" | custom-call | tf_op jit(solution)/shard_map/gather2/pallas_call | solution.py:126
  41.6 7.8 %gram0.1 = (f32[2048,128]{1,0:T(8,128)S(1)}, f32[2048,128]{1,0:T(8,128)S(1)}) custom-call(s32[896]{0:T(1024)S(1)} %get-tuple-element.41.refs_0_, s32[32]{0:T(128)S(1)} %get-tuple-element.42.refs_1_, s32[256]{0:T(256)S(1)} %get-tuple-element.43.refs_2_, bf16[3072,128]{1,0:T(8,128)(2,1)S(1)} %get-tuple-element.62.refs_3_, ...), custom_call_target="tpu_custom_call" | custom-call | flops 1000000000 | bytes 10000000 | tf_op jit(solution)/shard_map/gram0/pallas_call | solution.py:314
  49.4 6.0 %collective-permute-start.14 = (f32[2048,128]{1,0:T(8,128)S(1)}, f32[2048,128]{1,0:T(8,128)S(1)}, u32[]{:S(2)}, u32[]{:S(2)}) collective-permute-start(f32[2048,128]{1,0:T(8,128)S(1)} %get-tuple-element.63), channel_id=1, source_target_pairs={{0,2},{1,9},{2,4},{3,11},{4,6},{5,13},{6,0},{7,15},{8,10},{9,17},{... | collective-permute-start | bytes 3145736 | tf_op jit(solution)/shard_map/ppermute | solution.py:459
  55.4 2.7 %gather3.1 = (bf16[3072,128]{1,0:T(8,128)(2,1)S(1)}, bf16[3072,128]{1,0:T(8,128)(2,1)S(1)}, bf16[3072,128]{1,0:T(8,128)(2,1)S(1)}, bf16[3072,128]{1,0:T(8,128)(2,1)S(1)}, bf16[3072,128]{1,0:T(8,128)(2,1)S(1)}) custom-call(s32[4]{0:T(128)S(1)} %copy-done, s32[32]{0:T(128)S(1)} %bitcast.12, bf16[24576,128]{1,0:T(8,128)(2,1)} %bitcast.16), custom_call_target="tpu_custom_call" | custom-call | tf_op jit(solution)/shard_map/gather3/pallas_call | solution.py:126
  58.3 2.7 %collective-permute-start.11 = (bf16[3072,128]{1,0:T(8,128)(2,1)S(1)}, bf16[3072,128]{1,0:T(8,128)(2,1)S(1)}, u32[]{:S(2)}, u32[]{:S(2)}) collective-permute-start(bf16[3072,128]{1,0:T(8,128)(2,1)S(1)} %get-tuple-element.58), channel_id=1, source_target_pairs={{0,24},{1,7},{2,26},{3,1},{4,28},{5,3},{6,30},{7,5},{8,0},{9,15},{... | collective-permute-start | bytes 2359304 | tf_op jit(solution)/shard_map/ppermute | solution.py:456
  60.9 7.0 %collective-permute-done.8.refs_6_ = bf16[3072,128]{1,0:T(8,128)(2,1)S(1)} collective-permute-done((bf16[3072,128]{1,0:T(8,128)(2,1)S(1)}, bf16[3072,128]{1,0:T(8,128)(2,1)S(1)}, u32[]{:S(2)}, u32[]{:S(2)}) %collective-permute-start.8) | collective-permute-done | bytes 786464 | tf_op jit(solution)/shard_map/ppermute | solution.py:456
  68.0 6.2 %gram2.1 = (f32[2048,128]{1,0:T(8,128)S(1)}, f32[2048,128]{1,0:T(8,128)S(1)}) custom-call(s32[896]{0:T(1024)S(1)} %get-tuple-element.41.refs_0_, s32[32]{0:T(128)S(1)} %get-tuple-element.42.refs_1_, s32[256]{0:T(256)S(1)} %get-tuple-element.43.refs_2_, bf16[3072,128]{1,0:T(8,128)(2,1)S(1)} %get-tuple-element.51.refs_3_, ...), custom_call_target="tpu_custom_call" | custom-call | flops 1000000000 | bytes 10000000 | tf_op jit(solution)/shard_map/gram2/pallas_call | solution.py:314
  74.2 7.7 %collective-permute-done.13.refs_4_ = bf16[3072,128]{1,0:T(8,128)(2,1)S(1)} collective-permute-done((bf16[3072,128]{1,0:T(8,128)(2,1)S(1)}, bf16[3072,128]{1,0:T(8,128)(2,1)S(1)}, u32[]{:S(2)}, u32[]{:S(2)}) %collective-permute-start.13) | collective-permute-done | bytes 786464 | tf_op jit(solution)/shard_map/ppermute | solution.py:456
  84.6 4.3 %gram3.1 = (f32[2048,128]{1,0:T(8,128)S(1)}, f32[2048,128]{1,0:T(8,128)S(1)}) custom-call(s32[896]{0:T(1024)S(1)} %get-tuple-element.41.refs_0_, s32[32]{0:T(128)S(1)} %get-tuple-element.42.refs_1_, s32[256]{0:T(256)S(1)} %get-tuple-element.43.refs_2_, bf16[3072,128]{1,0:T(8,128)(2,1)S(1)} %get-tuple-element.60.refs_3_, ...), custom_call_target="tpu_custom_call" | custom-call | flops 1000000000 | bytes 10000000 | tf_op jit(solution)/shard_map/gram3/pallas_call | solution.py:314
  89.0 3.0 %collective-permute-done.12.refs_4_ = bf16[3072,128]{1,0:T(8,128)(2,1)S(1)} collective-permute-done((bf16[3072,128]{1,0:T(8,128)(2,1)S(1)}, bf16[3072,128]{1,0:T(8,128)(2,1)S(1)}, u32[]{:S(2)}, u32[]{:S(2)}) %collective-permute-start.12) | collective-permute-done | bytes 786464 | tf_op jit(solution)/shard_map/ppermute | solution.py:456
  92.0 5.8 %gram3b.1 = (f32[2048,128]{1,0:T(8,128)S(1)}, f32[2048,128]{1,0:T(8,128)S(1)}) custom-call(s32[896]{0:T(1024)S(1)} %get-tuple-element.41.refs_0_, s32[32]{0:T(128)S(1)} %get-tuple-element.42.refs_1_, s32[256]{0:T(256)S(1)} %get-tuple-element.43.refs_2_, bf16[3072,128]{1,0:T(8,128)(2,1)S(1)} %collective-permute-done.11.refs_3_, ...), custom_call_target="tpu_custom_call" | custom-call | flops 1000000000 | bytes 10000000 | tf_op jit(solution)/shard_map/gram3b/pallas_call | solution.py:314
  102.2 5.9 %gram1.1 = (f32[2048,128]{1,0:T(8,128)S(1)}, f32[2048,128]{1,0:T(8,128)S(1)}) custom-call(s32[896]{0:T(1024)S(1)} %get-tuple-element.41.refs_0_, s32[32]{0:T(128)S(1)} %get-tuple-element.42.refs_1_, s32[256]{0:T(256)S(1)} %get-tuple-element.43.refs_2_, bf16[3072,128]{1,0:T(8,128)(2,1)S(1)} %get-tuple-element.49.refs_3_, ...), custom_call_target="tpu_custom_call" | custom-call | flops 1000000000 | bytes 10000000 | tf_op jit(solution)/shard_map/gram1/pallas_call | solution.py:314
  108.1 5.0 %collective-permute-done.17.refs_1_ = f32[2048,128]{1,0:T(8,128)S(1)} collective-permute-done((f32[2048,128]{1,0:T(8,128)S(1)}, f32[2048,128]{1,0:T(8,128)S(1)}, u32[]{:S(2)}, u32[]{:S(2)}) %collective-permute-start.17) | collective-permute-done | bytes 1048608 | tf_op jit(solution)/shard_map/ppermute | solution.py:459
  113.4 5.2 %collective-permute-start.18 = (f32[2048,128]{1,0:T(8,128)S(1)}, f32[2048,128]{1,0:T(8,128)S(1)}, u32[]{:S(2)}, u32[]{:S(2)}) collective-permute-start(f32[2048,128]{1,0:T(8,128)S(1)} %other_total.1), channel_id=1, source_target_pairs={{0,1},{1,0},{2,3},{3,2},{4,5},{5,4},{6,7},{7,6},{8,9},{9,8},{10,11... | collective-permute-start | bytes 3145736 | tf_op jit(solution)/shard_map/ppermute | solution.py:472
  123.7 3.8 %collective-permute-start.20 = (f32[528,128]{1,0:T(8,128)S(1)}, f32[528,128]{1,0:T(8,128)S(1)}, u32[]{:S(2)}, u32[]{:S(2)}) collective-permute-start(f32[528,128]{1,0:T(8,128)S(1)} %get-tuple-element.72), channel_id=1, source_target_pairs={{0,64},{32,96},{64,0},{96,32},{1,65},{33,97},{65,1},{97,33},{2,66}... | collective-permute-start | bytes 811016 | tf_op jit(solution)/shard_map/ppermute | solution.py:476
  127.9 4.3 %collective-permute-done.19 = f32[528,128]{1,0:T(8,128)S(1)} collective-permute-done((f32[528,128]{1,0:T(8,128)S(1)}, f32[528,128]{1,0:T(8,128)S(1)}, u32[]{:S(2)}, u32[]{:S(2)}) %collective-permute-start.19) | collective-permute-done | bytes 270368 | tf_op jit(solution)/shard_map/ppermute | solution.py:476
  132.2 6.7 %collective-permute-done.20 = f32[528,128]{1,0:T(8,128)S(1)} collective-permute-done((f32[528,128]{1,0:T(8,128)S(1)}, f32[528,128]{1,0:T(8,128)S(1)}, u32[]{:S(2)}, u32[]{:S(2)}) %collective-permute-start.20) | collective-permute-done | bytes 270368 | tf_op jit(solution)/shard_map/ppermute | solution.py:476
  143.8 3.7 %collective-permute-done.22.refs_1_ = f32[528,128]{1,0:T(8,128)S(1)} collective-permute-done((f32[528,128]{1,0:T(8,128)S(1)}, f32[528,128]{1,0:T(8,128)S(1)}, u32[]{:S(2)}, u32[]{:S(2)}) %collective-permute-start.22) | collective-permute-done | bytes 270368 | tf_op jit(solution)/shard_map/ppermute | solution.py:477
  147.5 7.8 %collective-permute-done.23.refs_2_ = f32[528,128]{1,0:T(8,128)S(1)} collective-permute-done((f32[528,128]{1,0:T(8,128)S(1)}, f32[528,128]{1,0:T(8,128)S(1)}, u32[]{:S(2)}, u32[]{:S(2)}) %collective-permute-start.23) | collective-permute-done | bytes 270368 | tf_op jit(solution)/shard_map/ppermute | solution.py:477
  155.3 4.1 %finish.1 = (f32[32,128]{1,0:T(8,128)}, f32[32,128,128]{2,1,0:T(8,128)}) custom-call(s32[4]{0:T(128)S(1)} %copy-done, f32[528,128]{1,0:T(8,128)S(1)} %add_add_fusion.refs_0_, f32[528,128]{1,0:T(8,128)S(1)} %collective-permute-done.22.refs_1_, f32[528,128]{1,0:T(8,128)S(1)} %collective-permute-done.23.refs_2_, f32[528,128]{1,0:T(8,128)S(1)} %collective-permute-done.24.refs_3_), custom_call_target="tpu_custom_call" | custom-call | tf_op jit(solution)/shard_map/finish/pallas_call | solution.py:422
  (48 shorter events, 31.4 us)
Async XLA Ops:
  5.3 13.6 %collective-permute-start = (bf16[3088,128]{1,0:T(8,128)(2,1)}, bf16[3088,128]{1,0:T(8,128)(2,1)S(1)}, u32[]{:S(2)}, u32[]{:S(2)}) collective-permute-start(bf16[3088,128]{1,0:T(8,128)(2,1)} %get-tuple-element.38), channel_id=1, source_target_pairs={{0,8},{1,3},{2,10},{3,5},{4,12},{5,7},{6,14},{7,1},{8,16},{9,11},{... | collective-permute-start | bytes 2371592 | tf_op jit(solution)/shard_map/ppermute | solution.py:456
  7.5 21.5 %collective-permute-start.1 = (bf16[3088,128]{1,0:T(8,128)(2,1)}, bf16[3088,128]{1,0:T(8,128)(2,1)S(1)}, u32[]{:S(2)}, u32[]{:S(2)}) collective-permute-start(bf16[3088,128]{1,0:T(8,128)(2,1)} %get-tuple-element.39), channel_id=1, source_target_pairs={{0,24},{1,7},{2,26},{3,1},{4,28},{5,3},{6,30},{7,5},{8,0},{9,15},{... | collective-permute-start | bytes 2371592 | tf_op jit(solution)/shard_map/ppermute | solution.py:456
  9.1 19.9 %collective-permute-start.2 = (bf16[3088,128]{1,0:T(8,128)(2,1)}, bf16[3088,128]{1,0:T(8,128)(2,1)S(1)}, u32[]{:S(2)}, u32[]{:S(2)}) collective-permute-start(bf16[3088,128]{1,0:T(8,128)(2,1)} %get-tuple-element.40), channel_id=1, source_target_pairs={{0,16},{1,5},{2,18},{3,7},{4,20},{5,1},{6,22},{7,3},{8,24},{9,13},... | collective-permute-start | bytes 2371592 | tf_op jit(solution)/shard_map/ppermute | solution.py:456
  14.2 27.5 %collective-permute-start.3 = (bf16[3072,128]{1,0:T(8,128)(2,1)}, bf16[3072,128]{1,0:T(8,128)(2,1)S(1)}, u32[]{:S(2)}, u32[]{:S(2)}) collective-permute-start(bf16[3072,128]{1,0:T(8,128)(2,1)} %get-tuple-element.45), channel_id=1, source_target_pairs={{0,8},{1,3},{2,10},{3,5},{4,12},{5,7},{6,14},{7,1},{8,16},{9,11},{... | collective-permute-start | bytes 2359304 | tf_op jit(solution)/shard_map/ppermute | solution.py:456
  14.8 34.6 %collective-permute-start.4 = (bf16[3072,128]{1,0:T(8,128)(2,1)}, bf16[3072,128]{1,0:T(8,128)(2,1)}, u32[]{:S(2)}, u32[]{:S(2)}) collective-permute-start(bf16[3072,128]{1,0:T(8,128)(2,1)} %get-tuple-element.46), channel_id=1, source_target_pairs={{0,24},{1,7},{2,26},{3,1},{4,28},{5,3},{6,30},{7,5},{8,0},{9,15},{... | collective-permute-start | bytes 2359304 | tf_op jit(solution)/shard_map/ppermute | solution.py:456
  18.9 36.5 %collective-permute-start.5 = (bf16[3072,128]{1,0:T(8,128)(2,1)}, bf16[3072,128]{1,0:T(8,128)(2,1)}, u32[]{:S(2)}, u32[]{:S(2)}) collective-permute-start(bf16[3072,128]{1,0:T(8,128)(2,1)} %get-tuple-element.47), channel_id=1, source_target_pairs={{0,16},{1,5},{2,18},{3,7},{4,20},{5,1},{6,22},{7,3},{8,24},{9,13},... | collective-permute-start | bytes 2359304 | tf_op jit(solution)/shard_map/ppermute | solution.py:456
  38.9 19.3 %collective-permute-start.6 = (bf16[3072,128]{1,0:T(8,128)(2,1)S(1)}, bf16[3072,128]{1,0:T(8,128)(2,1)S(1)}, u32[]{:S(2)}, u32[]{:S(2)}) collective-permute-start(bf16[3072,128]{1,0:T(8,128)(2,1)S(1)} %get-tuple-element.52), channel_id=1, source_target_pairs={{0,8},{1,3},{2,10},{3,5},{4,12},{5,7},{6,14},{7,1},{8,16},{9,11},{... | collective-permute-start | bytes 2359304 | tf_op jit(solution)/shard_map/ppermute | solution.py:456
  39.4 18.9 %collective-permute-start.7 = (bf16[3072,128]{1,0:T(8,128)(2,1)S(1)}, bf16[3072,128]{1,0:T(8,128)(2,1)S(1)}, u32[]{:S(2)}, u32[]{:S(2)}) collective-permute-start(bf16[3072,128]{1,0:T(8,128)(2,1)S(1)} %get-tuple-element.53), channel_id=1, source_target_pairs={{0,24},{1,7},{2,26},{3,1},{4,28},{5,3},{6,30},{7,5},{8,0},{9,15},{... | collective-permute-start | bytes 2359304 | tf_op jit(solution)/shard_map/ppermute | solution.py:456
  41.6 26.3 %collective-permute-start.8 = (bf16[3072,128]{1,0:T(8,128)(2,1)S(1)}, bf16[3072,128]{1,0:T(8,128)(2,1)S(1)}, u32[]{:S(2)}, u32[]{:S(2)}) collective-permute-start(bf16[3072,128]{1,0:T(8,128)(2,1)S(1)} %get-tuple-element.54), channel_id=1, source_target_pairs={{0,16},{1,5},{2,18},{3,7},{4,20},{5,1},{6,22},{7,3},{8,24},{9,13},... | collective-permute-start | bytes 2359304 | tf_op jit(solution)/shard_map/ppermute | solution.py:456
  49.4 33.5 %collective-permute-start.14 = (f32[2048,128]{1,0:T(8,128)S(1)}, f32[2048,128]{1,0:T(8,128)S(1)}, u32[]{:S(2)}, u32[]{:S(2)}) collective-permute-start(f32[2048,128]{1,0:T(8,128)S(1)} %get-tuple-element.63), channel_id=1, source_target_pairs={{0,2},{1,9},{2,4},{3,11},{4,6},{5,13},{6,0},{7,15},{8,10},{9,17},{... | collective-permute-start | bytes 3145736 | tf_op jit(solution)/shard_map/ppermute | solution.py:459
  55.4 29.2 %collective-permute-start.15 = (f32[2048,128]{1,0:T(8,128)S(1)}, f32[2048,128]{1,0:T(8,128)S(1)}, u32[]{:S(2)}, u32[]{:S(2)}) collective-permute-start(f32[2048,128]{1,0:T(8,128)S(1)} %get-tuple-element.64), channel_id=1, source_target_pairs={{0,6},{1,25},{2,0},{3,27},{4,2},{5,29},{6,4},{7,31},{8,14},{9,1},{... | collective-permute-start | bytes 3145736 | tf_op jit(solution)/shard_map/ppermute | solution.py:459
  58.2 23.8 %collective-permute-start.13 = (bf16[3072,128]{1,0:T(8,128)(2,1)S(1)}, bf16[3072,128]{1,0:T(8,128)(2,1)S(1)}, u32[]{:S(2)}, u32[]{:S(2)}) collective-permute-start(bf16[3072,128]{1,0:T(8,128)(2,1)S(1)} %get-tuple-element.61), channel_id=1, source_target_pairs={{0,8},{1,3},{2,10},{3,5},{4,12},{5,7},{6,14},{7,1},{8,16},{9,11},{... | collective-permute-start | bytes 2359304 | tf_op jit(solution)/shard_map/ppermute | solution.py:456
  58.3 30.7 %collective-permute-start.11 = (bf16[3072,128]{1,0:T(8,128)(2,1)S(1)}, bf16[3072,128]{1,0:T(8,128)(2,1)S(1)}, u32[]{:S(2)}, u32[]{:S(2)}) collective-permute-start(bf16[3072,128]{1,0:T(8,128)(2,1)S(1)} %get-tuple-element.58), channel_id=1, source_target_pairs={{0,24},{1,7},{2,26},{3,1},{4,28},{5,3},{6,30},{7,5},{8,0},{9,15},{... | collective-permute-start | bytes 2359304 | tf_op jit(solution)/shard_map/ppermute | solution.py:456
  67.9 24.1 %collective-permute-start.12 = (bf16[3072,128]{1,0:T(8,128)(2,1)S(1)}, bf16[3072,128]{1,0:T(8,128)(2,1)S(1)}, u32[]{:S(2)}, u32[]{:S(2)}) collective-permute-start(bf16[3072,128]{1,0:T(8,128)(2,1)S(1)} %get-tuple-element.59), channel_id=1, source_target_pairs={{0,16},{1,5},{2,18},{3,7},{4,20},{5,1},{6,22},{7,3},{8,24},{9,13},... | collective-permute-start | bytes 2359304 | tf_op jit(solution)/shard_map/ppermute | solution.py:456
  81.9 20.2 %collective-permute-start.10 = (f32[2048,128]{1,0:T(8,128)S(1)}, f32[2048,128]{1,0:T(8,128)S(1)}, u32[]{:S(2)}, u32[]{:S(2)}) collective-permute-start(f32[2048,128]{1,0:T(8,128)S(1)} %get-tuple-element.56), channel_id=1, source_target_pairs={{0,2},{1,9},{2,4},{3,11},{4,6},{5,13},{6,0},{7,15},{8,10},{9,17},{... | collective-permute-start | bytes 3145736 | tf_op jit(solution)/shard_map/ppermute | solution.py:459
  83.0 19.2 %collective-permute-start.9 = (f32[2048,128]{1,0:T(8,128)S(1)}, f32[2048,128]{1,0:T(8,128)S(1)}, u32[]{:S(2)}, u32[]{:S(2)}) collective-permute-start(f32[2048,128]{1,0:T(8,128)S(1)} %get-tuple-element.55), channel_id=1, source_target_pairs={{0,6},{1,25},{2,0},{3,27},{4,2},{5,29},{6,4},{7,31},{8,14},{9,1},{... | collective-permute-start | bytes 3145736 | tf_op jit(solution)/shard_map/ppermute | solution.py:459
  97.9 15.2 %collective-permute-start.17 = (f32[2048,128]{1,0:T(8,128)S(1)}, f32[2048,128]{1,0:T(8,128)S(1)}, u32[]{:S(2)}, u32[]{:S(2)}) collective-permute-start(f32[2048,128]{1,0:T(8,128)S(1)} %get-tuple-element.69), channel_id=1, source_target_pairs={{0,6},{1,25},{2,0},{3,27},{4,2},{5,29},{6,4},{7,31},{8,14},{9,1},{... | collective-permute-start | bytes 3145736 | tf_op jit(solution)/shard_map/ppermute | solution.py:459
  100.2 18.5 %collective-permute-start.16 = (f32[2048,128]{1,0:T(8,128)S(1)}, f32[2048,128]{1,0:T(8,128)S(1)}, u32[]{:S(2)}, u32[]{:S(2)}) collective-permute-start(f32[2048,128]{1,0:T(8,128)S(1)} %get-tuple-element.67), channel_id=1, source_target_pairs={{0,2},{1,9},{2,4},{3,11},{4,6},{5,13},{6,0},{7,15},{8,10},{9,17},{... | collective-permute-start | bytes 3145736 | tf_op jit(solution)/shard_map/ppermute | solution.py:459
  121.8 10.5 %collective-permute-start.19 = (f32[528,128]{1,0:T(8,128)S(1)}, f32[528,128]{1,0:T(8,128)S(1)}, u32[]{:S(2)}, u32[]{:S(2)}) collective-permute-start(f32[528,128]{1,0:T(8,128)S(1)} %get-tuple-element.71), channel_id=1, source_target_pairs={{0,32},{32,64},{64,96},{96,0},{1,33},{33,65},{65,97},{97,1},{2,34}... | collective-permute-start | bytes 811016 | tf_op jit(solution)/shard_map/ppermute | solution.py:476
  123.7 15.2 %collective-permute-start.20 = (f32[528,128]{1,0:T(8,128)S(1)}, f32[528,128]{1,0:T(8,128)S(1)}, u32[]{:S(2)}, u32[]{:S(2)}) collective-permute-start(f32[528,128]{1,0:T(8,128)S(1)} %get-tuple-element.72), channel_id=1, source_target_pairs={{0,64},{32,96},{64,0},{96,32},{1,65},{33,97},{65,1},{97,33},{2,66}... | collective-permute-start | bytes 811016 | tf_op jit(solution)/shard_map/ppermute | solution.py:476
  127.5 11.4 %collective-permute-start.21 = (f32[528,128]{1,0:T(8,128)S(1)}, f32[528,128]{1,0:T(8,128)S(1)}, u32[]{:S(2)}, u32[]{:S(2)}) collective-permute-start(f32[528,128]{1,0:T(8,128)S(1)} %get-tuple-element.73), channel_id=1, source_target_pairs={{0,96},{32,0},{64,32},{96,64},{1,97},{33,1},{65,33},{97,65},{2,98}... | collective-permute-start | bytes 811016 | tf_op jit(solution)/shard_map/ppermute | solution.py:476
  138.9 8.5 %collective-permute-start.22 = (f32[528,128]{1,0:T(8,128)S(1)}, f32[528,128]{1,0:T(8,128)S(1)}, u32[]{:S(2)}, u32[]{:S(2)}) collective-permute-start(f32[528,128]{1,0:T(8,128)S(1)} %add_add_fusion.refs_0_), channel_id=1, source_target_pairs={{0,32},{32,64},{64,96},{96,0},{1,33},{33,65},{65,97},{97,1},{2,34}... | collective-permute-start | bytes 811016 | tf_op jit(solution)/shard_map/ppermute | solution.py:477
  141.3 14.0 %collective-permute-start.23 = (f32[528,128]{1,0:T(8,128)S(1)}, f32[528,128]{1,0:T(8,128)S(1)}, u32[]{:S(2)}, u32[]{:S(2)}) collective-permute-start(f32[528,128]{1,0:T(8,128)S(1)} %add_add_fusion.refs_0_), channel_id=1, source_target_pairs={{0,64},{32,96},{64,0},{96,32},{1,65},{33,97},{65,1},{97,33},{2,66}... | collective-permute-start | bytes 811016 | tf_op jit(solution)/shard_map/ppermute | solution.py:477
  143.4 11.9 %collective-permute-start.24 = (f32[528,128]{1,0:T(8,128)S(1)}, f32[528,128]{1,0:T(8,128)S(1)}, u32[]{:S(2)}, u32[]{:S(2)}) collective-permute-start(f32[528,128]{1,0:T(8,128)S(1)} %add_add_fusion.refs_0_), channel_id=1, source_target_pairs={{0,96},{32,0},{64,32},{96,64},{1,97},{33,1},{65,33},{97,65},{2,98}... | collective-permute-start | bytes 811016 | tf_op jit(solution)/shard_map/ppermute | solution.py:477
  (4 other events, 54.2 us)

commit v7 on v6

--- a/solution.py
+++ b/solution.py
@@ -16,6 +16,7 @@
 RUN = 24
 SLOTS = NC * RUN
 SHIFTS = (0, 1, 3, 2)
+Z_SHIFTS = (1, 3, 2)
 COPIES = 1
 GROUPS = len(SHIFTS)
 CHIP_CELLS = NC * CELL_DEV
@@ -398,7 +399,8 @@
         q = lax.rem(z + NZ - dz, NZ)
         part = parts[dz]
         sums = part[pl.ds(QPACKED, QCELL), :]
-        counts = jnp.broadcast_to(part[pl.ds(QPACKED + QCELL, QCELL), :][:, :1], (QCELL, D))
+        counts = part[pl.ds(QPACKED + QCELL, QCELL), :]
+        counts = jnp.where(lane[:QCELL] < ROWS, counts, pltpu.roll(counts, ROWS, 1))
         safe = jnp.maximum(counts, 1.0)
         mean = sums / safe
         inverse = jnp.where(counts > 0.0, 1.0 / safe, 0.0)
@@ -472,9 +474,10 @@
     swapped = lax.ppermute(other_total([other, other3]), "cell", SWAP)
     quarters = join(pos, [own, own1, swapped])
     mine = quarters[0]
-    for dz in range(1, NZ):
+    for dz in Z_SHIFTS:
         mine = mine + lax.ppermute(quarters[dz], "dp", dp_perm(dz))
-    whole = [mine] + [lax.ppermute(mine, "dp", dp_perm(dz)) for dz in range(1, NZ)]
+    whole = {dz: lax.ppermute(mine, "dp", dp_perm(dz)) for dz in Z_SHIFTS}
+    whole = [mine] + [whole[dz] for dz in range(1, NZ)]
     return tuple(finish(pos, whole))
 
 

time: 161 us -> 159 us (0.988)
    ppermute x12, starting transfers between devices: 23.7 us -> 28.7 us  [local(): lax.ppermute(run, 'cell', along(d))]
    ppermute x12, waiting for transfers between devices: 19.7 us -> 15 us  [local(): lax.ppermute(run, 'cell', along(d))]
    ppermute x6, waiting for transfers between devices: 7.02 us -> 10.8 us  [step(): return lax.ppermute(piece, 'cell', across(rel))]
    ppermute x6, starting transfers between devices: 10.9 us -> 8.87 us  [step(): return lax.ppermute(piece, 'cell', across(rel))]
    ppermute x3, starting transfers between devices: 4.88 us -> 3.12 us  [local(): whole = {dz: lax.ppermute(mine, 'dp', dp_perm(dz)) for dz in Z_SHIFTS}]
  transfers between devices with their start and end apart: 25 -> 25, of which waited for: 11 -> 13; matrix products, arithmetic and copies ran while one was open for 0% -> 0% of each run, Pallas kernels for 29% -> 29%
where the time goes in v7:
time: 159 us; the launch traced here: 156 us
  Pallas kernels  54.2 us (34%)
  waiting for transfers between devices  50.8 us (32%)
  starting transfers between devices  49.8 us (31%)
    pallas_call x5, Pallas kernels, gram(): pl.pallas_call(body, out_shape=outs, in_specs=[SMEM_SPEC] * 3 + [VMEM_SPE...  28.9 us
    ppermute x12, starting transfers between devices, local(): lax.ppermute(run, 'cell', along(d))  28.7 us
    ppermute x12, waiting for transfers between devices, local(): lax.ppermute(run, 'cell', along(d))  15 us
    pallas_call x4, Pallas kernels, gather_runs(): pl.pallas_call(body, out_shape=[jax.ShapeDtypeStruct((rows, D), vectors.d...  13.6 us
    ppermute x3, waiting for transfers between devices, local(): whole = {dz: lax.ppermute(mine, 'dp', dp_perm(dz)) for dz in Z_SHIFTS}  11.9 us
    ppermute x3, waiting for transfers between devices, local(): mine = mine + lax.ppermute(quarters[dz], 'dp', dp_perm(dz))  10.9 us
    ppermute x6, waiting for transfers between devices, step(): return lax.ppermute(piece, 'cell', across(rel))  10.8 us
    ppermute x6, starting transfers between devices, step(): return lax.ppermute(piece, 'cell', across(rel))  8.87 us
  transfers between devices with their start and end apart: 25, of which 13 were waited for; matrix products, arithmetic and copies ran while one was open for 0% of the time, Pallas kernels for 29%

profile of v7, /device:TPU:1, one launch (start us, length us, event | category | flops | bytes accessed | tf_op | source)
XLA Modules:
  0.0 156.5 jit_solution(15019299290370722468)
XLA Ops:
  1.3 4.3 %gather0.1 = (bf16[3088,128]{1,0:T(8,128)(2,1)}, bf16[3088,128]{1,0:T(8,128)(2,1)}, bf16[3088,128]{1,0:T(8,128)(2,1)}) custom-call(s32[4]{0:T(128)} %pad_add_fusion.refs_0_.pos, s32[32]{0:T(128)} %bitcast.7, bf16[24576,128]{1,0:T(8,128)(2,1)} %bitcast.13, s32[1,384]{1,0:T(1,128)} %refs_3_.1, s32[1,32]{1,0:T(1,128)} %bitcast.8), custom_call_target="tpu_custom_call" | custom-call | tf_op jit(solution)/shard_map/gather0/pallas_call | solution.py:127
  10.7 3.6 %gather1.1 = (bf16[3072,128]{1,0:T(8,128)(2,1)}, bf16[3072,128]{1,0:T(8,128)(2,1)}, bf16[3072,128]{1,0:T(8,128)(2,1)}) custom-call(s32[4]{0:T(128)S(1)} %copy-done, s32[32]{0:T(128)S(1)} %bitcast.9, bf16[24576,128]{1,0:T(8,128)(2,1)} %bitcast.14), custom_call_target="tpu_custom_call" | custom-call | tf_op jit(solution)/shard_map/gather1/pallas_call | solution.py:127
  18.8 10.2 %collective-permute-start.5 = (bf16[3072,128]{1,0:T(8,128)(2,1)}, bf16[3072,128]{1,0:T(8,128)(2,1)}, u32[]{:S(2)}, u32[]{:S(2)}) collective-permute-start(bf16[3072,128]{1,0:T(8,128)(2,1)} %get-tuple-element.47), channel_id=1, source_target_pairs={{0,16},{1,5},{2,18},{3,7},{4,20},{5,1},{6,22},{7,3},{8,24},{9,13},... | collective-permute-start | bytes 2359304 | tf_op jit(solution)/shard_map/ppermute | solution.py:458
  29.1 6.8 %lists.1 = (s32[896]{0:T(1024)S(1)}, s32[32]{0:T(128)S(1)}, s32[256]{0:T(256)S(1)}) custom-call(s32[4]{0:T(128)S(1)} %copy-done, s32[384]{0:T(512)S(1)} %reduce.own_cells, s32[32]{0:T(128)S(1)} %bitcast.10, bf16[3088,128]{1,0:T(8,128)(2,1)S(1)} %collective-permute-done.refs_0_.refs_4_, bf16[3088,128]{1,0:T(8,128)(2,1)S(1)} %collective-permute-done.1.refs_1_.refs_5_, ...), custom_call_target="tpu_custom_call" | custom-call | tf_op jit(solution)/shard_map/lists/pallas_call | solution.py:196
  36.0 2.9 %gather2.1 = (bf16[3072,128]{1,0:T(8,128)(2,1)S(1)}, bf16[3072,128]{1,0:T(8,128)(2,1)S(1)}, bf16[3072,128]{1,0:T(8,128)(2,1)S(1)}, bf16[3072,128]{1,0:T(8,128)(2,1)S(1)}, bf16[3072,128]{1,0:T(8,128)(2,1)S(1)}) custom-call(s32[4]{0:T(128)S(1)} %copy-done, s32[32]{0:T(128)S(1)} %bitcast.11, bf16[24576,128]{1,0:T(8,128)(2,1)} %bitcast.15), custom_call_target="tpu_custom_call" | custom-call | tf_op jit(solution)/shard_map/gather2/pallas_call | solution.py:127
  41.6 4.4 %collective-permute-start.8 = (bf16[3072,128]{1,0:T(8,128)(2,1)S(1)}, bf16[3072,128]{1,0:T(8,128)(2,1)S(1)}, u32[]{:S(2)}, u32[]{:S(2)}) collective-permute-start(bf16[3072,128]{1,0:T(8,128)(2,1)S(1)} %get-tuple-element.54), channel_id=1, source_target_pairs={{0,16},{1,5},{2,18},{3,7},{4,20},{5,1},{6,22},{7,3},{8,24},{9,13},... | collective-permute-start | bytes 2359304 | tf_op jit(solution)/shard_map/ppermute | solution.py:458
  46.0 6.6 %gram0.1 = (f32[2048,128]{1,0:T(8,128)S(1)}, f32[2048,128]{1,0:T(8,128)S(1)}) custom-call(s32[896]{0:T(1024)S(1)} %get-tuple-element.41.refs_0_, s32[32]{0:T(128)S(1)} %get-tuple-element.42.refs_1_, s32[256]{0:T(256)S(1)} %get-tuple-element.43.refs_2_, bf16[3072,128]{1,0:T(8,128)(2,1)S(1)} %get-tuple-element.62.refs_3_, ...), custom_call_target="tpu_custom_call" | custom-call | flops 1000000000 | bytes 10000000 | tf_op jit(solution)/shard_map/gram0/pallas_call | solution.py:315
  55.4 2.8 %gather3.1 = (bf16[3072,128]{1,0:T(8,128)(2,1)S(1)}, bf16[3072,128]{1,0:T(8,128)(2,1)S(1)}, bf16[3072,128]{1,0:T(8,128)(2,1)S(1)}, bf16[3072,128]{1,0:T(8,128)(2,1)S(1)}, bf16[3072,128]{1,0:T(8,128)(2,1)S(1)}) custom-call(s32[4]{0:T(128)S(1)} %copy-done, s32[32]{0:T(128)S(1)} %bitcast.12, bf16[24576,128]{1,0:T(8,128)(2,1)} %bitcast.16), custom_call_target="tpu_custom_call" | custom-call | tf_op jit(solution)/shard_map/gather3/pallas_call | solution.py:127
  61.0 7.0 %collective-permute-done.8.refs_6_ = bf16[3072,128]{1,0:T(8,128)(2,1)S(1)} collective-permute-done((bf16[3072,128]{1,0:T(8,128)(2,1)S(1)}, bf16[3072,128]{1,0:T(8,128)(2,1)S(1)}, u32[]{:S(2)}, u32[]{:S(2)}) %collective-permute-start.8) | collective-permute-done | bytes 786464 | tf_op jit(solution)/shard_map/ppermute | solution.py:458
  68.8 7.8 %gram2.1 = (f32[2048,128]{1,0:T(8,128)S(1)}, f32[2048,128]{1,0:T(8,128)S(1)}) custom-call(s32[896]{0:T(1024)S(1)} %get-tuple-element.41.refs_0_, s32[32]{0:T(128)S(1)} %get-tuple-element.42.refs_1_, s32[256]{0:T(256)S(1)} %get-tuple-element.43.refs_2_, bf16[3072,128]{1,0:T(8,128)(2,1)S(1)} %get-tuple-element.51.refs_3_, ...), custom_call_target="tpu_custom_call" | custom-call | flops 1000000000 | bytes 10000000 | tf_op jit(solution)/shard_map/gram2/pallas_call | solution.py:315
  76.5 5.5 %collective-permute-done.13.refs_4_ = bf16[3072,128]{1,0:T(8,128)(2,1)S(1)} collective-permute-done((bf16[3072,128]{1,0:T(8,128)(2,1)S(1)}, bf16[3072,128]{1,0:T(8,128)(2,1)S(1)}, u32[]{:S(2)}, u32[]{:S(2)}) %collective-permute-start.13) | collective-permute-done | bytes 786464 | tf_op jit(solution)/shard_map/ppermute | solution.py:458
  82.0 6.1 %collective-permute-done.14.refs_5_ = f32[2048,128]{1,0:T(8,128)S(1)} collective-permute-done((f32[2048,128]{1,0:T(8,128)S(1)}, f32[2048,128]{1,0:T(8,128)S(1)}, u32[]{:S(2)}, u32[]{:S(2)}) %collective-permute-start.14) | collective-permute-done | bytes 1048608 | tf_op jit(solution)/shard_map/ppermute | solution.py:461
  88.1 2.8 %gram3.1 = (f32[2048,128]{1,0:T(8,128)S(1)}, f32[2048,128]{1,0:T(8,128)S(1)}) custom-call(s32[896]{0:T(1024)S(1)} %get-tuple-element.41.refs_0_, s32[32]{0:T(128)S(1)} %get-tuple-element.42.refs_1_, s32[256]{0:T(256)S(1)} %get-tuple-element.43.refs_2_, bf16[3072,128]{1,0:T(8,128)(2,1)S(1)} %get-tuple-element.60.refs_3_, ...), custom_call_target="tpu_custom_call" | custom-call | flops 1000000000 | bytes 10000000 | tf_op jit(solution)/shard_map/gram3/pallas_call | solution.py:315
  91.6 4.7 %gram3b.1 = (f32[2048,128]{1,0:T(8,128)S(1)}, f32[2048,128]{1,0:T(8,128)S(1)}) custom-call(s32[896]{0:T(1024)S(1)} %get-tuple-element.41.refs_0_, s32[32]{0:T(128)S(1)} %get-tuple-element.42.refs_1_, s32[256]{0:T(256)S(1)} %get-tuple-element.43.refs_2_, bf16[3072,128]{1,0:T(8,128)(2,1)S(1)} %collective-permute-done.11.refs_3_, ...), custom_call_target="tpu_custom_call" | custom-call | flops 1000000000 | bytes 10000000 | tf_op jit(solution)/shard_map/gram3b/pallas_call | solution.py:315
  96.3 6.1 %collective-permute-start.17 = (f32[2048,128]{1,0:T(8,128)S(1)}, f32[2048,128]{1,0:T(8,128)S(1)}, u32[]{:S(2)}, u32[]{:S(2)}) collective-permute-start(f32[2048,128]{1,0:T(8,128)S(1)} %get-tuple-element.69), channel_id=1, source_target_pairs={{0,6},{1,25},{2,0},{3,27},{4,2},{5,29},{6,4},{7,31},{8,14},{9,1},{... | collective-permute-start | bytes 3145736 | tf_op jit(solution)/shard_map/ppermute | solution.py:461
  103.6 7.0 %gram1.1 = (f32[2048,128]{1,0:T(8,128)S(1)}, f32[2048,128]{1,0:T(8,128)S(1)}) custom-call(s32[896]{0:T(1024)S(1)} %get-tuple-element.41.refs_0_, s32[32]{0:T(128)S(1)} %get-tuple-element.42.refs_1_, s32[256]{0:T(256)S(1)} %get-tuple-element.43.refs_2_, bf16[3072,128]{1,0:T(8,128)(2,1)S(1)} %get-tuple-element.49.refs_3_, ...), custom_call_target="tpu_custom_call" | custom-call | flops 1000000000 | bytes 10000000 | tf_op jit(solution)/shard_map/gram1/pallas_call | solution.py:315
  110.7 3.5 %collective-permute-done.17.refs_1_ = f32[2048,128]{1,0:T(8,128)S(1)} collective-permute-done((f32[2048,128]{1,0:T(8,128)S(1)}, f32[2048,128]{1,0:T(8,128)S(1)}, u32[]{:S(2)}, u32[]{:S(2)}) %collective-permute-start.17) | collective-permute-done | bytes 1048608 | tf_op jit(solution)/shard_map/ppermute | solution.py:461
  114.5 3.6 %collective-permute-start.18 = (f32[2048,128]{1,0:T(8,128)S(1)}, f32[2048,128]{1,0:T(8,128)S(1)}, u32[]{:S(2)}, u32[]{:S(2)}) collective-permute-start(f32[2048,128]{1,0:T(8,128)S(1)} %other_total.1), channel_id=1, source_target_pairs={{0,1},{1,0},{2,3},{3,2},{4,5},{5,4},{6,7},{7,6},{8,9},{9,8},{10,11... | collective-permute-start | bytes 3145736 | tf_op jit(solution)/shard_map/ppermute | solution.py:474
  121.3 3.0 %collective-permute-start.19 = (f32[528,128]{1,0:T(8,128)S(1)}, f32[528,128]{1,0:T(8,128)S(1)}, u32[]{:S(2)}, u32[]{:S(2)}) collective-permute-start(f32[528,128]{1,0:T(8,128)S(1)} %get-tuple-element.71), channel_id=1, source_target_pairs={{0,32},{32,64},{64,96},{96,0},{1,33},{33,65},{65,97},{97,1},{2,34}... | collective-permute-start | bytes 811016 | tf_op jit(solution)/shard_map/ppermute | solution.py:478
  126.8 4.2 %collective-permute-done.19 = f32[528,128]{1,0:T(8,128)S(1)} collective-permute-done((f32[528,128]{1,0:T(8,128)S(1)}, f32[528,128]{1,0:T(8,128)S(1)}, u32[]{:S(2)}, u32[]{:S(2)}) %collective-permute-start.19) | collective-permute-done | bytes 270368 | tf_op jit(solution)/shard_map/ppermute | solution.py:478
  131.1 6.6 %collective-permute-done.21 = f32[528,128]{1,0:T(8,128)S(1)} collective-permute-done((f32[528,128]{1,0:T(8,128)S(1)}, f32[528,128]{1,0:T(8,128)S(1)}, u32[]{:S(2)}, u32[]{:S(2)}) %collective-permute-start.21) | collective-permute-done | bytes 270368 | tf_op jit(solution)/shard_map/ppermute | solution.py:478
  140.9 4.6 %collective-permute-done.22.refs_1_ = f32[528,128]{1,0:T(8,128)S(1)} collective-permute-done((f32[528,128]{1,0:T(8,128)S(1)}, f32[528,128]{1,0:T(8,128)S(1)}, u32[]{:S(2)}, u32[]{:S(2)}) %collective-permute-start.22) | collective-permute-done | bytes 270368 | tf_op jit(solution)/shard_map/ppermute | solution.py:479
  145.5 5.1 %collective-permute-done.23.refs_2_ = f32[528,128]{1,0:T(8,128)S(1)} collective-permute-done((f32[528,128]{1,0:T(8,128)S(1)}, f32[528,128]{1,0:T(8,128)S(1)}, u32[]{:S(2)}, u32[]{:S(2)}) %collective-permute-start.23) | collective-permute-done | bytes 270368 | tf_op jit(solution)/shard_map/ppermute | solution.py:479
  152.8 3.6 %finish.1 = (f32[32,128]{1,0:T(8,128)}, f32[32,128,128]{2,1,0:T(8,128)}) custom-call(s32[4]{0:T(128)S(1)} %copy-done, f32[528,128]{1,0:T(8,128)S(1)} %add_add_fusion.refs_0_, f32[528,128]{1,0:T(8,128)S(1)} %collective-permute-done.22.refs_1_, f32[528,128]{1,0:T(8,128)S(1)} %collective-permute-done.23.refs_2_, f32[528,128]{1,0:T(8,128)S(1)} %collective-permute-done.24.refs_3_), custom_call_target="tpu_custom_call" | custom-call | tf_op jit(solution)/shard_map/finish/pallas_call | solution.py:424
  (48 shorter events, 32.5 us)
Async XLA Ops:
  5.6 13.2 %collective-permute-start = (bf16[3088,128]{1,0:T(8,128)(2,1)}, bf16[3088,128]{1,0:T(8,128)(2,1)S(1)}, u32[]{:S(2)}, u32[]{:S(2)}) collective-permute-start(bf16[3088,128]{1,0:T(8,128)(2,1)} %get-tuple-element.38), channel_id=1, source_target_pairs={{0,8},{1,3},{2,10},{3,5},{4,12},{5,7},{6,14},{7,1},{8,16},{9,11},{... | collective-permute-start | bytes 2371592 | tf_op jit(solution)/shard_map/ppermute | solution.py:458
  7.5 21.6 %collective-permute-start.1 = (bf16[3088,128]{1,0:T(8,128)(2,1)}, bf16[3088,128]{1,0:T(8,128)(2,1)S(1)}, u32[]{:S(2)}, u32[]{:S(2)}) collective-permute-start(bf16[3088,128]{1,0:T(8,128)(2,1)} %get-tuple-element.39), channel_id=1, source_target_pairs={{0,24},{1,7},{2,26},{3,1},{4,28},{5,3},{6,30},{7,5},{8,0},{9,15},{... | collective-permute-start | bytes 2371592 | tf_op jit(solution)/shard_map/ppermute | solution.py:458
  9.0 20.1 %collective-permute-start.2 = (bf16[3088,128]{1,0:T(8,128)(2,1)}, bf16[3088,128]{1,0:T(8,128)(2,1)S(1)}, u32[]{:S(2)}, u32[]{:S(2)}) collective-permute-start(bf16[3088,128]{1,0:T(8,128)(2,1)} %get-tuple-element.40), channel_id=1, source_target_pairs={{0,16},{1,5},{2,18},{3,7},{4,20},{5,1},{6,22},{7,3},{8,24},{9,13},... | collective-permute-start | bytes 2371592 | tf_op jit(solution)/shard_map/ppermute | solution.py:458
  14.3 27.3 %collective-permute-start.3 = (bf16[3072,128]{1,0:T(8,128)(2,1)}, bf16[3072,128]{1,0:T(8,128)(2,1)S(1)}, u32[]{:S(2)}, u32[]{:S(2)}) collective-permute-start(bf16[3072,128]{1,0:T(8,128)(2,1)} %get-tuple-element.45), channel_id=1, source_target_pairs={{0,8},{1,3},{2,10},{3,5},{4,12},{5,7},{6,14},{7,1},{8,16},{9,11},{... | collective-permute-start | bytes 2359304 | tf_op jit(solution)/shard_map/ppermute | solution.py:458
  14.7 38.0 %collective-permute-start.4 = (bf16[3072,128]{1,0:T(8,128)(2,1)}, bf16[3072,128]{1,0:T(8,128)(2,1)}, u32[]{:S(2)}, u32[]{:S(2)}) collective-permute-start(bf16[3072,128]{1,0:T(8,128)(2,1)} %get-tuple-element.46), channel_id=1, source_target_pairs={{0,24},{1,7},{2,26},{3,1},{4,28},{5,3},{6,30},{7,5},{8,0},{9,15},{... | collective-permute-start | bytes 2359304 | tf_op jit(solution)/shard_map/ppermute | solution.py:458
  18.8 33.9 %collective-permute-start.5 = (bf16[3072,128]{1,0:T(8,128)(2,1)}, bf16[3072,128]{1,0:T(8,128)(2,1)}, u32[]{:S(2)}, u32[]{:S(2)}) collective-permute-start(bf16[3072,128]{1,0:T(8,128)(2,1)} %get-tuple-element.47), channel_id=1, source_target_pairs={{0,16},{1,5},{2,18},{3,7},{4,20},{5,1},{6,22},{7,3},{8,24},{9,13},... | collective-permute-start | bytes 2359304 | tf_op jit(solution)/shard_map/ppermute | solution.py:458
  38.8 19.4 %collective-permute-start.6 = (bf16[3072,128]{1,0:T(8,128)(2,1)S(1)}, bf16[3072,128]{1,0:T(8,128)(2,1)S(1)}, u32[]{:S(2)}, u32[]{:S(2)}) collective-permute-start(bf16[3072,128]{1,0:T(8,128)(2,1)S(1)} %get-tuple-element.52), channel_id=1, source_target_pairs={{0,8},{1,3},{2,10},{3,5},{4,12},{5,7},{6,14},{7,1},{8,16},{9,11},{... | collective-permute-start | bytes 2359304 | tf_op jit(solution)/shard_map/ppermute | solution.py:458
  38.9 19.4 %collective-permute-start.7 = (bf16[3072,128]{1,0:T(8,128)(2,1)S(1)}, bf16[3072,128]{1,0:T(8,128)(2,1)S(1)}, u32[]{:S(2)}, u32[]{:S(2)}) collective-permute-start(bf16[3072,128]{1,0:T(8,128)(2,1)S(1)} %get-tuple-element.53), channel_id=1, source_target_pairs={{0,24},{1,7},{2,26},{3,1},{4,28},{5,3},{6,30},{7,5},{8,0},{9,15},{... | collective-permute-start | bytes 2359304 | tf_op jit(solution)/shard_map/ppermute | solution.py:458
  41.6 26.5 %collective-permute-start.8 = (bf16[3072,128]{1,0:T(8,128)(2,1)S(1)}, bf16[3072,128]{1,0:T(8,128)(2,1)S(1)}, u32[]{:S(2)}, u32[]{:S(2)}) collective-permute-start(bf16[3072,128]{1,0:T(8,128)(2,1)S(1)} %get-tuple-element.54), channel_id=1, source_target_pairs={{0,16},{1,5},{2,18},{3,7},{4,20},{5,1},{6,22},{7,3},{8,24},{9,13},... | collective-permute-start | bytes 2359304 | tf_op jit(solution)/shard_map/ppermute | solution.py:458
  52.7 35.4 %collective-permute-start.14 = (f32[2048,128]{1,0:T(8,128)S(1)}, f32[2048,128]{1,0:T(8,128)S(1)}, u32[]{:S(2)}, u32[]{:S(2)}) collective-permute-start(f32[2048,128]{1,0:T(8,128)S(1)} %get-tuple-element.63), channel_id=1, source_target_pairs={{0,2},{1,9},{2,4},{3,11},{4,6},{5,13},{6,0},{7,15},{8,10},{9,17},{... | collective-permute-start | bytes 3145736 | tf_op jit(solution)/shard_map/ppermute | solution.py:461
  52.8 35.3 %collective-permute-start.15 = (f32[2048,128]{1,0:T(8,128)S(1)}, f32[2048,128]{1,0:T(8,128)S(1)}, u32[]{:S(2)}, u32[]{:S(2)}) collective-permute-start(f32[2048,128]{1,0:T(8,128)S(1)} %get-tuple-element.64), channel_id=1, source_target_pairs={{0,6},{1,25},{2,0},{3,27},{4,2},{5,29},{6,4},{7,31},{8,14},{9,1},{... | collective-permute-start | bytes 3145736 | tf_op jit(solution)/shard_map/ppermute | solution.py:461
  58.3 23.7 %collective-permute-start.13 = (bf16[3072,128]{1,0:T(8,128)(2,1)S(1)}, bf16[3072,128]{1,0:T(8,128)(2,1)S(1)}, u32[]{:S(2)}, u32[]{:S(2)}) collective-permute-start(bf16[3072,128]{1,0:T(8,128)(2,1)S(1)} %get-tuple-element.61), channel_id=1, source_target_pairs={{0,8},{1,3},{2,10},{3,5},{4,12},{5,7},{6,14},{7,1},{8,16},{9,11},{... | collective-permute-start | bytes 2359304 | tf_op jit(solution)/shard_map/ppermute | solution.py:458
  58.4 32.6 %collective-permute-start.11 = (bf16[3072,128]{1,0:T(8,128)(2,1)S(1)}, bf16[3072,128]{1,0:T(8,128)(2,1)S(1)}, u32[]{:S(2)}, u32[]{:S(2)}) collective-permute-start(bf16[3072,128]{1,0:T(8,128)(2,1)S(1)} %get-tuple-element.58), channel_id=1, source_target_pairs={{0,24},{1,7},{2,26},{3,1},{4,28},{5,3},{6,30},{7,5},{8,0},{9,15},{... | collective-permute-start | bytes 2359304 | tf_op jit(solution)/shard_map/ppermute | solution.py:458
  68.1 23.5 %collective-permute-start.12 = (bf16[3072,128]{1,0:T(8,128)(2,1)S(1)}, bf16[3072,128]{1,0:T(8,128)(2,1)S(1)}, u32[]{:S(2)}, u32[]{:S(2)}) collective-permute-start(bf16[3072,128]{1,0:T(8,128)(2,1)S(1)} %get-tuple-element.59), channel_id=1, source_target_pairs={{0,16},{1,5},{2,18},{3,7},{4,20},{5,1},{6,22},{7,3},{8,24},{9,13},... | collective-permute-start | bytes 2359304 | tf_op jit(solution)/shard_map/ppermute | solution.py:458
  82.0 21.6 %collective-permute-start.10 = (f32[2048,128]{1,0:T(8,128)S(1)}, f32[2048,128]{1,0:T(8,128)S(1)}, u32[]{:S(2)}, u32[]{:S(2)}) collective-permute-start(f32[2048,128]{1,0:T(8,128)S(1)} %get-tuple-element.56), channel_id=1, source_target_pairs={{0,2},{1,9},{2,4},{3,11},{4,6},{5,13},{6,0},{7,15},{8,10},{9,17},{... | collective-permute-start | bytes 3145736 | tf_op jit(solution)/shard_map/ppermute | solution.py:461
  88.1 15.6 %collective-permute-start.9 = (f32[2048,128]{1,0:T(8,128)S(1)}, f32[2048,128]{1,0:T(8,128)S(1)}, u32[]{:S(2)}, u32[]{:S(2)}) collective-permute-start(f32[2048,128]{1,0:T(8,128)S(1)} %get-tuple-element.55), channel_id=1, source_target_pairs={{0,6},{1,25},{2,0},{3,27},{4,2},{5,29},{6,4},{7,31},{8,14},{9,1},{... | collective-permute-start | bytes 3145736 | tf_op jit(solution)/shard_map/ppermute | solution.py:461
  96.3 17.9 %collective-permute-start.17 = (f32[2048,128]{1,0:T(8,128)S(1)}, f32[2048,128]{1,0:T(8,128)S(1)}, u32[]{:S(2)}, u32[]{:S(2)}) collective-permute-start(f32[2048,128]{1,0:T(8,128)S(1)} %get-tuple-element.69), channel_id=1, source_target_pairs={{0,6},{1,25},{2,0},{3,27},{4,2},{5,29},{6,4},{7,31},{8,14},{9,1},{... | collective-permute-start | bytes 3145736 | tf_op jit(solution)/shard_map/ppermute | solution.py:461
  102.4 15.7 %collective-permute-start.16 = (f32[2048,128]{1,0:T(8,128)S(1)}, f32[2048,128]{1,0:T(8,128)S(1)}, u32[]{:S(2)}, u32[]{:S(2)}) collective-permute-start(f32[2048,128]{1,0:T(8,128)S(1)} %get-tuple-element.67), channel_id=1, source_target_pairs={{0,2},{1,9},{2,4},{3,11},{4,6},{5,13},{6,0},{7,15},{8,10},{9,17},{... | collective-permute-start | bytes 3145736 | tf_op jit(solution)/shard_map/ppermute | solution.py:461
  121.3 9.8 %collective-permute-start.19 = (f32[528,128]{1,0:T(8,128)S(1)}, f32[528,128]{1,0:T(8,128)S(1)}, u32[]{:S(2)}, u32[]{:S(2)}) collective-permute-start(f32[528,128]{1,0:T(8,128)S(1)} %get-tuple-element.71), channel_id=1, source_target_pairs={{0,32},{32,64},{64,96},{96,0},{1,33},{33,65},{65,97},{97,1},{2,34}... | collective-permute-start | bytes 811016 | tf_op jit(solution)/shard_map/ppermute | solution.py:478
  124.2 6.8 %collective-permute-start.20 = (f32[528,128]{1,0:T(8,128)S(1)}, f32[528,128]{1,0:T(8,128)S(1)}, u32[]{:S(2)}, u32[]{:S(2)}) collective-permute-start(f32[528,128]{1,0:T(8,128)S(1)} %get-tuple-element.72), channel_id=1, source_target_pairs={{0,96},{32,0},{64,32},{96,64},{1,97},{33,1},{65,33},{97,65},{2,98}... | collective-permute-start | bytes 811016 | tf_op jit(solution)/shard_map/ppermute | solution.py:478
  125.3 12.5 %collective-permute-start.21 = (f32[528,128]{1,0:T(8,128)S(1)}, f32[528,128]{1,0:T(8,128)S(1)}, u32[]{:S(2)}, u32[]{:S(2)}) collective-permute-start(f32[528,128]{1,0:T(8,128)S(1)} %get-tuple-element.73), channel_id=1, source_target_pairs={{0,64},{32,96},{64,0},{96,32},{1,65},{33,97},{65,1},{97,33},{2,66}... | collective-permute-start | bytes 811016 | tf_op jit(solution)/shard_map/ppermute | solution.py:478
  137.8 7.7 %collective-permute-start.22 = (f32[528,128]{1,0:T(8,128)S(1)}, f32[528,128]{1,0:T(8,128)S(1)}, u32[]{:S(2)}, u32[]{:S(2)}) collective-permute-start(f32[528,128]{1,0:T(8,128)S(1)} %add_add_fusion.refs_0_), channel_id=1, source_target_pairs={{0,32},{32,64},{64,96},{96,0},{1,33},{33,65},{65,97},{97,1},{2,34}... | collective-permute-start | bytes 811016 | tf_op jit(solution)/shard_map/ppermute | solution.py:479
  138.4 12.2 %collective-permute-start.23 = (f32[528,128]{1,0:T(8,128)S(1)}, f32[528,128]{1,0:T(8,128)S(1)}, u32[]{:S(2)}, u32[]{:S(2)}) collective-permute-start(f32[528,128]{1,0:T(8,128)S(1)} %add_add_fusion.refs_0_), channel_id=1, source_target_pairs={{0,64},{32,96},{64,0},{96,32},{1,65},{33,97},{65,1},{97,33},{2,66}... | collective-permute-start | bytes 811016 | tf_op jit(solution)/shard_map/ppermute | solution.py:479
  140.5 12.4 %collective-permute-start.24 = (f32[528,128]{1,0:T(8,128)S(1)}, f32[528,128]{1,0:T(8,128)S(1)}, u32[]{:S(2)}, u32[]{:S(2)}) collective-permute-start(f32[528,128]{1,0:T(8,128)S(1)} %add_add_fusion.refs_0_), channel_id=1, source_target_pairs={{0,96},{32,0},{64,32},{96,64},{1,97},{33,1},{65,33},{97,65},{2,98}... | collective-permute-start | bytes 811016 | tf_op jit(solution)/shard_map/ppermute | solution.py:479
  (4 other events, 53.0 us)

commit v8 on v7

--- a/solution.py
+++ b/solution.py
@@ -467,8 +467,8 @@
     fore, back = step(1, fore), step(3, back)
     left, right = grams(2)
     other1, own3 = step(1, left), step(3, right)
-    left, right = grams(3, (fore,), (back,), members=(0, 1))
-    left, right = grams(3, (left,), (right,), members=(2, 3), counted=False)
+    left, right = grams(3, (fore,), (back,), members=(0, 1, 2))
+    left, right = grams(3, (left,), (right,), members=(3,), counted=False)
     own1, other3 = step(1, left), step(3, right)
     own, other = grams(1, (own3,), (other1,))
     swapped = lax.ppermute(other_total([other, other3]), "cell", SWAP)

time: 159 us -> 158 us (level)
    ppermute x6, starting transfers between devices: 8.87 us -> 13.7 us  [step(): return lax.ppermute(piece, 'cell', across(rel))]
    ppermute x6, waiting for transfers between devices: 10.8 us -> 6.05 us  [step(): return lax.ppermute(piece, 'cell', across(rel))]
    ppermute x12, starting transfers between devices: 28.7 us -> 24.1 us  [local(): lax.ppermute(run, 'cell', along(d))]
    ppermute x12, waiting for transfers between devices: 15 us -> 19 us  [local(): lax.ppermute(run, 'cell', along(d))]
  transfers between devices with their start and end apart: 25 -> 25, of which waited for: 13 -> 11; matrix products, arithmetic and copies ran while one was open for 0% -> 0% of each run, Pallas kernels for 29% -> 29%
where the time goes in v8:
time: 158 us; the launch traced here: 156 us
  Pallas kernels  53.5 us (34%)
  waiting for transfers between devices  51.2 us (32%)
  starting transfers between devices  50 us (32%)
    pallas_call x5, Pallas kernels, gram(): pl.pallas_call(body, out_shape=outs, in_specs=[SMEM_SPEC] * 3 + [VMEM_SPE...  28.9 us
    ppermute x12, starting transfers between devices, local(): lax.ppermute(run, 'cell', along(d))  24.1 us
    ppermute x12, waiting for transfers between devices, local(): lax.ppermute(run, 'cell', along(d))  19 us
    ppermute x6, starting transfers between devices, step(): return lax.ppermute(piece, 'cell', across(rel))  13.7 us
    pallas_call x4, Pallas kernels, gather_runs(): pl.pallas_call(body, out_shape=[jax.ShapeDtypeStruct((rows, D), vectors.d...  13 us
    ppermute x3, waiting for transfers between devices, local(): whole = {dz: lax.ppermute(mine, 'dp', dp_perm(dz)) for dz in Z_SHIFTS}  11.9 us
    ppermute x3, waiting for transfers between devices, local(): mine = mine + lax.ppermute(quarters[dz], 'dp', dp_perm(dz))  11.9 us
    pallas_call x1, Pallas kernels, make_lists(): pl.pallas_call(lists_body, out_shape=[jax.ShapeDtypeStruct((LIST,), I32),...  6.71 us
  transfers between devices with their start and end apart: 25, of which 11 were waited for; matrix products, arithmetic and copies ran while one was open for 0% of the time, Pallas kernels for 29%

profile of v8, /device:TPU:1, one launch (start us, length us, event | category | flops | bytes accessed | tf_op | source)
XLA Modules:
  0.0 156.3 jit_solution(17478962497979725945)
XLA Ops:
  1.3 3.9 %gather0.1 = (bf16[3088,128]{1,0:T(8,128)(2,1)}, bf16[3088,128]{1,0:T(8,128)(2,1)}, bf16[3088,128]{1,0:T(8,128)(2,1)}) custom-call(s32[4]{0:T(128)} %pad_add_fusion.refs_0_.pos, s32[32]{0:T(128)} %bitcast.7, bf16[24576,128]{1,0:T(8,128)(2,1)} %bitcast.13, s32[1,384]{1,0:T(1,128)} %refs_3_.1, s32[1,32]{1,0:T(1,128)} %bitcast.8), custom_call_target="tpu_custom_call" | custom-call | tf_op jit(solution)/shard_map/gather0/pallas_call | solution.py:127
  10.6 3.6 %gather1.1 = (bf16[3072,128]{1,0:T(8,128)(2,1)}, bf16[3072,128]{1,0:T(8,128)(2,1)}, bf16[3072,128]{1,0:T(8,128)(2,1)}) custom-call(s32[4]{0:T(128)S(1)} %copy-done, s32[32]{0:T(128)S(1)} %bitcast.9, bf16[24576,128]{1,0:T(8,128)(2,1)} %bitcast.14), custom_call_target="tpu_custom_call" | custom-call | tf_op jit(solution)/shard_map/gather1/pallas_call | solution.py:127
  18.8 10.1 %collective-permute-start.5 = (bf16[3072,128]{1,0:T(8,128)(2,1)}, bf16[3072,128]{1,0:T(8,128)(2,1)}, u32[]{:S(2)}, u32[]{:S(2)}) collective-permute-start(bf16[3072,128]{1,0:T(8,128)(2,1)} %get-tuple-element.47), channel_id=1, source_target_pairs={{0,16},{1,5},{2,18},{3,7},{4,20},{5,1},{6,22},{7,3},{8,24},{9,13},... | collective-permute-start | bytes 2359304 | tf_op jit(solution)/shard_map/ppermute | solution.py:458
  29.0 6.7 %lists.1 = (s32[896]{0:T(1024)S(1)}, s32[32]{0:T(128)S(1)}, s32[256]{0:T(256)S(1)}) custom-call(s32[4]{0:T(128)S(1)} %copy-done, s32[384]{0:T(512)S(1)} %reduce.own_cells, s32[32]{0:T(128)S(1)} %bitcast.10, bf16[3088,128]{1,0:T(8,128)(2,1)S(1)} %collective-permute-done.refs_0_.refs_4_, bf16[3088,128]{1,0:T(8,128)(2,1)S(1)} %collective-permute-done.1.refs_1_.refs_5_, ...), custom_call_target="tpu_custom_call" | custom-call | tf_op jit(solution)/shard_map/lists/pallas_call | solution.py:196
  35.7 2.8 %gather2.1 = (bf16[3072,128]{1,0:T(8,128)(2,1)S(1)}, bf16[3072,128]{1,0:T(8,128)(2,1)S(1)}, bf16[3072,128]{1,0:T(8,128)(2,1)S(1)}, bf16[3072,128]{1,0:T(8,128)(2,1)S(1)}, bf16[3072,128]{1,0:T(8,128)(2,1)S(1)}) custom-call(s32[4]{0:T(128)S(1)} %copy-done, s32[32]{0:T(128)S(1)} %bitcast.11, bf16[24576,128]{1,0:T(8,128)(2,1)} %bitcast.15), custom_call_target="tpu_custom_call" | custom-call | tf_op jit(solution)/shard_map/gather2/pallas_call | solution.py:127
  41.2 6.6 %gram0.1 = (f32[2048,128]{1,0:T(8,128)S(1)}, f32[2048,128]{1,0:T(8,128)S(1)}) custom-call(s32[896]{0:T(1024)S(1)} %get-tuple-element.41.refs_0_, s32[32]{0:T(128)S(1)} %get-tuple-element.42.refs_1_, s32[256]{0:T(256)S(1)} %get-tuple-element.43.refs_2_, bf16[3072,128]{1,0:T(8,128)(2,1)S(1)} %get-tuple-element.62.refs_3_, ...), custom_call_target="tpu_custom_call" | custom-call | flops 1000000000 | bytes 10000000 | tf_op jit(solution)/shard_map/gram0/pallas_call | solution.py:315
  47.9 6.4 %collective-permute-start.14 = (f32[2048,128]{1,0:T(8,128)S(1)}, f32[2048,128]{1,0:T(8,128)S(1)}, u32[]{:S(2)}, u32[]{:S(2)}) collective-permute-start(f32[2048,128]{1,0:T(8,128)S(1)} %get-tuple-element.63), channel_id=1, source_target_pairs={{0,2},{1,9},{2,4},{3,11},{4,6},{5,13},{6,0},{7,15},{8,10},{9,17},{... | collective-permute-start | bytes 3145736 | tf_op jit(solution)/shard_map/ppermute | solution.py:461
  54.3 2.7 %gather3.1 = (bf16[3072,128]{1,0:T(8,128)(2,1)S(1)}, bf16[3072,128]{1,0:T(8,128)(2,1)S(1)}, bf16[3072,128]{1,0:T(8,128)(2,1)S(1)}, bf16[3072,128]{1,0:T(8,128)(2,1)S(1)}, bf16[3072,128]{1,0:T(8,128)(2,1)S(1)}) custom-call(s32[4]{0:T(128)S(1)} %copy-done, s32[32]{0:T(128)S(1)} %bitcast.12, bf16[24576,128]{1,0:T(8,128)(2,1)} %bitcast.16), custom_call_target="tpu_custom_call" | custom-call | tf_op jit(solution)/shard_map/gather3/pallas_call | solution.py:127
  57.2 3.2 %collective-permute-start.13 = (bf16[3072,128]{1,0:T(8,128)(2,1)S(1)}, bf16[3072,128]{1,0:T(8,128)(2,1)S(1)}, u32[]{:S(2)}, u32[]{:S(2)}) collective-permute-start(bf16[3072,128]{1,0:T(8,128)(2,1)S(1)} %get-tuple-element.61), channel_id=1, source_target_pairs={{0,24},{1,7},{2,26},{3,1},{4,28},{5,3},{6,30},{7,5},{8,0},{9,15},{... | collective-permute-start | bytes 2359304 | tf_op jit(solution)/shard_map/ppermute | solution.py:458
  60.3 9.1 %collective-permute-done.8.refs_6_ = bf16[3072,128]{1,0:T(8,128)(2,1)S(1)} collective-permute-done((bf16[3072,128]{1,0:T(8,128)(2,1)S(1)}, bf16[3072,128]{1,0:T(8,128)(2,1)S(1)}, u32[]{:S(2)}, u32[]{:S(2)}) %collective-permute-start.8) | collective-permute-done | bytes 786464 | tf_op jit(solution)/shard_map/ppermute | solution.py:458
  69.4 5.9 %gram2.1 = (f32[2048,128]{1,0:T(8,128)S(1)}, f32[2048,128]{1,0:T(8,128)S(1)}) custom-call(s32[896]{0:T(1024)S(1)} %get-tuple-element.41.refs_0_, s32[32]{0:T(128)S(1)} %get-tuple-element.42.refs_1_, s32[256]{0:T(256)S(1)} %get-tuple-element.43.refs_2_, bf16[3072,128]{1,0:T(8,128)(2,1)S(1)} %get-tuple-element.51.refs_3_, ...), custom_call_target="tpu_custom_call" | custom-call | flops 1000000000 | bytes 10000000 | tf_op jit(solution)/shard_map/gram2/pallas_call | solution.py:315
  75.2 6.7 %collective-permute-done.12.refs_4_ = bf16[3072,128]{1,0:T(8,128)(2,1)S(1)} collective-permute-done((bf16[3072,128]{1,0:T(8,128)(2,1)S(1)}, bf16[3072,128]{1,0:T(8,128)(2,1)S(1)}, u32[]{:S(2)}, u32[]{:S(2)}) %collective-permute-start.12) | collective-permute-done | bytes 786464 | tf_op jit(solution)/shard_map/ppermute | solution.py:458
  84.6 5.9 %gram3.1 = (f32[2048,128]{1,0:T(8,128)S(1)}, f32[2048,128]{1,0:T(8,128)S(1)}) custom-call(s32[896]{0:T(1024)S(1)} %get-tuple-element.41.refs_0_, s32[32]{0:T(128)S(1)} %get-tuple-element.42.refs_1_, s32[256]{0:T(256)S(1)} %get-tuple-element.43.refs_2_, bf16[3072,128]{1,0:T(8,128)(2,1)S(1)} %get-tuple-element.59.refs_3_, ...), custom_call_target="tpu_custom_call" | custom-call | flops 1000000000 | bytes 10000000 | tf_op jit(solution)/shard_map/gram3/pallas_call | solution.py:315
  91.8 2.8 %gram3b.1 = (f32[2048,128]{1,0:T(8,128)S(1)}, f32[2048,128]{1,0:T(8,128)S(1)}) custom-call(s32[896]{0:T(1024)S(1)} %get-tuple-element.41.refs_0_, s32[32]{0:T(128)S(1)} %get-tuple-element.42.refs_1_, s32[256]{0:T(256)S(1)} %get-tuple-element.43.refs_2_, bf16[3072,128]{1,0:T(8,128)(2,1)S(1)} %collective-permute-done.11.refs_3_, ...), custom_call_target="tpu_custom_call" | custom-call | flops 1000000000 | bytes 10000000 | tf_op jit(solution)/shard_map/gram3b/pallas_call | solution.py:315
  94.6 4.6 %collective-permute-start.17 = (f32[2048,128]{1,0:T(8,128)S(1)}, f32[2048,128]{1,0:T(8,128)S(1)}, u32[]{:S(2)}, u32[]{:S(2)}) collective-permute-start(f32[2048,128]{1,0:T(8,128)S(1)} %get-tuple-element.69), channel_id=1, source_target_pairs={{0,6},{1,25},{2,0},{3,27},{4,2},{5,29},{6,4},{7,31},{8,14},{9,1},{... | collective-permute-start | bytes 3145736 | tf_op jit(solution)/shard_map/ppermute | solution.py:461
  99.2 3.4 %collective-permute-done.10.refs_8_ = f32[2048,128]{1,0:T(8,128)S(1)} collective-permute-done((f32[2048,128]{1,0:T(8,128)S(1)}, f32[2048,128]{1,0:T(8,128)S(1)}, u32[]{:S(2)}, u32[]{:S(2)}) %collective-permute-start.10) | collective-permute-done | bytes 1048608 | tf_op jit(solution)/shard_map/ppermute | solution.py:461
  102.7 7.8 %gram1.1 = (f32[2048,128]{1,0:T(8,128)S(1)}, f32[2048,128]{1,0:T(8,128)S(1)}) custom-call(s32[896]{0:T(1024)S(1)} %get-tuple-element.41.refs_0_, s32[32]{0:T(128)S(1)} %get-tuple-element.42.refs_1_, s32[256]{0:T(256)S(1)} %get-tuple-element.43.refs_2_, bf16[3072,128]{1,0:T(8,128)(2,1)S(1)} %get-tuple-element.49.refs_3_, ...), custom_call_target="tpu_custom_call" | custom-call | flops 1000000000 | bytes 10000000 | tf_op jit(solution)/shard_map/gram1/pallas_call | solution.py:315
  113.5 2.8 %collective-permute-start.18 = (f32[2048,128]{1,0:T(8,128)S(1)}, f32[2048,128]{1,0:T(8,128)S(1)}, u32[]{:S(2)}, u32[]{:S(2)}) collective-permute-start(f32[2048,128]{1,0:T(8,128)S(1)} %other_total.1), channel_id=1, source_target_pairs={{0,1},{1,0},{2,3},{3,2},{4,5},{5,4},{6,7},{7,6},{8,9},{9,8},{10,11... | collective-permute-start | bytes 3145736 | tf_op jit(solution)/shard_map/ppermute | solution.py:474
  121.7 2.7 %collective-permute-start.20 = (f32[528,128]{1,0:T(8,128)S(1)}, f32[528,128]{1,0:T(8,128)S(1)}, u32[]{:S(2)}, u32[]{:S(2)}) collective-permute-start(f32[528,128]{1,0:T(8,128)S(1)} %get-tuple-element.72), channel_id=1, source_target_pairs={{0,96},{32,0},{64,32},{96,64},{1,97},{33,1},{65,33},{97,65},{2,98}... | collective-permute-start | bytes 811016 | tf_op jit(solution)/shard_map/ppermute | solution.py:478
  125.7 5.2 %collective-permute-done.19 = f32[528,128]{1,0:T(8,128)S(1)} collective-permute-done((f32[528,128]{1,0:T(8,128)S(1)}, f32[528,128]{1,0:T(8,128)S(1)}, u32[]{:S(2)}, u32[]{:S(2)}) %collective-permute-start.19) | collective-permute-done | bytes 270368 | tf_op jit(solution)/shard_map/ppermute | solution.py:478
  130.9 6.6 %collective-permute-done.21 = f32[528,128]{1,0:T(8,128)S(1)} collective-permute-done((f32[528,128]{1,0:T(8,128)S(1)}, f32[528,128]{1,0:T(8,128)S(1)}, u32[]{:S(2)}, u32[]{:S(2)}) %collective-permute-start.21) | collective-permute-done | bytes 270368 | tf_op jit(solution)/shard_map/ppermute | solution.py:478
  140.7 7.9 %collective-permute-done.22.refs_1_ = f32[528,128]{1,0:T(8,128)S(1)} collective-permute-done((f32[528,128]{1,0:T(8,128)S(1)}, f32[528,128]{1,0:T(8,128)S(1)}, u32[]{:S(2)}, u32[]{:S(2)}) %collective-permute-start.22) | collective-permute-done | bytes 270368 | tf_op jit(solution)/shard_map/ppermute | solution.py:479
  148.6 4.0 %collective-permute-done.24.refs_3_ = f32[528,128]{1,0:T(8,128)S(1)} collective-permute-done((f32[528,128]{1,0:T(8,128)S(1)}, f32[528,128]{1,0:T(8,128)S(1)}, u32[]{:S(2)}, u32[]{:S(2)}) %collective-permute-start.24) | collective-permute-done | bytes 270368 | tf_op jit(solution)/shard_map/ppermute | solution.py:479
  152.7 3.6 %finish.1 = (f32[32,128]{1,0:T(8,128)}, f32[32,128,128]{2,1,0:T(8,128)}) custom-call(s32[4]{0:T(128)S(1)} %copy-done, f32[528,128]{1,0:T(8,128)S(1)} %add_add_fusion.refs_0_, f32[528,128]{1,0:T(8,128)S(1)} %collective-permute-done.22.refs_1_, f32[528,128]{1,0:T(8,128)S(1)} %collective-permute-done.23.refs_2_, f32[528,128]{1,0:T(8,128)S(1)} %collective-permute-done.24.refs_3_), custom_call_target="tpu_custom_call" | custom-call | tf_op jit(solution)/shard_map/finish/pallas_call | solution.py:424
  (48 shorter events, 30.4 us)
Async XLA Ops:
  5.3 13.6 %collective-permute-start = (bf16[3088,128]{1,0:T(8,128)(2,1)}, bf16[3088,128]{1,0:T(8,128)(2,1)S(1)}, u32[]{:S(2)}, u32[]{:S(2)}) collective-permute-start(bf16[3088,128]{1,0:T(8,128)(2,1)} %get-tuple-element.38), channel_id=1, source_target_pairs={{0,8},{1,3},{2,10},{3,5},{4,12},{5,7},{6,14},{7,1},{8,16},{9,11},{... | collective-permute-start | bytes 2371592 | tf_op jit(solution)/shard_map/ppermute | solution.py:458
  7.5 21.5 %collective-permute-start.1 = (bf16[3088,128]{1,0:T(8,128)(2,1)}, bf16[3088,128]{1,0:T(8,128)(2,1)S(1)}, u32[]{:S(2)}, u32[]{:S(2)}) collective-permute-start(bf16[3088,128]{1,0:T(8,128)(2,1)} %get-tuple-element.39), channel_id=1, source_target_pairs={{0,24},{1,7},{2,26},{3,1},{4,28},{5,3},{6,30},{7,5},{8,0},{9,15},{... | collective-permute-start | bytes 2371592 | tf_op jit(solution)/shard_map/ppermute | solution.py:458
  9.0 20.0 %collective-permute-start.2 = (bf16[3088,128]{1,0:T(8,128)(2,1)}, bf16[3088,128]{1,0:T(8,128)(2,1)S(1)}, u32[]{:S(2)}, u32[]{:S(2)}) collective-permute-start(bf16[3088,128]{1,0:T(8,128)(2,1)} %get-tuple-element.40), channel_id=1, source_target_pairs={{0,16},{1,5},{2,18},{3,7},{4,20},{5,1},{6,22},{7,3},{8,24},{9,13},... | collective-permute-start | bytes 2371592 | tf_op jit(solution)/shard_map/ppermute | solution.py:458
  14.2 27.0 %collective-permute-start.3 = (bf16[3072,128]{1,0:T(8,128)(2,1)}, bf16[3072,128]{1,0:T(8,128)(2,1)S(1)}, u32[]{:S(2)}, u32[]{:S(2)}) collective-permute-start(bf16[3072,128]{1,0:T(8,128)(2,1)} %get-tuple-element.45), channel_id=1, source_target_pairs={{0,8},{1,3},{2,10},{3,5},{4,12},{5,7},{6,14},{7,1},{8,16},{9,11},{... | collective-permute-start | bytes 2359304 | tf_op jit(solution)/shard_map/ppermute | solution.py:458
  14.6 33.2 %collective-permute-start.4 = (bf16[3072,128]{1,0:T(8,128)(2,1)}, bf16[3072,128]{1,0:T(8,128)(2,1)}, u32[]{:S(2)}, u32[]{:S(2)}) collective-permute-start(bf16[3072,128]{1,0:T(8,128)(2,1)} %get-tuple-element.46), channel_id=1, source_target_pairs={{0,24},{1,7},{2,26},{3,1},{4,28},{5,3},{6,30},{7,5},{8,0},{9,15},{... | collective-permute-start | bytes 2359304 | tf_op jit(solution)/shard_map/ppermute | solution.py:458
  18.8 35.5 %collective-permute-start.5 = (bf16[3072,128]{1,0:T(8,128)(2,1)}, bf16[3072,128]{1,0:T(8,128)(2,1)}, u32[]{:S(2)}, u32[]{:S(2)}) collective-permute-start(bf16[3072,128]{1,0:T(8,128)(2,1)} %get-tuple-element.47), channel_id=1, source_target_pairs={{0,16},{1,5},{2,18},{3,7},{4,20},{5,1},{6,22},{7,3},{8,24},{9,13},... | collective-permute-start | bytes 2359304 | tf_op jit(solution)/shard_map/ppermute | solution.py:458
  38.5 18.6 %collective-permute-start.6 = (bf16[3072,128]{1,0:T(8,128)(2,1)S(1)}, bf16[3072,128]{1,0:T(8,128)(2,1)S(1)}, u32[]{:S(2)}, u32[]{:S(2)}) collective-permute-start(bf16[3072,128]{1,0:T(8,128)(2,1)S(1)} %get-tuple-element.52), channel_id=1, source_target_pairs={{0,8},{1,3},{2,10},{3,5},{4,12},{5,7},{6,14},{7,1},{8,16},{9,11},{... | collective-permute-start | bytes 2359304 | tf_op jit(solution)/shard_map/ppermute | solution.py:458
  39.3 17.8 %collective-permute-start.7 = (bf16[3072,128]{1,0:T(8,128)(2,1)S(1)}, bf16[3072,128]{1,0:T(8,128)(2,1)S(1)}, u32[]{:S(2)}, u32[]{:S(2)}) collective-permute-start(bf16[3072,128]{1,0:T(8,128)(2,1)S(1)} %get-tuple-element.53), channel_id=1, source_target_pairs={{0,24},{1,7},{2,26},{3,1},{4,28},{5,3},{6,30},{7,5},{8,0},{9,15},{... | collective-permute-start | bytes 2359304 | tf_op jit(solution)/shard_map/ppermute | solution.py:458
  41.2 28.1 %collective-permute-start.8 = (bf16[3072,128]{1,0:T(8,128)(2,1)S(1)}, bf16[3072,128]{1,0:T(8,128)(2,1)S(1)}, u32[]{:S(2)}, u32[]{:S(2)}) collective-permute-start(bf16[3072,128]{1,0:T(8,128)(2,1)S(1)} %get-tuple-element.54), channel_id=1, source_target_pairs={{0,16},{1,5},{2,18},{3,7},{4,20},{5,1},{6,22},{7,3},{8,24},{9,13},... | collective-permute-start | bytes 2359304 | tf_op jit(solution)/shard_map/ppermute | solution.py:458
  47.9 36.7 %collective-permute-start.14 = (f32[2048,128]{1,0:T(8,128)S(1)}, f32[2048,128]{1,0:T(8,128)S(1)}, u32[]{:S(2)}, u32[]{:S(2)}) collective-permute-start(f32[2048,128]{1,0:T(8,128)S(1)} %get-tuple-element.63), channel_id=1, source_target_pairs={{0,2},{1,9},{2,4},{3,11},{4,6},{5,13},{6,0},{7,15},{8,10},{9,17},{... | collective-permute-start | bytes 3145736 | tf_op jit(solution)/shard_map/ppermute | solution.py:461
  54.3 30.3 %collective-permute-start.15 = (f32[2048,128]{1,0:T(8,128)S(1)}, f32[2048,128]{1,0:T(8,128)S(1)}, u32[]{:S(2)}, u32[]{:S(2)}) collective-permute-start(f32[2048,128]{1,0:T(8,128)S(1)} %get-tuple-element.64), channel_id=1, source_target_pairs={{0,6},{1,25},{2,0},{3,27},{4,2},{5,29},{6,4},{7,31},{8,14},{9,1},{... | collective-permute-start | bytes 3145736 | tf_op jit(solution)/shard_map/ppermute | solution.py:461
  57.1 24.8 %collective-permute-start.12 = (bf16[3072,128]{1,0:T(8,128)(2,1)S(1)}, bf16[3072,128]{1,0:T(8,128)(2,1)S(1)}, u32[]{:S(2)}, u32[]{:S(2)}) collective-permute-start(bf16[3072,128]{1,0:T(8,128)(2,1)S(1)} %get-tuple-element.60), channel_id=1, source_target_pairs={{0,8},{1,3},{2,10},{3,5},{4,12},{5,7},{6,14},{7,1},{8,16},{9,11},{... | collective-permute-start | bytes 2359304 | tf_op jit(solution)/shard_map/ppermute | solution.py:458
  57.2 25.9 %collective-permute-start.13 = (bf16[3072,128]{1,0:T(8,128)(2,1)S(1)}, bf16[3072,128]{1,0:T(8,128)(2,1)S(1)}, u32[]{:S(2)}, u32[]{:S(2)}) collective-permute-start(bf16[3072,128]{1,0:T(8,128)(2,1)S(1)} %get-tuple-element.61), channel_id=1, source_target_pairs={{0,24},{1,7},{2,26},{3,1},{4,28},{5,3},{6,30},{7,5},{8,0},{9,15},{... | collective-permute-start | bytes 2359304 | tf_op jit(solution)/shard_map/ppermute | solution.py:458
  69.4 22.5 %collective-permute-start.11 = (bf16[3072,128]{1,0:T(8,128)(2,1)S(1)}, bf16[3072,128]{1,0:T(8,128)(2,1)S(1)}, u32[]{:S(2)}, u32[]{:S(2)}) collective-permute-start(bf16[3072,128]{1,0:T(8,128)(2,1)S(1)} %get-tuple-element.58), channel_id=1, source_target_pairs={{0,16},{1,5},{2,18},{3,7},{4,20},{5,1},{6,22},{7,3},{8,24},{9,13},... | collective-permute-start | bytes 2359304 | tf_op jit(solution)/shard_map/ppermute | solution.py:458
  81.9 20.7 %collective-permute-start.10 = (f32[2048,128]{1,0:T(8,128)S(1)}, f32[2048,128]{1,0:T(8,128)S(1)}, u32[]{:S(2)}, u32[]{:S(2)}) collective-permute-start(f32[2048,128]{1,0:T(8,128)S(1)} %get-tuple-element.56), channel_id=1, source_target_pairs={{0,2},{1,9},{2,4},{3,11},{4,6},{5,13},{6,0},{7,15},{8,10},{9,17},{... | collective-permute-start | bytes 3145736 | tf_op jit(solution)/shard_map/ppermute | solution.py:461
  83.1 19.6 %collective-permute-start.9 = (f32[2048,128]{1,0:T(8,128)S(1)}, f32[2048,128]{1,0:T(8,128)S(1)}, u32[]{:S(2)}, u32[]{:S(2)}) collective-permute-start(f32[2048,128]{1,0:T(8,128)S(1)} %get-tuple-element.55), channel_id=1, source_target_pairs={{0,6},{1,25},{2,0},{3,27},{4,2},{5,29},{6,4},{7,31},{8,14},{9,1},{... | collective-permute-start | bytes 3145736 | tf_op jit(solution)/shard_map/ppermute | solution.py:461
  94.6 18.4 %collective-permute-start.17 = (f32[2048,128]{1,0:T(8,128)S(1)}, f32[2048,128]{1,0:T(8,128)S(1)}, u32[]{:S(2)}, u32[]{:S(2)}) collective-permute-start(f32[2048,128]{1,0:T(8,128)S(1)} %get-tuple-element.69), channel_id=1, source_target_pairs={{0,6},{1,25},{2,0},{3,27},{4,2},{5,29},{6,4},{7,31},{8,14},{9,1},{... | collective-permute-start | bytes 3145736 | tf_op jit(solution)/shard_map/ppermute | solution.py:461
  99.2 17.0 %collective-permute-start.16 = (f32[2048,128]{1,0:T(8,128)S(1)}, f32[2048,128]{1,0:T(8,128)S(1)}, u32[]{:S(2)}, u32[]{:S(2)}) collective-permute-start(f32[2048,128]{1,0:T(8,128)S(1)} %get-tuple-element.67), channel_id=1, source_target_pairs={{0,2},{1,9},{2,4},{3,11},{4,6},{5,13},{6,0},{7,15},{8,10},{9,17},{... | collective-permute-start | bytes 3145736 | tf_op jit(solution)/shard_map/ppermute | solution.py:461
  119.4 11.5 %collective-permute-start.19 = (f32[528,128]{1,0:T(8,128)S(1)}, f32[528,128]{1,0:T(8,128)S(1)}, u32[]{:S(2)}, u32[]{:S(2)}) collective-permute-start(f32[528,128]{1,0:T(8,128)S(1)} %get-tuple-element.71), channel_id=1, source_target_pairs={{0,32},{32,64},{64,96},{96,0},{1,33},{33,65},{65,97},{97,1},{2,34}... | collective-permute-start | bytes 811016 | tf_op jit(solution)/shard_map/ppermute | solution.py:478
  121.7 9.2 %collective-permute-start.20 = (f32[528,128]{1,0:T(8,128)S(1)}, f32[528,128]{1,0:T(8,128)S(1)}, u32[]{:S(2)}, u32[]{:S(2)}) collective-permute-start(f32[528,128]{1,0:T(8,128)S(1)} %get-tuple-element.72), channel_id=1, source_target_pairs={{0,96},{32,0},{64,32},{96,64},{1,97},{33,1},{65,33},{97,65},{2,98}... | collective-permute-start | bytes 811016 | tf_op jit(solution)/shard_map/ppermute | solution.py:478
  124.4 13.1 %collective-permute-start.21 = (f32[528,128]{1,0:T(8,128)S(1)}, f32[528,128]{1,0:T(8,128)S(1)}, u32[]{:S(2)}, u32[]{:S(2)}) collective-permute-start(f32[528,128]{1,0:T(8,128)S(1)} %get-tuple-element.73), channel_id=1, source_target_pairs={{0,64},{32,96},{64,0},{96,32},{1,65},{33,97},{65,1},{97,33},{2,66}... | collective-permute-start | bytes 811016 | tf_op jit(solution)/shard_map/ppermute | solution.py:478
  137.6 11.0 %collective-permute-start.22 = (f32[528,128]{1,0:T(8,128)S(1)}, f32[528,128]{1,0:T(8,128)S(1)}, u32[]{:S(2)}, u32[]{:S(2)}) collective-permute-start(f32[528,128]{1,0:T(8,128)S(1)} %add_add_fusion.refs_0_), channel_id=1, source_target_pairs={{0,32},{32,64},{64,96},{96,0},{1,33},{33,65},{65,97},{97,1},{2,34}... | collective-permute-start | bytes 811016 | tf_op jit(solution)/shard_map/ppermute | solution.py:479
  138.2 10.4 %collective-permute-start.23 = (f32[528,128]{1,0:T(8,128)S(1)}, f32[528,128]{1,0:T(8,128)S(1)}, u32[]{:S(2)}, u32[]{:S(2)}) collective-permute-start(f32[528,128]{1,0:T(8,128)S(1)} %add_add_fusion.refs_0_), channel_id=1, source_target_pairs={{0,64},{32,96},{64,0},{96,32},{1,65},{33,97},{65,1},{97,33},{2,66}... | collective-permute-start | bytes 811016 | tf_op jit(solution)/shard_map/ppermute | solution.py:479
  139.0 13.7 %collective-permute-start.24 = (f32[528,128]{1,0:T(8,128)S(1)}, f32[528,128]{1,0:T(8,128)S(1)}, u32[]{:S(2)}, u32[]{:S(2)}) collective-permute-start(f32[528,128]{1,0:T(8,128)S(1)} %add_add_fusion.refs_0_), channel_id=1, source_target_pairs={{0,96},{32,0},{64,32},{96,64},{1,97},{33,1},{65,33},{97,65},{2,98}... | collective-permute-start | bytes 811016 | tf_op jit(solution)/shard_map/ppermute | solution.py:479
  (4 other events, 51.8 us)

commit v9 on v8

--- a/solution.py
+++ b/solution.py
@@ -465,7 +465,8 @@
 
     fore, back = grams(0)
     fore, back = step(1, fore), step(3, back)
-    left, right = grams(2)
+    left, right = grams(2, members=(0, 1, 2))
+    left, right = grams(2, (left,), (right,), members=(3,), counted=False)
     other1, own3 = step(1, left), step(3, right)
     left, right = grams(3, (fore,), (back,), members=(0, 1, 2))
     left, right = grams(3, (left,), (right,), members=(3,), counted=False)

time: 158 us -> 158 us (level)
  Pallas kernels: 53.5 us -> 59 us
  starting transfers between devices: 50 us -> 44.6 us
    pallas_call x5 -> x6, Pallas kernels: 28.9 us -> 33.6 us  [gram(): pl.pallas_call(body, out_shape=outs, in_specs=[SMEM_SPEC] * 3 + [VMEM_SPE...]
    ppermute x12, starting transfers between devices: 24.1 us -> 21.3 us  [local(): lax.ppermute(run, 'cell', along(d))]
    ppermute x6, starting transfers between devices: 13.7 us -> 11.2 us  [step(): return lax.ppermute(piece, 'cell', across(rel))]
  transfers between devices with their start and end apart: 25 -> 25, of which waited for: 11 -> 13; matrix products, arithmetic and copies ran while one was open for 0% -> 0% of each run, Pallas kernels for 29% -> 33%
where the time goes in v9:
time: 158 us; the launch traced here: 156 us
  Pallas kernels  59 us (37%)
  waiting for transfers between devices  50.5 us (32%)
  starting transfers between devices  44.6 us (28%)
    pallas_call x6, Pallas kernels, gram(): pl.pallas_call(body, out_shape=outs, in_specs=[SMEM_SPEC] * 3 + [VMEM_SPE...  33.6 us
    ppermute x12, starting transfers between devices, local(): lax.ppermute(run, 'cell', along(d))  21.3 us
    ppermute x12, waiting for transfers between devices, local(): lax.ppermute(run, 'cell', along(d))  18.4 us
    pallas_call x4, Pallas kernels, gather_runs(): pl.pallas_call(body, out_shape=[jax.ShapeDtypeStruct((rows, D), vectors.d...  13 us
    ppermute x3, waiting for transfers between devices, local(): whole = {dz: lax.ppermute(mine, 'dp', dp_perm(dz)) for dz in Z_SHIFTS}  11.9 us
    ppermute x3, waiting for transfers between devices, local(): mine = mine + lax.ppermute(quarters[dz], 'dp', dp_perm(dz))  11.3 us
    ppermute x6, starting transfers between devices, step(): return lax.ppermute(piece, 'cell', across(rel))  11.2 us
    pallas_call x1, Pallas kernels, make_lists(): pl.pallas_call(lists_body, out_shape=[jax.ShapeDtypeStruct((LIST,), I32),...  7.45 us
  transfers between devices with their start and end apart: 25, of which 13 were waited for; matrix products, arithmetic and copies ran while one was open for 0% of the time, Pallas kernels for 33%

profile of v9, /device:TPU:1, one launch (start us, length us, event | category | flops | bytes accessed | tf_op | source)
XLA Modules:
  0.0 155.6 jit_solution(17319377754459077116)
XLA Ops:
  1.3 3.9 %gather0.1 = (bf16[3088,128]{1,0:T(8,128)(2,1)}, bf16[3088,128]{1,0:T(8,128)(2,1)}, bf16[3088,128]{1,0:T(8,128)(2,1)}) custom-call(s32[4]{0:T(128)} %pad_add_fusion.refs_0_.pos, s32[32]{0:T(128)} %bitcast.7, bf16[24576,128]{1,0:T(8,128)(2,1)} %bitcast.13, s32[1,384]{1,0:T(1,128)} %refs_3_.1, s32[1,32]{1,0:T(1,128)} %bitcast.8), custom_call_target="tpu_custom_call" | custom-call | tf_op jit(solution)/shard_map/gather0/pallas_call | solution.py:127
  10.6 3.6 %gather1.1 = (bf16[3072,128]{1,0:T(8,128)(2,1)}, bf16[3072,128]{1,0:T(8,128)(2,1)}, bf16[3072,128]{1,0:T(8,128)(2,1)}) custom-call(s32[4]{0:T(128)S(1)} %copy-done, s32[32]{0:T(128)S(1)} %bitcast.9, bf16[24576,128]{1,0:T(8,128)(2,1)} %bitcast.14), custom_call_target="tpu_custom_call" | custom-call | tf_op jit(solution)/shard_map/gather1/pallas_call | solution.py:127
  20.5 8.0 %collective-permute-done.2.refs_2_.refs_6_ = bf16[3088,128]{1,0:T(8,128)(2,1)S(1)} collective-permute-done((bf16[3088,128]{1,0:T(8,128)(2,1)}, bf16[3088,128]{1,0:T(8,128)(2,1)S(1)}, u32[]{:S(2)}, u32[]{:S(2)}) %collective-permute-start.2) | collective-permute-done | bytes 790560 | tf_op jit(solution)/shard_map/ppermute | solution.py:458
  28.5 7.4 %lists.1 = (s32[896]{0:T(1024)S(1)}, s32[32]{0:T(128)S(1)}, s32[256]{0:T(256)S(1)}) custom-call(s32[4]{0:T(128)S(1)} %copy-done, s32[384]{0:T(512)S(1)} %reduce.own_cells, s32[32]{0:T(128)S(1)} %bitcast.10, bf16[3088,128]{1,0:T(8,128)(2,1)S(1)} %collective-permute-done.refs_0_.refs_4_, bf16[3088,128]{1,0:T(8,128)(2,1)S(1)} %collective-permute-done.1.refs_1_.refs_5_, ...), custom_call_target="tpu_custom_call" | custom-call | tf_op jit(solution)/shard_map/lists/pallas_call | solution.py:196
  36.0 2.7 %gather2.1 = (bf16[3072,128]{1,0:T(8,128)(2,1)S(1)}, bf16[3072,128]{1,0:T(8,128)(2,1)S(1)}, bf16[3072,128]{1,0:T(8,128)(2,1)S(1)}, bf16[3072,128]{1,0:T(8,128)(2,1)S(1)}, bf16[3072,128]{1,0:T(8,128)(2,1)S(1)}) custom-call(s32[4]{0:T(128)S(1)} %copy-done, s32[32]{0:T(128)S(1)} %bitcast.11, bf16[24576,128]{1,0:T(8,128)(2,1)} %bitcast.15), custom_call_target="tpu_custom_call" | custom-call | tf_op jit(solution)/shard_map/gather2/pallas_call | solution.py:127
  41.5 7.0 %gram0.1 = (f32[2048,128]{1,0:T(8,128)S(1)}, f32[2048,128]{1,0:T(8,128)S(1)}) custom-call(s32[896]{0:T(1024)S(1)} %get-tuple-element.43.refs_0_, s32[32]{0:T(128)S(1)} %get-tuple-element.44.refs_1_, s32[256]{0:T(256)S(1)} %get-tuple-element.45.refs_2_, bf16[3072,128]{1,0:T(8,128)(2,1)S(1)} %get-tuple-element.66.refs_3_, ...), custom_call_target="tpu_custom_call" | custom-call | flops 1000000000 | bytes 10000000 | tf_op jit(solution)/shard_map/gram0/pallas_call | solution.py:315
  48.6 2.7 %collective-permute-start.15 = (f32[2048,128]{1,0:T(8,128)S(1)}, f32[2048,128]{1,0:T(8,128)S(1)}, u32[]{:S(2)}, u32[]{:S(2)}) collective-permute-start(f32[2048,128]{1,0:T(8,128)S(1)} %get-tuple-element.68), channel_id=1, source_target_pairs={{0,6},{1,25},{2,0},{3,27},{4,2},{5,29},{6,4},{7,31},{8,14},{9,1},{... | collective-permute-start | bytes 3145736 | tf_op jit(solution)/shard_map/ppermute | solution.py:461
  51.3 2.7 %gather3.1 = (bf16[3072,128]{1,0:T(8,128)(2,1)S(1)}, bf16[3072,128]{1,0:T(8,128)(2,1)S(1)}, bf16[3072,128]{1,0:T(8,128)(2,1)S(1)}, bf16[3072,128]{1,0:T(8,128)(2,1)S(1)}, bf16[3072,128]{1,0:T(8,128)(2,1)S(1)}) custom-call(s32[4]{0:T(128)S(1)} %copy-done, s32[32]{0:T(128)S(1)} %bitcast.12, bf16[24576,128]{1,0:T(8,128)(2,1)} %bitcast.16), custom_call_target="tpu_custom_call" | custom-call | tf_op jit(solution)/shard_map/gather3/pallas_call | solution.py:127
  54.6 6.2 %collective-permute-start.13 = (bf16[3072,128]{1,0:T(8,128)(2,1)S(1)}, bf16[3072,128]{1,0:T(8,128)(2,1)S(1)}, u32[]{:S(2)}, u32[]{:S(2)}) collective-permute-start(bf16[3072,128]{1,0:T(8,128)(2,1)S(1)} %get-tuple-element.65), channel_id=1, source_target_pairs={{0,24},{1,7},{2,26},{3,1},{4,28},{5,3},{6,30},{7,5},{8,0},{9,15},{... | collective-permute-start | bytes 2359304 | tf_op jit(solution)/shard_map/ppermute | solution.py:458
  60.8 5.4 %collective-permute-done.6.refs_3_ = bf16[3072,128]{1,0:T(8,128)(2,1)S(1)} collective-permute-done((bf16[3072,128]{1,0:T(8,128)(2,1)S(1)}, bf16[3072,128]{1,0:T(8,128)(2,1)S(1)}, u32[]{:S(2)}, u32[]{:S(2)}) %collective-permute-start.6) | collective-permute-done | bytes 786464 | tf_op jit(solution)/shard_map/ppermute | solution.py:458
  68.3 4.7 %gram2.1 = (f32[2048,128]{1,0:T(8,128)S(1)}, f32[2048,128]{1,0:T(8,128)S(1)}) custom-call(s32[896]{0:T(1024)S(1)} %get-tuple-element.43.refs_0_, s32[32]{0:T(128)S(1)} %get-tuple-element.44.refs_1_, s32[256]{0:T(256)S(1)} %get-tuple-element.45.refs_2_, bf16[3072,128]{1,0:T(8,128)(2,1)S(1)} %get-tuple-element.54.refs_3_, ...), custom_call_target="tpu_custom_call" | custom-call | flops 1000000000 | bytes 10000000 | tf_op jit(solution)/shard_map/gram2/pallas_call | solution.py:315
  73.0 3.6 %gram2b.1 = (f32[2048,128]{1,0:T(8,128)S(1)}, f32[2048,128]{1,0:T(8,128)S(1)}) custom-call(s32[896]{0:T(1024)S(1)} %get-tuple-element.43.refs_0_, s32[32]{0:T(128)S(1)} %get-tuple-element.44.refs_1_, s32[256]{0:T(256)S(1)} %get-tuple-element.45.refs_2_, bf16[3072,128]{1,0:T(8,128)(2,1)S(1)} %collective-permute-done.6.refs_3_, ...), custom_call_target="tpu_custom_call" | custom-call | flops 1000000000 | bytes 10000000 | tf_op jit(solution)/shard_map/gram2b/pallas_call | solution.py:315
  79.2 3.4 %collective-permute-start.10 = (f32[2048,128]{1,0:T(8,128)S(1)}, f32[2048,128]{1,0:T(8,128)S(1)}, u32[]{:S(2)}, u32[]{:S(2)}) collective-permute-start(f32[2048,128]{1,0:T(8,128)S(1)} %get-tuple-element.60), channel_id=1, source_target_pairs={{0,2},{1,9},{2,4},{3,11},{4,6},{5,13},{6,0},{7,15},{8,10},{9,17},{... | collective-permute-start | bytes 3145736 | tf_op jit(solution)/shard_map/ppermute | solution.py:461
  83.3 6.6 %gram3.1 = (f32[2048,128]{1,0:T(8,128)S(1)}, f32[2048,128]{1,0:T(8,128)S(1)}) custom-call(s32[896]{0:T(1024)S(1)} %get-tuple-element.43.refs_0_, s32[32]{0:T(128)S(1)} %get-tuple-element.44.refs_1_, s32[256]{0:T(256)S(1)} %get-tuple-element.45.refs_2_, bf16[3072,128]{1,0:T(8,128)(2,1)S(1)} %get-tuple-element.63.refs_3_, ...), custom_call_target="tpu_custom_call" | custom-call | flops 1000000000 | bytes 10000000 | tf_op jit(solution)/shard_map/gram3/pallas_call | solution.py:315
  90.4 2.8 %gram3b.1 = (f32[2048,128]{1,0:T(8,128)S(1)}, f32[2048,128]{1,0:T(8,128)S(1)}) custom-call(s32[896]{0:T(1024)S(1)} %get-tuple-element.43.refs_0_, s32[32]{0:T(128)S(1)} %get-tuple-element.44.refs_1_, s32[256]{0:T(256)S(1)} %get-tuple-element.45.refs_2_, bf16[3072,128]{1,0:T(8,128)(2,1)S(1)} %collective-permute-done.11.refs_3_, ...), custom_call_target="tpu_custom_call" | custom-call | flops 1000000000 | bytes 10000000 | tf_op jit(solution)/shard_map/gram3b/pallas_call | solution.py:315
  93.2 4.4 %collective-permute-start.17 = (f32[2048,128]{1,0:T(8,128)S(1)}, f32[2048,128]{1,0:T(8,128)S(1)}, u32[]{:S(2)}, u32[]{:S(2)}) collective-permute-start(f32[2048,128]{1,0:T(8,128)S(1)} %get-tuple-element.73), channel_id=1, source_target_pairs={{0,6},{1,25},{2,0},{3,27},{4,2},{5,29},{6,4},{7,31},{8,14},{9,1},{... | collective-permute-start | bytes 3145736 | tf_op jit(solution)/shard_map/ppermute | solution.py:461
  97.6 4.8 %collective-permute-done.10.refs_8_ = f32[2048,128]{1,0:T(8,128)S(1)} collective-permute-done((f32[2048,128]{1,0:T(8,128)S(1)}, f32[2048,128]{1,0:T(8,128)S(1)}, u32[]{:S(2)}, u32[]{:S(2)}) %collective-permute-start.10) | collective-permute-done | bytes 1048608 | tf_op jit(solution)/shard_map/ppermute | solution.py:461
  102.5 8.9 %gram1.1 = (f32[2048,128]{1,0:T(8,128)S(1)}, f32[2048,128]{1,0:T(8,128)S(1)}) custom-call(s32[896]{0:T(1024)S(1)} %get-tuple-element.43.refs_0_, s32[32]{0:T(128)S(1)} %get-tuple-element.44.refs_1_, s32[256]{0:T(256)S(1)} %get-tuple-element.45.refs_2_, bf16[3072,128]{1,0:T(8,128)(2,1)S(1)} %get-tuple-element.51.refs_3_, ...), custom_call_target="tpu_custom_call" | custom-call | flops 1000000000 | bytes 10000000 | tf_op jit(solution)/shard_map/gram1/pallas_call | solution.py:315
  113.4 3.7 %collective-permute-start.18 = (f32[2048,128]{1,0:T(8,128)S(1)}, f32[2048,128]{1,0:T(8,128)S(1)}, u32[]{:S(2)}, u32[]{:S(2)}) collective-permute-start(f32[2048,128]{1,0:T(8,128)S(1)} %other_total.1), channel_id=1, source_target_pairs={{0,1},{1,0},{2,3},{3,2},{4,5},{5,4},{6,7},{7,6},{8,9},{9,8},{10,11... | collective-permute-start | bytes 3145736 | tf_op jit(solution)/shard_map/ppermute | solution.py:475
  125.6 4.7 %collective-permute-done.19 = f32[528,128]{1,0:T(8,128)S(1)} collective-permute-done((f32[528,128]{1,0:T(8,128)S(1)}, f32[528,128]{1,0:T(8,128)S(1)}, u32[]{:S(2)}, u32[]{:S(2)}) %collective-permute-start.19) | collective-permute-done | bytes 270368 | tf_op jit(solution)/shard_map/ppermute | solution.py:479
  130.4 6.5 %collective-permute-done.21 = f32[528,128]{1,0:T(8,128)S(1)} collective-permute-done((f32[528,128]{1,0:T(8,128)S(1)}, f32[528,128]{1,0:T(8,128)S(1)}, u32[]{:S(2)}, u32[]{:S(2)}) %collective-permute-start.21) | collective-permute-done | bytes 270368 | tf_op jit(solution)/shard_map/ppermute | solution.py:479
  140.1 8.0 %collective-permute-done.22.refs_1_ = f32[528,128]{1,0:T(8,128)S(1)} collective-permute-done((f32[528,128]{1,0:T(8,128)S(1)}, f32[528,128]{1,0:T(8,128)S(1)}, u32[]{:S(2)}, u32[]{:S(2)}) %collective-permute-start.22) | collective-permute-done | bytes 270368 | tf_op jit(solution)/shard_map/ppermute | solution.py:480
  148.1 3.9 %collective-permute-done.24.refs_3_ = f32[528,128]{1,0:T(8,128)S(1)} collective-permute-done((f32[528,128]{1,0:T(8,128)S(1)}, f32[528,128]{1,0:T(8,128)S(1)}, u32[]{:S(2)}, u32[]{:S(2)}) %collective-permute-start.24) | collective-permute-done | bytes 270368 | tf_op jit(solution)/shard_map/ppermute | solution.py:480
  152.0 3.6 %finish.1 = (f32[32,128]{1,0:T(8,128)}, f32[32,128,128]{2,1,0:T(8,128)}) custom-call(s32[4]{0:T(128)S(1)} %copy-done, f32[528,128]{1,0:T(8,128)S(1)} %add_add_fusion.refs_0_, f32[528,128]{1,0:T(8,128)S(1)} %collective-permute-done.22.refs_1_, f32[528,128]{1,0:T(8,128)S(1)} %collective-permute-done.23.refs_2_, f32[528,128]{1,0:T(8,128)S(1)} %collective-permute-done.24.refs_3_), custom_call_target="tpu_custom_call" | custom-call | tf_op jit(solution)/shard_map/finish/pallas_call | solution.py:424
  (49 shorter events, 35.3 us)
Async XLA Ops:
  5.3 13.6 %collective-permute-start = (bf16[3088,128]{1,0:T(8,128)(2,1)}, bf16[3088,128]{1,0:T(8,128)(2,1)S(1)}, u32[]{:S(2)}, u32[]{:S(2)}) collective-permute-start(bf16[3088,128]{1,0:T(8,128)(2,1)} %get-tuple-element.40), channel_id=1, source_target_pairs={{0,8},{1,3},{2,10},{3,5},{4,12},{5,7},{6,14},{7,1},{8,16},{9,11},{... | collective-permute-start | bytes 2371592 | tf_op jit(solution)/shard_map/ppermute | solution.py:458
  7.6 12.9 %collective-permute-start.1 = (bf16[3088,128]{1,0:T(8,128)(2,1)}, bf16[3088,128]{1,0:T(8,128)(2,1)S(1)}, u32[]{:S(2)}, u32[]{:S(2)}) collective-permute-start(bf16[3088,128]{1,0:T(8,128)(2,1)} %get-tuple-element.41), channel_id=1, source_target_pairs={{0,24},{1,7},{2,26},{3,1},{4,28},{5,3},{6,30},{7,5},{8,0},{9,15},{... | collective-permute-start | bytes 2371592 | tf_op jit(solution)/shard_map/ppermute | solution.py:458
  9.0 19.5 %collective-permute-start.2 = (bf16[3088,128]{1,0:T(8,128)(2,1)}, bf16[3088,128]{1,0:T(8,128)(2,1)S(1)}, u32[]{:S(2)}, u32[]{:S(2)}) collective-permute-start(bf16[3088,128]{1,0:T(8,128)(2,1)} %get-tuple-element.42), channel_id=1, source_target_pairs={{0,16},{1,5},{2,18},{3,7},{4,20},{5,1},{6,22},{7,3},{8,24},{9,13},... | collective-permute-start | bytes 2371592 | tf_op jit(solution)/shard_map/ppermute | solution.py:458
  14.2 27.3 %collective-permute-start.3 = (bf16[3072,128]{1,0:T(8,128)(2,1)}, bf16[3072,128]{1,0:T(8,128)(2,1)S(1)}, u32[]{:S(2)}, u32[]{:S(2)}) collective-permute-start(bf16[3072,128]{1,0:T(8,128)(2,1)} %get-tuple-element.47), channel_id=1, source_target_pairs={{0,8},{1,3},{2,10},{3,5},{4,12},{5,7},{6,14},{7,1},{8,16},{9,11},{... | collective-permute-start | bytes 2359304 | tf_op jit(solution)/shard_map/ppermute | solution.py:458
  14.7 33.9 %collective-permute-start.4 = (bf16[3072,128]{1,0:T(8,128)(2,1)}, bf16[3072,128]{1,0:T(8,128)(2,1)}, u32[]{:S(2)}, u32[]{:S(2)}) collective-permute-start(bf16[3072,128]{1,0:T(8,128)(2,1)} %get-tuple-element.48), channel_id=1, source_target_pairs={{0,24},{1,7},{2,26},{3,1},{4,28},{5,3},{6,30},{7,5},{8,0},{9,15},{... | collective-permute-start | bytes 2359304 | tf_op jit(solution)/shard_map/ppermute | solution.py:458
  18.8 29.8 %collective-permute-start.5 = (bf16[3072,128]{1,0:T(8,128)(2,1)}, bf16[3072,128]{1,0:T(8,128)(2,1)}, u32[]{:S(2)}, u32[]{:S(2)}) collective-permute-start(bf16[3072,128]{1,0:T(8,128)(2,1)} %get-tuple-element.49), channel_id=1, source_target_pairs={{0,16},{1,5},{2,18},{3,7},{4,20},{5,1},{6,22},{7,3},{8,24},{9,13},... | collective-permute-start | bytes 2359304 | tf_op jit(solution)/shard_map/ppermute | solution.py:458
  38.7 15.3 %collective-permute-start.7 = (bf16[3072,128]{1,0:T(8,128)(2,1)S(1)}, bf16[3072,128]{1,0:T(8,128)(2,1)S(1)}, u32[]{:S(2)}, u32[]{:S(2)}) collective-permute-start(bf16[3072,128]{1,0:T(8,128)(2,1)S(1)} %get-tuple-element.55), channel_id=1, source_target_pairs={{0,8},{1,3},{2,10},{3,5},{4,12},{5,7},{6,14},{7,1},{8,16},{9,11},{... | collective-permute-start | bytes 2359304 | tf_op jit(solution)/shard_map/ppermute | solution.py:458
  38.9 15.7 %collective-permute-start.8 = (bf16[3072,128]{1,0:T(8,128)(2,1)S(1)}, bf16[3072,128]{1,0:T(8,128)(2,1)S(1)}, u32[]{:S(2)}, u32[]{:S(2)}) collective-permute-start(bf16[3072,128]{1,0:T(8,128)(2,1)S(1)} %get-tuple-element.56), channel_id=1, source_target_pairs={{0,24},{1,7},{2,26},{3,1},{4,28},{5,3},{6,30},{7,5},{8,0},{9,15},{... | collective-permute-start | bytes 2359304 | tf_op jit(solution)/shard_map/ppermute | solution.py:458
  41.5 24.8 %collective-permute-start.6 = (bf16[3072,128]{1,0:T(8,128)(2,1)S(1)}, bf16[3072,128]{1,0:T(8,128)(2,1)S(1)}, u32[]{:S(2)}, u32[]{:S(2)}) collective-permute-start(bf16[3072,128]{1,0:T(8,128)(2,1)S(1)} %get-tuple-element.53), channel_id=1, source_target_pairs={{0,16},{1,5},{2,18},{3,7},{4,20},{5,1},{6,22},{7,3},{8,24},{9,13},... | collective-permute-start | bytes 2359304 | tf_op jit(solution)/shard_map/ppermute | solution.py:458
  48.5 34.8 %collective-permute-start.14 = (f32[2048,128]{1,0:T(8,128)S(1)}, f32[2048,128]{1,0:T(8,128)S(1)}, u32[]{:S(2)}, u32[]{:S(2)}) collective-permute-start(f32[2048,128]{1,0:T(8,128)S(1)} %get-tuple-element.67), channel_id=1, source_target_pairs={{0,2},{1,9},{2,4},{3,11},{4,6},{5,13},{6,0},{7,15},{8,10},{9,17},{... | collective-permute-start | bytes 3145736 | tf_op jit(solution)/shard_map/ppermute | solution.py:461
  48.6 34.7 %collective-permute-start.15 = (f32[2048,128]{1,0:T(8,128)S(1)}, f32[2048,128]{1,0:T(8,128)S(1)}, u32[]{:S(2)}, u32[]{:S(2)}) collective-permute-start(f32[2048,128]{1,0:T(8,128)S(1)} %get-tuple-element.68), channel_id=1, source_target_pairs={{0,6},{1,25},{2,0},{3,27},{4,2},{5,29},{6,4},{7,31},{8,14},{9,1},{... | collective-permute-start | bytes 3145736 | tf_op jit(solution)/shard_map/ppermute | solution.py:461
  54.0 25.2 %collective-permute-start.12 = (bf16[3072,128]{1,0:T(8,128)(2,1)S(1)}, bf16[3072,128]{1,0:T(8,128)(2,1)S(1)}, u32[]{:S(2)}, u32[]{:S(2)}) collective-permute-start(bf16[3072,128]{1,0:T(8,128)(2,1)S(1)} %get-tuple-element.64), channel_id=1, source_target_pairs={{0,8},{1,3},{2,10},{3,5},{4,12},{5,7},{6,14},{7,1},{8,16},{9,11},{... | collective-permute-start | bytes 2359304 | tf_op jit(solution)/shard_map/ppermute | solution.py:458
  54.6 28.0 %collective-permute-start.13 = (bf16[3072,128]{1,0:T(8,128)(2,1)S(1)}, bf16[3072,128]{1,0:T(8,128)(2,1)S(1)}, u32[]{:S(2)}, u32[]{:S(2)}) collective-permute-start(bf16[3072,128]{1,0:T(8,128)(2,1)S(1)} %get-tuple-element.65), channel_id=1, source_target_pairs={{0,24},{1,7},{2,26},{3,1},{4,28},{5,3},{6,30},{7,5},{8,0},{9,15},{... | collective-permute-start | bytes 2359304 | tf_op jit(solution)/shard_map/ppermute | solution.py:458
  66.3 24.2 %collective-permute-start.11 = (bf16[3072,128]{1,0:T(8,128)(2,1)S(1)}, bf16[3072,128]{1,0:T(8,128)(2,1)S(1)}, u32[]{:S(2)}, u32[]{:S(2)}) collective-permute-start(bf16[3072,128]{1,0:T(8,128)(2,1)S(1)} %get-tuple-element.62), channel_id=1, source_target_pairs={{0,16},{1,5},{2,18},{3,7},{4,20},{5,1},{6,22},{7,3},{8,24},{9,13},... | collective-permute-start | bytes 2359304 | tf_op jit(solution)/shard_map/ppermute | solution.py:458
  79.2 23.2 %collective-permute-start.10 = (f32[2048,128]{1,0:T(8,128)S(1)}, f32[2048,128]{1,0:T(8,128)S(1)}, u32[]{:S(2)}, u32[]{:S(2)}) collective-permute-start(f32[2048,128]{1,0:T(8,128)S(1)} %get-tuple-element.60), channel_id=1, source_target_pairs={{0,2},{1,9},{2,4},{3,11},{4,6},{5,13},{6,0},{7,15},{8,10},{9,17},{... | collective-permute-start | bytes 3145736 | tf_op jit(solution)/shard_map/ppermute | solution.py:461
  82.6 19.8 %collective-permute-start.9 = (f32[2048,128]{1,0:T(8,128)S(1)}, f32[2048,128]{1,0:T(8,128)S(1)}, u32[]{:S(2)}, u32[]{:S(2)}) collective-permute-start(f32[2048,128]{1,0:T(8,128)S(1)} %get-tuple-element.59), channel_id=1, source_target_pairs={{0,6},{1,25},{2,0},{3,27},{4,2},{5,29},{6,4},{7,31},{8,14},{9,1},{... | collective-permute-start | bytes 3145736 | tf_op jit(solution)/shard_map/ppermute | solution.py:461
  93.2 19.8 %collective-permute-start.17 = (f32[2048,128]{1,0:T(8,128)S(1)}, f32[2048,128]{1,0:T(8,128)S(1)}, u32[]{:S(2)}, u32[]{:S(2)}) collective-permute-start(f32[2048,128]{1,0:T(8,128)S(1)} %get-tuple-element.73), channel_id=1, source_target_pairs={{0,6},{1,25},{2,0},{3,27},{4,2},{5,29},{6,4},{7,31},{8,14},{9,1},{... | collective-permute-start | bytes 3145736 | tf_op jit(solution)/shard_map/ppermute | solution.py:461
  97.6 19.6 %collective-permute-start.16 = (f32[2048,128]{1,0:T(8,128)S(1)}, f32[2048,128]{1,0:T(8,128)S(1)}, u32[]{:S(2)}, u32[]{:S(2)}) collective-permute-start(f32[2048,128]{1,0:T(8,128)S(1)} %get-tuple-element.71), channel_id=1, source_target_pairs={{0,2},{1,9},{2,4},{3,11},{4,6},{5,13},{6,0},{7,15},{8,10},{9,17},{... | collective-permute-start | bytes 3145736 | tf_op jit(solution)/shard_map/ppermute | solution.py:461
  120.3 10.0 %collective-permute-start.19 = (f32[528,128]{1,0:T(8,128)S(1)}, f32[528,128]{1,0:T(8,128)S(1)}, u32[]{:S(2)}, u32[]{:S(2)}) collective-permute-start(f32[528,128]{1,0:T(8,128)S(1)} %get-tuple-element.75), channel_id=1, source_target_pairs={{0,32},{32,64},{64,96},{96,0},{1,33},{33,65},{65,97},{97,1},{2,34}... | collective-permute-start | bytes 811016 | tf_op jit(solution)/shard_map/ppermute | solution.py:479
  121.9 8.5 %collective-permute-start.20 = (f32[528,128]{1,0:T(8,128)S(1)}, f32[528,128]{1,0:T(8,128)S(1)}, u32[]{:S(2)}, u32[]{:S(2)}) collective-permute-start(f32[528,128]{1,0:T(8,128)S(1)} %get-tuple-element.76), channel_id=1, source_target_pairs={{0,96},{32,0},{64,32},{96,64},{1,97},{33,1},{65,33},{97,65},{2,98}... | collective-permute-start | bytes 811016 | tf_op jit(solution)/shard_map/ppermute | solution.py:479
  124.5 12.5 %collective-permute-start.21 = (f32[528,128]{1,0:T(8,128)S(1)}, f32[528,128]{1,0:T(8,128)S(1)}, u32[]{:S(2)}, u32[]{:S(2)}) collective-permute-start(f32[528,128]{1,0:T(8,128)S(1)} %get-tuple-element.77), channel_id=1, source_target_pairs={{0,64},{32,96},{64,0},{96,32},{1,65},{33,97},{65,1},{97,33},{2,66}... | collective-permute-start | bytes 811016 | tf_op jit(solution)/shard_map/ppermute | solution.py:479
  137.0 11.1 %collective-permute-start.22 = (f32[528,128]{1,0:T(8,128)S(1)}, f32[528,128]{1,0:T(8,128)S(1)}, u32[]{:S(2)}, u32[]{:S(2)}) collective-permute-start(f32[528,128]{1,0:T(8,128)S(1)} %add_add_fusion.refs_0_), channel_id=1, source_target_pairs={{0,32},{32,64},{64,96},{96,0},{1,33},{33,65},{65,97},{97,1},{2,34}... | collective-permute-start | bytes 811016 | tf_op jit(solution)/shard_map/ppermute | solution.py:480
  137.6 10.5 %collective-permute-start.23 = (f32[528,128]{1,0:T(8,128)S(1)}, f32[528,128]{1,0:T(8,128)S(1)}, u32[]{:S(2)}, u32[]{:S(2)}) collective-permute-start(f32[528,128]{1,0:T(8,128)S(1)} %add_add_fusion.refs_0_), channel_id=1, source_target_pairs={{0,64},{32,96},{64,0},{96,32},{1,65},{33,97},{65,1},{97,33},{2,66}... | collective-permute-start | bytes 811016 | tf_op jit(solution)/shard_map/ppermute | solution.py:480
  138.2 13.8 %collective-permute-start.24 = (f32[528,128]{1,0:T(8,128)S(1)}, f32[528,128]{1,0:T(8,128)S(1)}, u32[]{:S(2)}, u32[]{:S(2)}) collective-permute-start(f32[528,128]{1,0:T(8,128)S(1)} %add_add_fusion.refs_0_), channel_id=1, source_target_pairs={{0,96},{32,0},{64,32},{96,64},{1,97},{33,1},{65,33},{97,65},{2,98}... | collective-permute-start | bytes 811016 | tf_op jit(solution)/shard_map/ppermute | solution.py:480
  (4 other events, 44.3 us)
